TPU v7x, 32 devices: a whole 2x2x4 slice. The times are simulated.
32 devices in a mesh: dp: 8 (over y, x, core), tensor: 4 (over z).
Axes of the slice: x: 2, y: 2, z: 4, core: 2. Of those that a mesh axis runs over, the one named last changes fastest.
Arguments:
- rm_hidden: bfloat16 [8, 256, 3584], P('dp', 'tensor'), may hold values from -6 to 6
- rm_cotangent: bfloat16 [8, 256, 3584], P('dp', 'tensor'), may hold values from -6 to 6
- rm_gain: float32 [3584], replicated, may hold values from 0.25 to 1.75
- rewards: float32 [8], P('dp'), may hold values from 0.25 to 8, as said below
- visual_pos: int32 [8, 128], P('dp', 'tensor'), may hold values from 0 to 255, as said below
- bridge: bfloat16 [3584, 2048], P(None, 'tensor'), may hold values from -0.09375 to 0.09375
- img_query: bfloat16 [8, 512, 2048], P('dp', 'tensor'), may hold values from -8 to 8
- img_key: bfloat16 [8, 512, 2048], P('dp', 'tensor'), may hold values from -8 to 8
- img_value: bfloat16 [8, 512, 2048], P('dp', 'tensor'), may hold values from -6 to 6
Outputs:
- grad_query: bfloat16 [8, 512, 2048], P('dp', 'tensor')
- grad_key: bfloat16 [8, 512, 2048], P('dp', 'tensor')
- grad_value: bfloat16 [8, 512, 2048], P('dp', 'tensor')
Inputs may be any that keep to these rules, and one draw needn't show every extreme that they name: `visual_pos`: strictly increasing in each sample; rows 64 * t to 64 * t + 63 of a reward sequence hold exactly 32 visual tokens, for every t. `rewards`: positive.
All inputs are finite; a program needn't handle non-finite values.
Results may differ from a plain program's by a relative error of at most 0.0082.
Values may be sent and summed in bfloat16 or wider, within the bound.
No kernel may reach another device: no remote copies, remote signals or barrier semaphores. Data moves between devices by JAX's collectives and lax.ppermute only.
A program may use at most 64 MiB of HBM per device.

v0:
```python
import functools

import jax
import jax.numpy as jnp
from jax import lax
from jax.experimental import pallas as pl
from jax.experimental.pallas import tpu as pltpu
from jax.sharding import PartitionSpec as P


HD = 128
GW = 64
GROUPS = 2


def norm_backward(hidden, cotangent, gain):
    hidden_f = hidden.astype(jnp.float32)
    scaled_cot = cotangent.astype(jnp.float32) * gain
    inv_rms = lax.rsqrt(jnp.mean(hidden_f * hidden_f, axis=-1, keepdims=True) + 1e-06)
    mixed = jnp.mean(hidden_f * scaled_cot, axis=-1, keepdims=True)
    return (inv_rms * scaled_cot - hidden_f * inv_rms * inv_rms * inv_rms * mixed).astype(
        jnp.bfloat16
    )


def total_over(value, axis):
    size = lax.axis_size(axis)
    if size & (size - 1):
        return lax.psum(value, axis)
    step = 1
    while step < size:
        value = value + lax.ppermute(value, axis, [(i, i ^ step) for i in range(size)])
        step *= 2
    return value


def relayed_blocks(block, axis):
    size = lax.axis_size(axis)
    here = lax.axis_index(axis)
    upward, downward = [], []
    up = down = block
    for step in range(size - 1):
        up = lax.ppermute(up, axis, [(i, i + 1) for i in range(step, size - 1)])
        down = lax.ppermute(down, axis, [(i + 1, i) for i in range(size - 1 - step)])
        upward.append(up)
        downward.append(down)
    return [block] + [
        jnp.where(here >= k, upward[k - 1], downward[size - k - 1]) for k in range(1, size)
    ]


def attend_kernel(count, scale, chunk, *refs):
    _, handed_ref, query_ref, key_ref, value_ref = refs[:5]
    blocks = refs[5 : 4 + count]
    outs = refs[4 + count : 4 + 2 * count]
    q_s, k_s, v_s, g_s, dq_s, dk_s, dv_s = refs[4 + 2 * count :]
    rows = query_ref.shape[1]
    length = rows * count
    seen = handed_ref.shape[0] // count
    q_s[pl.ds(0, rows)] = query_ref[0]
    k_s[pl.ds(0, rows)] = key_ref[0]
    v_s[pl.ds(0, rows)] = value_ref[0]
    for j, block in enumerate(blocks, 1):
        at = pl.ds(j * rows, rows)
        q_s[at] = block[0]
        k_s[at] = block[1]
        v_s[at] = block[2]
    token = lax.broadcasted_iota(jnp.int32, (rows, seen), 0)
    source = lax.broadcasted_iota(jnp.int32, (rows, seen), 1)
    spread = jnp.where(
        (token // (2 * GW)) * (GW // 2) + (token % GW) // 2 == source, 1.0, 0.0
    ).astype(jnp.bfloat16)
    for j in range(count):
        g_s[pl.ds(j * rows, rows)] = jnp.dot(
            spread, handed_ref[pl.ds(j * seen, seen)], preferred_element_type=jnp.float32
        ).astype(jnp.bfloat16)
    dk_s[...] = jnp.zeros_like(dk_s)
    dv_s[...] = jnp.zeros_like(dv_s)
    key_rows = k_s[...]
    value_rows = v_s[...]
    key_columns = key_rows.T
    both_last = (((1,), (1,)), ((), ()))

    def step(c, carry):
        at = pl.ds(pl.multiple_of(c * chunk, chunk), chunk)
        q = q_s[at]
        g = g_s[at]
        scores = lax.dot_general(key_rows, q, both_last, preferred_element_type=jnp.float32) * scale
        exp_scores = jnp.exp(scores - jnp.max(scores, axis=0, keepdims=True))
        weights = exp_scores * (1.0 / jnp.sum(exp_scores, axis=0, keepdims=True))
        grad_weights = lax.dot_general(value_rows, g, both_last, preferred_element_type=jnp.float32)
        row_dot = jnp.sum(weights * grad_weights, axis=0, keepdims=True)
        grad_scores = (weights * (grad_weights - row_dot)).astype(jnp.bfloat16)
        dv_s[...] += jnp.dot(weights.astype(jnp.bfloat16), g, preferred_element_type=jnp.float32)
        dk_s[...] += jnp.dot(grad_scores, q, preferred_element_type=jnp.float32)
        dq = jnp.dot(key_columns, grad_scores, preferred_element_type=jnp.float32)
        dq_s[at] = (dq * scale).T.astype(jnp.bfloat16)
        return carry

    lax.fori_loop(0, length // chunk, step, 0)
    for j, out in enumerate(outs):
        at = pl.ds(j * rows, rows)
        out[0] = dq_s[at]
        out[1] = (dk_s[at] * scale).astype(jnp.bfloat16)
        out[2] = dv_s[at].astype(jnp.bfloat16)


def attend(here, handed, own, blocks, group, groups, count):
    rows = own[0].shape[1]
    local_heads = handed.shape[1] // HD
    heads = local_heads // groups
    length = rows * count
    chunk = min(256, length)
    first = group * heads
    own_spec = pl.BlockSpec((1, rows, HD), lambda h, t: (0, 0, t[0] * local_heads + first + h))
    block_spec = pl.BlockSpec((3, rows, HD), lambda h, t: (0, 0, h))
    flops = 10 * heads * length * length * HD
    return pl.pallas_call(
        functools.partial(attend_kernel, count, HD**-0.5, chunk),
        grid_spec=pltpu.PrefetchScalarGridSpec(
            num_scalar_prefetch=1,
            grid=(heads,),
            in_specs=[pl.BlockSpec((handed.shape[0], HD), lambda h, t: (0, first + h))]
            + [own_spec] * 3
            + [block_spec] * (count - 1),
            out_specs=[block_spec] * count,
            scratch_shapes=[pltpu.VMEM((length, HD), jnp.bfloat16)] * 5
            + [pltpu.VMEM((length, HD), jnp.float32)] * 2,
        ),
        out_shape=[jax.ShapeDtypeStruct((3, rows, heads * HD), jnp.bfloat16)] * count,
        cost_estimate=pl.CostEstimate(
            flops=flops,
            bytes_accessed=12 * length * heads * HD,
            transcendentals=heads * length * length,
        ),
    )(here, handed, *own, *blocks)


def place_kernel(count, groups, *refs):
    parts = refs[1 : 1 + count * groups]
    outs = refs[1 + count * groups :]
    width = parts[0].shape[2]
    for k in range(count):

        @pl.when(pl.program_id(0) == k)
        def _():
            for g in range(groups):
                for i, out in enumerate(outs):
                    out[0, :, pl.ds(g * width, width)] = parts[k * groups + g][i]


def place(here, parts, count):
    groups = len(parts[0])
    rows, width = parts[0][0].shape[1:]
    flat = [part for ranked in parts for part in ranked]
    part_spec = pl.BlockSpec((3, rows, width), lambda k, t: (0, 0, 0))
    out_spec = pl.BlockSpec((1, rows, width * groups), lambda k, t: (0, 0, lax.rem(t[0] + k, count)))
    return pl.pallas_call(
        functools.partial(place_kernel, count, groups),
        grid_spec=pltpu.PrefetchScalarGridSpec(
            num_scalar_prefetch=1,
            grid=(count,),
            in_specs=[part_spec] * len(flat),
            out_specs=[out_spec] * 3,
        ),
        out_shape=[jax.ShapeDtypeStruct((1, rows, width * groups * count), jnp.bfloat16)] * 3,
        name="place",
    )(here, *flat)


def work(
    rm_hidden, rm_cotangent, rm_gain, rewards, visual_pos, bridge, img_query, img_key, img_value
):
    count = lax.axis_size("tensor")
    here = lax.axis_index("tensor")
    place_of = here[None].astype(jnp.int32)
    own_width = img_query.shape[2] // count
    groups = min(GROUPS, own_width // HD)
    width = own_width // groups

    def columns(array, k, g):
        first = lax.rem(here + k, count) * own_width + g * width
        return lax.dynamic_slice_in_dim(array[0], first, width, 1)

    arrived = []
    for g in range(groups):
        arrived.append(
            [
                lax.ppermute(
                    jnp.stack([columns(a, k, g) for a in (img_query, img_key, img_value)]),
                    "tensor",
                    [(i, (i + k) % count) for i in range(count)],
                )
                for k in range(1, count)
            ]
        )

    reward_sum = total_over(jnp.sum(rewards), "dp")
    sample_count = lax.axis_size("dp") * rewards.shape[0]
    reward_weight = rewards[0] * sample_count / reward_sum
    row_offset = here * rm_hidden.shape[1]
    local_rows = visual_pos[0] - row_offset
    vis_hidden = jnp.take(rm_hidden[0], local_rows, axis=0)
    vis_cot = jnp.take(rm_cotangent[0], local_rows, axis=0)
    visual_grad = norm_backward(vis_hidden, vis_cot, rm_gain)
    visual_blocks = relayed_blocks(visual_grad, "tensor")
    handed = (
        jnp.dot(
            jnp.concatenate(visual_blocks, axis=0), bridge, preferred_element_type=jnp.float32
        )
        * reward_weight
    ).astype(jnp.bfloat16)

    parts = [[] for _ in range(count)]
    for g in range(groups):
        grads = attend(
            place_of, handed, (img_query, img_key, img_value), arrived[g], g, groups, count
        )
        parts[0].append(grads[0])
        for k in range(1, count):
            parts[k].append(
                lax.ppermute(grads[k], "tensor", [(i, (i - k) % count) for i in range(count)])
            )
    return tuple(place(place_of, parts, count))


def solution(mesh):
    placed = (
        P("dp", "tensor", None),
        P("dp", "tensor", None),
        P(),
        P("dp"),
        P("dp", "tensor"),
        P(None, "tensor"),
        P("dp", "tensor", None),
        P("dp", "tensor", None),
        P("dp", "tensor", None),
    )
    return jax.shard_map(
        work,
        mesh=mesh,
        in_specs=placed,
        out_specs=(P("dp", "tensor", None), P("dp", "tensor", None), P("dp", "tensor", None)),
        check_vma=False,
    )
```

profile of v0, /device:TPU:2, one launch (start us, length us, event | category | flops | bytes accessed | tf_op | source)
XLA Modules:
  0.0 96.6 jit_solution(12602885011181757590)
XLA Ops:
  0.7 0.7 compare_and_fusion
  1.7 0.7 gather_fusion.1
  2.4 0.7 gather_fusion
  3.7 1.3 %collective-permute-start.1 = (bf16[32,3584]{1,0:T(8,128)(2,1)S(1)}, bf16[32,3584]{1,0:T(8,128)(2,1)S(1)}, u32[]{:S(2)}, u32[]{:S(2)}) collective-permute-start(bf16[32,3584]{1,0:T(8,128)(2,1)S(1)} %fusion.13), channel_id=1, source_target_pairs={{1,0},{2,1},{3,2},{5,4},{6,5},{7,6},{9,8},{10,9},{11,10},{13,12},{... | collective-permute-start | bytes 688136 | tf_op jit(solution)/shard_map/ppermute | solution.py:44
  5.0 5.2 %collective-permute-start = (bf16[32,3584]{1,0:T(8,128)(2,1)S(1)}, bf16[32,3584]{1,0:T(8,128)(2,1)}, u32[]{:S(2)}, u32[]{:S(2)}) collective-permute-start(bf16[32,3584]{1,0:T(8,128)(2,1)S(1)} %fusion.13), channel_id=1, source_target_pairs={{0,1},{1,2},{2,3},{4,5},{5,6},{6,7},{8,9},{9,10},{10,11},{12,13},{... | collective-permute-start | bytes 688136 | tf_op jit(solution)/shard_map/ppermute | solution.py:43
  10.5 1.1 %collective-permute-start.9 = (bf16[3,128,256]{2,1,0:T(8,128)(2,1)S(1)}, bf16[3,128,256]{2,1,0:T(8,128)(2,1)}, u32[]{:S(2)}, u32[]{:S(2)}) collective-permute-start(bf16[3,128,256]{2,1,0:T(8,128)(2,1)S(1)} %pad_maximum_fusion), channel_id=1, source_target_pairs={{0,1},{1,2},{2,3},{3,0},{4,5},{5,6},{6,7},{7,4},{8,9},{9,10},{10,1... | collective-permute-start | bytes 589832 | tf_op jit(solution)/shard_map/ppermute | solution.py:189
  11.6 1.1 %collective-permute-start.10 = (bf16[3,128,256]{2,1,0:T(8,128)(2,1)S(1)}, bf16[3,128,256]{2,1,0:T(8,128)(2,1)}, u32[]{:S(2)}, u32[]{:S(2)}) collective-permute-start(bf16[3,128,256]{2,1,0:T(8,128)(2,1)S(1)} %pad_maximum_fusion.1), channel_id=1, source_target_pairs={{0,2},{1,3},{2,0},{3,1},{4,6},{5,7},{6,4},{7,5},{8,10},{9,11},{10,... | collective-permute-start | bytes 589832 | tf_op jit(solution)/shard_map/ppermute | solution.py:189
  13.4 1.3 %collective-permute-start.2 = (bf16[32,3584]{1,0:T(8,128)(2,1)S(1)}, bf16[32,3584]{1,0:T(8,128)(2,1)S(1)}, u32[]{:S(2)}, u32[]{:S(2)}) collective-permute-start(bf16[32,3584]{1,0:T(8,128)(2,1)S(1)} %collective-permute-done.1), channel_id=1, source_target_pairs={{1,0},{2,1},{5,4},{6,5},{9,8},{10,9},{13,12},{14,13},{17,16},{18,1... | collective-permute-start | bytes 688136 | tf_op jit(solution)/shard_map/ppermute | solution.py:44
  14.7 0.8 collective-permute-done
  16.9 1.5 %collective-permute-start.7 = (f32[]{:T(128)}, f32[]{:T(128)}, u32[]{:S(2)}, u32[]{:S(2)}) collective-permute-start(f32[]{:T(128)} %add.53), channel_id=1, source_target_pairs={{0,8},{4,12},{8,0},{12,4},{16,24},{20,28},{24,16},{28,20},{1,9},{5... | collective-permute-start | bytes 20 | tf_op jit(solution)/shard_map/ppermute | solution.py:32
  18.4 2.1 %collective-permute-done.7 = f32[]{:T(128)} collective-permute-done((f32[]{:T(128)}, f32[]{:T(128)}, u32[]{:S(2)}, u32[]{:S(2)}) %collective-permute-start.7) | collective-permute-done | bytes 36 | tf_op jit(solution)/shard_map/ppermute | solution.py:32
  21.1 2.9 %collective-permute-start.8 = (f32[]{:T(128)}, f32[]{:T(128)}, u32[]{:S(2)}, u32[]{:S(2)}) collective-permute-start(f32[]{:T(128)} %add.104), channel_id=1, source_target_pairs={{0,16},{4,20},{8,24},{12,28},{16,0},{20,4},{24,8},{28,12},{1,17},{... | collective-permute-start | bytes 20 | tf_op jit(solution)/shard_map/ppermute | solution.py:32
  24.0 0.7 collective-permute-done.8
  24.7 5.2 %collective-permute-start.11 = (bf16[3,128,256]{2,1,0:T(8,128)(2,1)S(1)}, bf16[3,128,256]{2,1,0:T(8,128)(2,1)}, u32[]{:S(2)}, u32[]{:S(2)}) collective-permute-start(bf16[3,128,256]{2,1,0:T(8,128)(2,1)S(1)} %pad_maximum_fusion.2), channel_id=1, source_target_pairs={{0,3},{1,0},{2,1},{3,2},{4,7},{5,4},{6,5},{7,6},{8,11},{9,8},{10,9... | collective-permute-start | bytes 589832 | tf_op jit(solution)/shard_map/ppermute | solution.py:189
  30.6 3.1 %collective-permute-start.12 = (bf16[3,128,256]{2,1,0:T(8,128)(2,1)S(1)}, bf16[3,128,256]{2,1,0:T(8,128)(2,1)}, u32[]{:S(2)}, u32[]{:S(2)}) collective-permute-start(bf16[3,128,256]{2,1,0:T(8,128)(2,1)S(1)} %pad_maximum_fusion.3), channel_id=1, source_target_pairs={{0,1},{1,2},{2,3},{3,0},{4,5},{5,6},{6,7},{7,4},{8,9},{9,10},{10,1... | collective-permute-start | bytes 589832 | tf_op jit(solution)/shard_map/ppermute | solution.py:189
  33.7 1.3 %collective-permute-start.3 = (bf16[32,3584]{1,0:T(8,128)(2,1)S(1)}, bf16[32,3584]{1,0:T(8,128)(2,1)S(1)}, u32[]{:S(2)}, u32[]{:S(2)}) collective-permute-start(bf16[32,3584]{1,0:T(8,128)(2,1)S(1)} %collective-permute-done.2), channel_id=1, source_target_pairs={{1,0},{5,4},{9,8},{13,12},{17,16},{21,20},{25,24},{29,28}} | collective-permute-start | bytes 688136 | tf_op jit(solution)/shard_map/ppermute | solution.py:44
  35.0 9.4 %collective-permute-done.3 = bf16[32,3584]{1,0:T(8,128)(2,1)S(1)} collective-permute-done((bf16[32,3584]{1,0:T(8,128)(2,1)S(1)}, bf16[32,3584]{1,0:T(8,128)(2,1)S(1)}, u32[]{:S(2)}, u32[]{:S(2)}) %collective-permute-start.3) | collective-permute-done | bytes 229408 | tf_op jit(solution)/shard_map/ppermute | solution.py:44
  45.2 1.2 %collective-permute-start.13 = (bf16[3,128,256]{2,1,0:T(8,128)(2,1)S(1)}, bf16[3,128,256]{2,1,0:T(8,128)(2,1)S(1)}, u32[]{:S(2)}, u32[]{:S(2)}) collective-permute-start(bf16[3,128,256]{2,1,0:T(8,128)(2,1)S(1)} %pad_maximum_fusion.4), channel_id=1, source_target_pairs={{0,2},{1,3},{2,0},{3,1},{4,6},{5,7},{6,4},{7,5},{8,10},{9,11},{10,... | collective-permute-start | bytes 589832 | tf_op jit(solution)/shard_map/ppermute | solution.py:189
  46.4 3.3 %fusion.refs_1_ = bf16[128,512]{1,0:T(8,128)(2,1)} fusion(bf16[3584,512]{1,0:T(8,128)(2,1)} %param.16, bf16[32,3584]{1,0:T(8,128)(2,1)S(1)} %broadcast_select_fusion.2, bf16[32,3584]{1,0:T(8,128)(2,1)S(1)} %broadcast_select_fusion.3, bf16[32,3584]{1,0:T(8,128)(2,1)S(1)} %broadcast_select_fusion.4, bf16[32,3584]{1,0:T(8,128)(2,1)S(1)} %fusion.13, f32[]{:T(128)S(6)} %div.11), kind=kOutput, calls=%fused_computation.3 | convolution fusion | flops 473563136 | bytes 4718596 | tf_op jit(solution)/shard_map/dot_general | solution.py:208
  49.7 1.9 %collective-permute-start.14 = (bf16[3,128,256]{2,1,0:T(8,128)(2,1)S(1)}, bf16[3,128,256]{2,1,0:T(8,128)(2,1)S(1)}, u32[]{:S(2)}, u32[]{:S(2)}) collective-permute-start(bf16[3,128,256]{2,1,0:T(8,128)(2,1)S(1)} %pad_maximum_fusion.5), channel_id=1, source_target_pairs={{0,3},{1,0},{2,1},{3,2},{4,7},{5,4},{6,5},{7,6},{8,11},{9,8},{10,9... | collective-permute-start | bytes 589832 | tf_op jit(solution)/shard_map/ppermute | solution.py:189
  51.7 5.8 %shard_map.112 = (bf16[3,128,256]{2,1,0:T(8,128)(2,1)}, bf16[3,128,256]{2,1,0:T(8,128)(2,1)}, bf16[3,128,256]{2,1,0:T(8,128)(2,1)}, bf16[3,128,256]{2,1,0:T(8,128)(2,1)}) custom-call(s32[1]{0:T(128)} %bitcast.refs_0_, bf16[128,512]{1,0:T(8,128)(2,1)} %fusion.refs_1_, bf16[1,128,2048]{2,1,0:T(8,128)(2,1)} %refs_2_.3, bf16[1,128,2048]{2,1,0:T(8,128)(2,1)} %refs_3_.3, ...), custom_call_target="tpu_custom_call" | custom-call | flops 671088640 | bytes 1572864 | tf_op jit(solution)/shard_map/pallas_call | solution.py:118
  57.5 1.4 %collective-permute-start.15 = (bf16[3,128,256]{2,1,0:T(8,128)(2,1)}, bf16[3,128,256]{2,1,0:T(8,128)(2,1)S(1)}, u32[]{:S(2)}, u32[]{:S(2)}) collective-permute-start(bf16[3,128,256]{2,1,0:T(8,128)(2,1)} %get-tuple-element.14), channel_id=1, source_target_pairs={{0,3},{1,0},{2,1},{3,2},{4,7},{5,4},{6,5},{7,6},{8,11},{9,8},{10,9... | collective-permute-start | bytes 589832 | tf_op jit(solution)/shard_map/ppermute | solution.py:222
  58.9 0.7 collective-permute-start.17
  59.6 1.9 %collective-permute-start.19 = (bf16[3,128,256]{2,1,0:T(8,128)(2,1)}, bf16[3,128,256]{2,1,0:T(8,128)(2,1)S(1)}, u32[]{:S(2)}, u32[]{:S(2)}) collective-permute-start(bf16[3,128,256]{2,1,0:T(8,128)(2,1)} %get-tuple-element.18), channel_id=1, source_target_pairs={{0,1},{1,2},{2,3},{3,0},{4,5},{5,6},{6,7},{7,4},{8,9},{9,10},{10,1... | collective-permute-start | bytes 589832 | tf_op jit(solution)/shard_map/ppermute | solution.py:222
  61.6 0.7 copy-done.12
  62.9 5.9 %shard_map.113 = (bf16[3,128,256]{2,1,0:T(8,128)(2,1)}, bf16[3,128,256]{2,1,0:T(8,128)(2,1)}, bf16[3,128,256]{2,1,0:T(8,128)(2,1)}, bf16[3,128,256]{2,1,0:T(8,128)(2,1)}) custom-call(s32[1]{0:T(128)} %bitcast.refs_0_, bf16[128,512]{1,0:T(8,128)(2,1)} %fusion.refs_1_, bf16[1,128,2048]{2,1,0:T(8,128)(2,1)} %refs_2_.3, bf16[1,128,2048]{2,1,0:T(8,128)(2,1)} %refs_3_.3, ...), custom_call_target="tpu_custom_call" | custom-call | flops 671088640 | bytes 1572864 | tf_op jit(solution)/shard_map/pallas_call | solution.py:118
  68.8 1.9 %collective-permute-start.16 = (bf16[3,128,256]{2,1,0:T(8,128)(2,1)}, bf16[3,128,256]{2,1,0:T(8,128)(2,1)S(1)}, u32[]{:S(2)}, u32[]{:S(2)}) collective-permute-start(bf16[3,128,256]{2,1,0:T(8,128)(2,1)} %get-tuple-element.15), channel_id=1, source_target_pairs={{0,3},{1,0},{2,1},{3,2},{4,7},{5,4},{6,5},{7,6},{8,11},{9,8},{10,9... | collective-permute-start | bytes 589832 | tf_op jit(solution)/shard_map/ppermute | solution.py:222
  70.7 1.5 %collective-permute-start.18 = (bf16[3,128,256]{2,1,0:T(8,128)(2,1)}, bf16[3,128,256]{2,1,0:T(8,128)(2,1)S(1)}, u32[]{:S(2)}, u32[]{:S(2)}) collective-permute-start(bf16[3,128,256]{2,1,0:T(8,128)(2,1)} %get-tuple-element.17), channel_id=1, source_target_pairs={{0,2},{1,3},{2,0},{3,1},{4,6},{5,7},{6,4},{7,5},{8,10},{9,11},{10,... | collective-permute-start | bytes 589832 | tf_op jit(solution)/shard_map/ppermute | solution.py:222
  72.2 2.1 %collective-permute-start.20 = (bf16[3,128,256]{2,1,0:T(8,128)(2,1)}, bf16[3,128,256]{2,1,0:T(8,128)(2,1)S(1)}, u32[]{:S(2)}, u32[]{:S(2)}) collective-permute-start(bf16[3,128,256]{2,1,0:T(8,128)(2,1)} %get-tuple-element.19), channel_id=1, source_target_pairs={{0,1},{1,2},{2,3},{3,0},{4,5},{5,6},{6,7},{7,4},{8,9},{9,10},{10,1... | collective-permute-start | bytes 589832 | tf_op jit(solution)/shard_map/ppermute | solution.py:222
  74.3 11.2 %collective-permute-done.17.refs_5_ = bf16[3,128,256]{2,1,0:T(8,128)(2,1)S(1)} collective-permute-done((bf16[3,128,256]{2,1,0:T(8,128)(2,1)}, bf16[3,128,256]{2,1,0:T(8,128)(2,1)S(1)}, u32[]{:S(2)}, u32[]{:S(2)}) %collective-permute-start.17) | collective-permute-done | bytes 196640 | tf_op jit(solution)/shard_map/ppermute | solution.py:222
  85.6 7.1 %collective-permute-done.18.refs_6_ = bf16[3,128,256]{2,1,0:T(8,128)(2,1)S(1)} collective-permute-done((bf16[3,128,256]{2,1,0:T(8,128)(2,1)}, bf16[3,128,256]{2,1,0:T(8,128)(2,1)S(1)}, u32[]{:S(2)}, u32[]{:S(2)}) %collective-permute-start.18) | collective-permute-done | bytes 196640 | tf_op jit(solution)/shard_map/ppermute | solution.py:222
  93.4 3.1 %place.1 = (bf16[1,128,2048]{2,1,0:T(8,128)(2,1)}, bf16[1,128,2048]{2,1,0:T(8,128)(2,1)}, bf16[1,128,2048]{2,1,0:T(8,128)(2,1)}) custom-call(s32[1]{0:T(128)} %bitcast.refs_0_, bf16[3,128,256]{2,1,0:T(8,128)(2,1)} %get-tuple-element.12.refs_1_, bf16[3,128,256]{2,1,0:T(8,128)(2,1)} %get-tuple-element.13.refs_2_, bf16[3,128,256]{2,1,0:T(8,128)(2,1)} %copy-done.5, ...), custom_call_target="tpu_custom_call" | custom-call | tf_op jit(solution)/shard_map/place/pallas_call | solution.py:158
  (60 shorter events, 4.1 us)
Async XLA Ops:
  0.6 1.0 %copy-start = (bf16[1,64,3584]{2,1,0:T(8,128)(2,1)S(1)}, bf16[1,64,3584]{2,1,0:T(8,128)(2,1)}, u32[]{:S(2)}) copy-start(bf16[1,64,3584]{2,1,0:T(8,128)(2,1)} %param.12) | copy-start | bytes 1376260
  0.6 1.7 %copy-start.1 = (bf16[1,64,3584]{2,1,0:T(8,128)(2,1)S(1)}, bf16[1,64,3584]{2,1,0:T(8,128)(2,1)}, u32[]{:S(2)}) copy-start(bf16[1,64,3584]{2,1,0:T(8,128)(2,1)} %param.11) | copy-start | bytes 1376260
  1.7 1.4 %copy-start.11 = (f32[3584]{0:T(1024)S(1)}, f32[3584]{0:T(1024)}, u32[]{:S(2)}) copy-start(f32[3584]{0:T(1024)} %param.13) | copy-start | bytes 43012
  2.4 7.9 %copy-start.2 = (bf16[1,128,2048]{2,1,0:T(8,128)(2,1)S(1)}, bf16[1,128,2048]{2,1,0:T(8,128)(2,1)}, u32[]{:S(2)}) copy-start(bf16[1,128,2048]{2,1,0:T(8,128)(2,1)} %refs_2_.3) | copy-start | bytes 1572868
  2.4 7.9 %copy-start.3 = (bf16[1,128,2048]{2,1,0:T(8,128)(2,1)S(1)}, bf16[1,128,2048]{2,1,0:T(8,128)(2,1)}, u32[]{:S(2)}) copy-start(bf16[1,128,2048]{2,1,0:T(8,128)(2,1)} %refs_3_.3) | copy-start | bytes 1572868
  2.4 7.9 %copy-start.4 = (bf16[1,128,2048]{2,1,0:T(8,128)(2,1)S(1)}, bf16[1,128,2048]{2,1,0:T(8,128)(2,1)}, u32[]{:S(2)}) copy-start(bf16[1,128,2048]{2,1,0:T(8,128)(2,1)} %refs_4_.3) | copy-start | bytes 1572868
  3.7 9.7 %collective-permute-start.1 = (bf16[32,3584]{1,0:T(8,128)(2,1)S(1)}, bf16[32,3584]{1,0:T(8,128)(2,1)S(1)}, u32[]{:S(2)}, u32[]{:S(2)}) collective-permute-start(bf16[32,3584]{1,0:T(8,128)(2,1)S(1)} %fusion.13), channel_id=1, source_target_pairs={{1,0},{2,1},{3,2},{5,4},{6,5},{7,6},{9,8},{10,9},{11,10},{13,12},{... | collective-permute-start | bytes 688136 | tf_op jit(solution)/shard_map/ppermute | solution.py:44
  5.0 10.5 %collective-permute-start = (bf16[32,3584]{1,0:T(8,128)(2,1)S(1)}, bf16[32,3584]{1,0:T(8,128)(2,1)}, u32[]{:S(2)}, u32[]{:S(2)}) collective-permute-start(bf16[32,3584]{1,0:T(8,128)(2,1)S(1)} %fusion.13), channel_id=1, source_target_pairs={{0,1},{1,2},{2,3},{4,5},{5,6},{6,7},{8,9},{9,10},{10,11},{12,13},{... | collective-permute-start | bytes 688136 | tf_op jit(solution)/shard_map/ppermute | solution.py:43
  10.2 6.0 %collective-permute-start.6 = (f32[]{:T(128)}, f32[]{:T(128)}, u32[]{:S(2)}, u32[]{:S(2)}) collective-permute-start(f32[]{:T(128)} %bitcast.4), channel_id=1, source_target_pairs={{0,4},{4,0},{8,12},{12,8},{16,20},{20,16},{24,28},{28,24},{1,5},{5... | collective-permute-start | bytes 20 | tf_op jit(solution)/shard_map/ppermute | solution.py:32
  10.5 39.3 %collective-permute-start.9 = (bf16[3,128,256]{2,1,0:T(8,128)(2,1)S(1)}, bf16[3,128,256]{2,1,0:T(8,128)(2,1)}, u32[]{:S(2)}, u32[]{:S(2)}) collective-permute-start(bf16[3,128,256]{2,1,0:T(8,128)(2,1)S(1)} %pad_maximum_fusion), channel_id=1, source_target_pairs={{0,1},{1,2},{2,3},{3,0},{4,5},{5,6},{6,7},{7,4},{8,9},{9,10},{10,1... | collective-permute-start | bytes 589832 | tf_op jit(solution)/shard_map/ppermute | solution.py:189
  11.6 40.1 %collective-permute-start.10 = (bf16[3,128,256]{2,1,0:T(8,128)(2,1)S(1)}, bf16[3,128,256]{2,1,0:T(8,128)(2,1)}, u32[]{:S(2)}, u32[]{:S(2)}) collective-permute-start(bf16[3,128,256]{2,1,0:T(8,128)(2,1)S(1)} %pad_maximum_fusion.1), channel_id=1, source_target_pairs={{0,2},{1,3},{2,0},{3,1},{4,6},{5,7},{6,4},{7,5},{8,10},{9,11},{10,... | collective-permute-start | bytes 589832 | tf_op jit(solution)/shard_map/ppermute | solution.py:189
  13.4 17.2 %collective-permute-start.2 = (bf16[32,3584]{1,0:T(8,128)(2,1)S(1)}, bf16[32,3584]{1,0:T(8,128)(2,1)S(1)}, u32[]{:S(2)}, u32[]{:S(2)}) collective-permute-start(bf16[32,3584]{1,0:T(8,128)(2,1)S(1)} %collective-permute-done.1), channel_id=1, source_target_pairs={{1,0},{2,1},{5,4},{6,5},{9,8},{10,9},{13,12},{14,13},{17,16},{18,1... | collective-permute-start | bytes 688136 | tf_op jit(solution)/shard_map/ppermute | solution.py:44
  15.5 18.2 %collective-permute-start.4 = (bf16[32,3584]{1,0:T(8,128)(2,1)}, bf16[32,3584]{1,0:T(8,128)(2,1)S(1)}, u32[]{:S(2)}, u32[]{:S(2)}) collective-permute-start(bf16[32,3584]{1,0:T(8,128)(2,1)} %collective-permute-done), channel_id=1, source_target_pairs={{1,2},{2,3},{5,6},{6,7},{9,10},{10,11},{13,14},{14,15},{17,18},{18... | collective-permute-start | bytes 688136 | tf_op jit(solution)/shard_map/ppermute | solution.py:43
  16.9 3.6 %collective-permute-start.7 = (f32[]{:T(128)}, f32[]{:T(128)}, u32[]{:S(2)}, u32[]{:S(2)}) collective-permute-start(f32[]{:T(128)} %add.53), channel_id=1, source_target_pairs={{0,8},{4,12},{8,0},{12,4},{16,24},{20,28},{24,16},{28,20},{1,9},{5... | collective-permute-start | bytes 20 | tf_op jit(solution)/shard_map/ppermute | solution.py:32
  21.1 3.6 %collective-permute-start.8 = (f32[]{:T(128)}, f32[]{:T(128)}, u32[]{:S(2)}, u32[]{:S(2)}) collective-permute-start(f32[]{:T(128)} %add.104), channel_id=1, source_target_pairs={{0,16},{4,20},{8,24},{12,28},{16,0},{20,4},{24,8},{28,12},{1,17},{... | collective-permute-start | bytes 20 | tf_op jit(solution)/shard_map/ppermute | solution.py:32
  24.7 27.0 %collective-permute-start.11 = (bf16[3,128,256]{2,1,0:T(8,128)(2,1)S(1)}, bf16[3,128,256]{2,1,0:T(8,128)(2,1)}, u32[]{:S(2)}, u32[]{:S(2)}) collective-permute-start(bf16[3,128,256]{2,1,0:T(8,128)(2,1)S(1)} %pad_maximum_fusion.2), channel_id=1, source_target_pairs={{0,3},{1,0},{2,1},{3,2},{4,7},{5,4},{6,5},{7,6},{8,11},{9,8},{10,9... | collective-permute-start | bytes 589832 | tf_op jit(solution)/shard_map/ppermute | solution.py:189
  30.6 29.0 %collective-permute-start.12 = (bf16[3,128,256]{2,1,0:T(8,128)(2,1)S(1)}, bf16[3,128,256]{2,1,0:T(8,128)(2,1)}, u32[]{:S(2)}, u32[]{:S(2)}) collective-permute-start(bf16[3,128,256]{2,1,0:T(8,128)(2,1)S(1)} %pad_maximum_fusion.3), channel_id=1, source_target_pairs={{0,1},{1,2},{2,3},{3,0},{4,5},{5,6},{6,7},{7,4},{8,9},{9,10},{10,1... | collective-permute-start | bytes 589832 | tf_op jit(solution)/shard_map/ppermute | solution.py:189
  33.7 10.8 %collective-permute-start.3 = (bf16[32,3584]{1,0:T(8,128)(2,1)S(1)}, bf16[32,3584]{1,0:T(8,128)(2,1)S(1)}, u32[]{:S(2)}, u32[]{:S(2)}) collective-permute-start(bf16[32,3584]{1,0:T(8,128)(2,1)S(1)} %collective-permute-done.2), channel_id=1, source_target_pairs={{1,0},{5,4},{9,8},{13,12},{17,16},{21,20},{25,24},{29,28}} | collective-permute-start | bytes 688136 | tf_op jit(solution)/shard_map/ppermute | solution.py:44
  44.5 0.7 collective-permute-start.5
  45.2 16.4 %collective-permute-start.13 = (bf16[3,128,256]{2,1,0:T(8,128)(2,1)S(1)}, bf16[3,128,256]{2,1,0:T(8,128)(2,1)S(1)}, u32[]{:S(2)}, u32[]{:S(2)}) collective-permute-start(bf16[3,128,256]{2,1,0:T(8,128)(2,1)S(1)} %pad_maximum_fusion.4), channel_id=1, source_target_pairs={{0,2},{1,3},{2,0},{3,1},{4,6},{5,7},{6,4},{7,5},{8,10},{9,11},{10,... | collective-permute-start | bytes 589832 | tf_op jit(solution)/shard_map/ppermute | solution.py:189
  49.7 11.8 %collective-permute-start.14 = (bf16[3,128,256]{2,1,0:T(8,128)(2,1)S(1)}, bf16[3,128,256]{2,1,0:T(8,128)(2,1)S(1)}, u32[]{:S(2)}, u32[]{:S(2)}) collective-permute-start(bf16[3,128,256]{2,1,0:T(8,128)(2,1)S(1)} %pad_maximum_fusion.5), channel_id=1, source_target_pairs={{0,3},{1,0},{2,1},{3,2},{4,7},{5,4},{6,5},{7,6},{8,11},{9,8},{10,9... | collective-permute-start | bytes 589832 | tf_op jit(solution)/shard_map/ppermute | solution.py:189
  57.5 14.7 %collective-permute-start.15 = (bf16[3,128,256]{2,1,0:T(8,128)(2,1)}, bf16[3,128,256]{2,1,0:T(8,128)(2,1)S(1)}, u32[]{:S(2)}, u32[]{:S(2)}) collective-permute-start(bf16[3,128,256]{2,1,0:T(8,128)(2,1)} %get-tuple-element.14), channel_id=1, source_target_pairs={{0,3},{1,0},{2,1},{3,2},{4,7},{5,4},{6,5},{7,6},{8,11},{9,8},{10,9... | collective-permute-start | bytes 589832 | tf_op jit(solution)/shard_map/ppermute | solution.py:222
  58.9 26.6 %collective-permute-start.17 = (bf16[3,128,256]{2,1,0:T(8,128)(2,1)}, bf16[3,128,256]{2,1,0:T(8,128)(2,1)S(1)}, u32[]{:S(2)}, u32[]{:S(2)}) collective-permute-start(bf16[3,128,256]{2,1,0:T(8,128)(2,1)} %get-tuple-element.16), channel_id=1, source_target_pairs={{0,2},{1,3},{2,0},{3,1},{4,6},{5,7},{6,4},{7,5},{8,10},{9,11},{10,... | collective-permute-start | bytes 589832 | tf_op jit(solution)/shard_map/ppermute | solution.py:222
  59.6 25.9 %collective-permute-start.19 = (bf16[3,128,256]{2,1,0:T(8,128)(2,1)}, bf16[3,128,256]{2,1,0:T(8,128)(2,1)S(1)}, u32[]{:S(2)}, u32[]{:S(2)}) collective-permute-start(bf16[3,128,256]{2,1,0:T(8,128)(2,1)} %get-tuple-element.18), channel_id=1, source_target_pairs={{0,1},{1,2},{2,3},{3,0},{4,5},{5,6},{6,7},{7,4},{8,9},{9,10},{10,1... | collective-permute-start | bytes 589832 | tf_op jit(solution)/shard_map/ppermute | solution.py:222
  68.8 16.7 %collective-permute-start.16 = (bf16[3,128,256]{2,1,0:T(8,128)(2,1)}, bf16[3,128,256]{2,1,0:T(8,128)(2,1)S(1)}, u32[]{:S(2)}, u32[]{:S(2)}) collective-permute-start(bf16[3,128,256]{2,1,0:T(8,128)(2,1)} %get-tuple-element.15), channel_id=1, source_target_pairs={{0,3},{1,0},{2,1},{3,2},{4,7},{5,4},{6,5},{7,6},{8,11},{9,8},{10,9... | collective-permute-start | bytes 589832 | tf_op jit(solution)/shard_map/ppermute | solution.py:222
  70.7 22.0 %collective-permute-start.18 = (bf16[3,128,256]{2,1,0:T(8,128)(2,1)}, bf16[3,128,256]{2,1,0:T(8,128)(2,1)S(1)}, u32[]{:S(2)}, u32[]{:S(2)}) collective-permute-start(bf16[3,128,256]{2,1,0:T(8,128)(2,1)} %get-tuple-element.17), channel_id=1, source_target_pairs={{0,2},{1,3},{2,0},{3,1},{4,6},{5,7},{6,4},{7,5},{8,10},{9,11},{10,... | collective-permute-start | bytes 589832 | tf_op jit(solution)/shard_map/ppermute | solution.py:222
  72.2 20.4 %copy-start.5 = (bf16[3,128,256]{2,1,0:T(8,128)(2,1)}, bf16[3,128,256]{2,1,0:T(8,128)(2,1)S(1)}, u32[]{:S(2)}) copy-start(bf16[3,128,256]{2,1,0:T(8,128)(2,1)S(1)} %collective-permute-done.15.refs_3_) | copy-start | bytes 589828
  72.2 20.4 %collective-permute-start.20 = (bf16[3,128,256]{2,1,0:T(8,128)(2,1)}, bf16[3,128,256]{2,1,0:T(8,128)(2,1)S(1)}, u32[]{:S(2)}, u32[]{:S(2)}) collective-permute-start(bf16[3,128,256]{2,1,0:T(8,128)(2,1)} %get-tuple-element.19), channel_id=1, source_target_pairs={{0,1},{1,2},{2,3},{3,0},{4,5},{5,6},{6,7},{7,4},{8,9},{9,10},{10,1... | collective-permute-start | bytes 589832 | tf_op jit(solution)/shard_map/ppermute | solution.py:222
  85.5 7.2 %copy-start.6 = (bf16[3,128,256]{2,1,0:T(8,128)(2,1)}, bf16[3,128,256]{2,1,0:T(8,128)(2,1)S(1)}, u32[]{:S(2)}) copy-start(bf16[3,128,256]{2,1,0:T(8,128)(2,1)S(1)} %collective-permute-done.17.refs_5_) | copy-start | bytes 589828
  85.5 7.2 %copy-start.7 = (bf16[3,128,256]{2,1,0:T(8,128)(2,1)}, bf16[3,128,256]{2,1,0:T(8,128)(2,1)S(1)}, u32[]{:S(2)}) copy-start(bf16[3,128,256]{2,1,0:T(8,128)(2,1)S(1)} %collective-permute-done.19.refs_7_) | copy-start | bytes 589828
  85.5 7.2 %copy-start.8 = (bf16[3,128,256]{2,1,0:T(8,128)(2,1)}, bf16[3,128,256]{2,1,0:T(8,128)(2,1)S(1)}, u32[]{:S(2)}) copy-start(bf16[3,128,256]{2,1,0:T(8,128)(2,1)S(1)} %collective-permute-done.16.refs_4_) | copy-start | bytes 589828
  92.7 0.8 copy-start.10
  (3 other events, 2.1 us)
where the time goes:
time: 97.9 us; the launch traced here: 96.6 us
  starting transfers between devices  38 us (39%)
  waiting for transfers between devices  31.4 us (32%)
  Pallas kernels  14.8 us (15%)
  local copies, waits for them, and re-layouts  3.92 us (4%)
  between operations  3.51 us (4%)
  matrix products  3.34 us (3%)
  other arithmetic  1.58 us (2%)
    ppermute x6, waiting for transfers between devices, work(): lax.ppermute(grads[k], 'tensor', [(i, (i - k) % count) for i in range(cou...  18.3 us
    ppermute x6, starting transfers between devices, work(): lax.ppermute(jnp.stack([columns(a, k, g) for a in (img_query, img_key, im...  13.6 us
    pallas_call x2, Pallas kernels, attend(): pl.pallas_call(functools.partial(attend_kernel, count, HD ** (-0.5), chun...  11.7 us
    ppermute x6, starting transfers between devices, work(): lax.ppermute(grads[k], 'tensor', [(i, (i - k) % count) for i in range(cou...  9.58 us
    ppermute x3, waiting for transfers between devices, relayed_blocks(): lax.ppermute(down, axis, [(i + 1, i) for i in range(size - 1 - step)])  9.45 us
    ppermute x3, starting transfers between devices, relayed_blocks(): up = lax.ppermute(up, axis, [(i, i + 1) for i in range(step, size - 1)])  6.57 us
    ppermute x3, starting transfers between devices, total_over(): lax.ppermute(value, axis, [(i, i ^ step) for i in range(size)])  4.34 us
    ppermute x3, starting transfers between devices, relayed_blocks(): lax.ppermute(down, axis, [(i + 1, i) for i in range(size - 1 - step)])  3.87 us
  transfers between devices with their start and end apart: 21, of which 6 were waited for; matrix products, arithmetic and copies ran while one was open for 4% of the time, Pallas kernels for 12%

commit v1 on v0

--- a/solution.py
+++ b/solution.py
@@ -10,7 +10,6 @@
 
 HD = 128
 GW = 64
-GROUPS = 2
 
 
 def norm_backward(hidden, cotangent, gain):
@@ -21,6 +20,10 @@
     return (inv_rms * scaled_cot - hidden_f * inv_rms * inv_rms * inv_rms * mixed).astype(
         jnp.bfloat16
     )
+
+
+def head_groups(heads):
+    return (1, 1, heads - 2) if heads > 2 else (heads,)
 
 
 def total_over(value, axis):
@@ -105,13 +108,11 @@
         out[2] = dv_s[at].astype(jnp.bfloat16)
 
 
-def attend(here, handed, own, blocks, group, groups, count):
+def attend(here, handed, own, blocks, first, heads, count):
     rows = own[0].shape[1]
     local_heads = handed.shape[1] // HD
-    heads = local_heads // groups
     length = rows * count
     chunk = min(256, length)
-    first = group * heads
     own_spec = pl.BlockSpec((1, rows, HD), lambda h, t: (0, 0, t[0] * local_heads + first + h))
     block_spec = pl.BlockSpec((3, rows, HD), lambda h, t: (0, 0, h))
     flops = 10 * heads * length * length * HD
@@ -136,36 +137,45 @@
     )(here, handed, *own, *blocks)
 
 
-def place_kernel(count, groups, *refs):
-    parts = refs[1 : 1 + count * groups]
-    outs = refs[1 + count * groups :]
+def place_kernel(count, first, *refs):
+    here = refs[0][0]
+    parts = refs[1 : 1 + count]
+    outs = refs[-4:-1]
+    sems = refs[-1]
     width = parts[0].shape[2]
-    for k in range(count):
-
-        @pl.when(pl.program_id(0) == k)
-        def _():
-            for g in range(groups):
-                for i, out in enumerate(outs):
-                    out[0, :, pl.ds(g * width, width)] = parts[k * groups + g][i]
-
-
-def place(here, parts, count):
-    groups = len(parts[0])
-    rows, width = parts[0][0].shape[1:]
-    flat = [part for ranked in parts for part in ranked]
-    part_spec = pl.BlockSpec((3, rows, width), lambda k, t: (0, 0, 0))
-    out_spec = pl.BlockSpec((1, rows, width * groups), lambda k, t: (0, 0, lax.rem(t[0] + k, count)))
+    own_width = outs[0].shape[2] // count
+    copies = []
+    for k, part in enumerate(parts):
+        column = pl.multiple_of(lax.rem(here + k, count) * own_width + first, HD)
+        for i, out in enumerate(outs):
+            copies.append(
+                pltpu.make_async_copy(
+                    part.at[i], out.at[0, :, pl.ds(column, width)], sems.at[3 * k + i]
+                )
+            )
+    for copy in copies:
+        copy.start()
+    for copy in copies:
+        copy.wait()
+
+
+def place(here, parts, outs, shape, first):
+    count = len(parts)
+    anywhere = pl.BlockSpec(memory_space=pl.ANY)
+    held = len(outs)
     return pl.pallas_call(
-        functools.partial(place_kernel, count, groups),
-        grid_spec=pltpu.PrefetchScalarGridSpec(
-            num_scalar_prefetch=1,
-            grid=(count,),
-            in_specs=[part_spec] * len(flat),
-            out_specs=[out_spec] * 3,
+        functools.partial(place_kernel, count, first),
+        in_specs=[pl.BlockSpec(memory_space=pltpu.SMEM)]
+        + [pl.BlockSpec(memory_space=pltpu.VMEM)] * count
+        + [anywhere] * held,
+        out_specs=[anywhere] * 3,
+        out_shape=[jax.ShapeDtypeStruct(shape, jnp.bfloat16)] * 3,
+        input_output_aliases={1 + count + i: i for i in range(held)},
+        scratch_shapes=[pltpu.SemaphoreType.DMA((3 * count,))],
+        cost_estimate=pl.CostEstimate(
+            flops=0, bytes_accessed=4 * count * parts[0].size, transcendentals=0
         ),
-        out_shape=[jax.ShapeDtypeStruct((1, rows, width * groups * count), jnp.bfloat16)] * 3,
-        name="place",
-    )(here, *flat)
+    )(here, *parts, *outs)
 
 
 def work(
@@ -175,15 +185,15 @@
     here = lax.axis_index("tensor")
     place_of = here[None].astype(jnp.int32)
     own_width = img_query.shape[2] // count
-    groups = min(GROUPS, own_width // HD)
-    width = own_width // groups
+    groups = head_groups(own_width // HD)
+    starts = [sum(groups[:g]) for g in range(len(groups))]
 
     def columns(array, k, g):
-        first = lax.rem(here + k, count) * own_width + g * width
-        return lax.dynamic_slice_in_dim(array[0], first, width, 1)
+        first = lax.rem(here + k, count) * own_width + starts[g] * HD
+        return lax.dynamic_slice_in_dim(array[0], first, groups[g] * HD, 1)
 
     arrived = []
-    for g in range(groups):
+    for g in range(len(groups)):
         arrived.append(
             [
                 lax.ppermute(
@@ -211,17 +221,17 @@
         * reward_weight
     ).astype(jnp.bfloat16)
 
-    parts = [[] for _ in range(count)]
-    for g in range(groups):
+    outs = ()
+    for g, heads in enumerate(groups):
         grads = attend(
-            place_of, handed, (img_query, img_key, img_value), arrived[g], g, groups, count
+            place_of, handed, (img_query, img_key, img_value), arrived[g], starts[g], heads, count
         )
-        parts[0].append(grads[0])
-        for k in range(1, count):
-            parts[k].append(
-                lax.ppermute(grads[k], "tensor", [(i, (i - k) % count) for i in range(count)])
-            )
-    return tuple(place(place_of, parts, count))
+        parts = [grads[0]] + [
+            lax.ppermute(grads[k], "tensor", [(i, (i - k) % count) for i in range(count)])
+            for k in range(1, count)
+        ]
+        outs = place(place_of, parts, outs, img_query.shape, starts[g] * HD)
+    return tuple(outs)
 
 
 def solution(mesh):

time: 97.9 us -> 108 us (1.10)
  starting transfers between devices: 38 us -> 45.9 us
  waiting for transfers between devices: 31.4 us -> 25.7 us
  Pallas kernels: 14.8 us -> 19.4 us
  other arithmetic: 1.58 us -> 2.86 us
    ppermute x6 -> x9, starting transfers between devices: 9.58 us -> 16.4 us  [work(): lax.ppermute(grads[k], 'tensor', [(i, (i - k) % count) for i in range(cou...]
    ppermute x3, waiting for transfers between devices: 9.45 us -> 6.58 us  [relayed_blocks(): lax.ppermute(down, axis, [(i + 1, i) for i in range(size - 1 - step)])]
    ppermute x6 -> x9, waiting for transfers between devices: 18.3 us -> 15.5 us  [work(): lax.ppermute(grads[k], 'tensor', [(i, (i - k) % count) for i in range(cou...]
    pallas_call x1 -> x3, Pallas kernels: 3.15 us -> 5.93 us  [place(): pl.pallas_call(functools.partial(place_kernel, count, first), in_specs=[p...]
    pallas_call x2 -> x3, Pallas kernels: 11.7 us -> 13.4 us  [attend(): pl.pallas_call(functools.partial(attend_kernel, count, HD ** (-0.5), chun...]
    another operation x6 -> x9, other arithmetic: 0.15 us -> 1.44 us  [work(): jnp.stack([columns(a, k, g) for a in (img_query, img_key, img_value)])]
    ppermute x6 -> x9, starting transfers between devices: 13.6 us -> 14.9 us  [work(): lax.ppermute(jnp.stack([columns(a, k, g) for a in (img_query, img_key, im...]
    ppermute x6 -> x9, waiting for transfers between devices: 0.02 us -> 1.19 us  [work(): lax.ppermute(jnp.stack([columns(a, k, g) for a in (img_query, img_key, im...]
  transfers between devices with their start and end apart: 21 -> 27, of which waited for: 6 -> 5; matrix products, arithmetic and copies ran while one was open for 4% -> 5% of each run, Pallas kernels for 12% -> 16%
where the time goes in v1:
time: 108 us; the launch traced here: 106 us
  starting transfers between devices  45.9 us (42%)
  waiting for transfers between devices  25.7 us (24%)
  Pallas kernels  19.4 us (18%)
  local copies, waits for them, and re-layouts  4.77 us (4%)
  between operations  3.73 us (3%)
  matrix products  3.34 us (3%)
  other arithmetic  2.86 us (3%)
    ppermute x9, starting transfers between devices, work(): lax.ppermute(grads[k], 'tensor', [(i, (i - k) % count) for i in range(cou...  16.4 us
    ppermute x9, waiting for transfers between devices, work(): lax.ppermute(grads[k], 'tensor', [(i, (i - k) % count) for i in range(cou...  15.5 us
    ppermute x9, starting transfers between devices, work(): lax.ppermute(jnp.stack([columns(a, k, g) for a in (img_query, img_key, im...  14.9 us
    pallas_call x3, Pallas kernels, attend(): pl.pallas_call(functools.partial(attend_kernel, count, HD ** (-0.5), chun...  13.4 us
    ppermute x3, waiting for transfers between devices, relayed_blocks(): lax.ppermute(down, axis, [(i + 1, i) for i in range(size - 1 - step)])  6.58 us
    pallas_call x3, Pallas kernels, place(): pl.pallas_call(functools.partial(place_kernel, count, first), in_specs=[p...  5.93 us
    ppermute x3, starting transfers between devices, relayed_blocks(): up = lax.ppermute(up, axis, [(i, i + 1) for i in range(step, size - 1)])  5.9 us
    ppermute x3, starting transfers between devices, total_over(): lax.ppermute(value, axis, [(i, i ^ step) for i in range(size)])  4.85 us
  transfers between devices with their start and end apart: 27, of which 5 were waited for; matrix products, arithmetic and copies ran while one was open for 5% of the time, Pallas kernels for 16%

profile of v1, /device:TPU:2, one launch (start us, length us, event | category | flops | bytes accessed | tf_op | source)
XLA Modules:
  0.0 105.7 jit_solution(12111913177134211145)
XLA Ops:
  0.7 0.7 compare_and_fusion
  3.7 1.3 %collective-permute-start.1 = (bf16[32,3584]{1,0:T(8,128)(2,1)S(1)}, bf16[32,3584]{1,0:T(8,128)(2,1)S(1)}, u32[]{:S(2)}, u32[]{:S(2)}) collective-permute-start(bf16[32,3584]{1,0:T(8,128)(2,1)S(1)} %fusion.13), channel_id=1, source_target_pairs={{1,0},{2,1},{3,2},{5,4},{6,5},{7,6},{9,8},{10,9},{11,10},{13,12},{... | collective-permute-start | bytes 688136 | tf_op jit(solution)/shard_map/ppermute | solution.py:47
  5.0 4.6 %collective-permute-start = (bf16[32,3584]{1,0:T(8,128)(2,1)S(1)}, bf16[32,3584]{1,0:T(8,128)(2,1)S(1)}, u32[]{:S(2)}, u32[]{:S(2)}) collective-permute-start(bf16[32,3584]{1,0:T(8,128)(2,1)S(1)} %fusion.13), channel_id=1, source_target_pairs={{0,1},{1,2},{2,3},{4,5},{5,6},{6,7},{8,9},{9,10},{10,11},{12,13},{... | collective-permute-start | bytes 688136 | tf_op jit(solution)/shard_map/ppermute | solution.py:46
  10.6 1.6 %collective-permute-start.21 = (bf16[3,128,128]{2,1,0:T(8,128)(2,1)}, bf16[3,128,128]{2,1,0:T(8,128)(2,1)}, u32[]{:S(2)}, u32[]{:S(2)}) collective-permute-start(bf16[3,128,128]{2,1,0:T(8,128)(2,1)} %pad_maximum_fusion.6), channel_id=1, source_target_pairs={{0,1},{1,2},{2,3},{3,0},{4,5},{5,6},{6,7},{7,4},{8,9},{9,10},{10,1... | collective-permute-start | bytes 294920 | tf_op jit(solution)/shard_map/ppermute | solution.py:199
  12.8 1.0 collective-permute-start.22
  14.8 1.3 %collective-permute-start.2 = (bf16[32,3584]{1,0:T(8,128)(2,1)S(1)}, bf16[32,3584]{1,0:T(8,128)(2,1)S(1)}, u32[]{:S(2)}, u32[]{:S(2)}) collective-permute-start(bf16[32,3584]{1,0:T(8,128)(2,1)S(1)} %collective-permute-done.1), channel_id=1, source_target_pairs={{1,0},{2,1},{5,4},{6,5},{9,8},{10,9},{13,12},{14,13},{17,16},{18,1... | collective-permute-start | bytes 688136 | tf_op jit(solution)/shard_map/ppermute | solution.py:47
  17.4 1.9 %collective-permute-start.7 = (f32[]{:T(128)}, f32[]{:T(128)}, u32[]{:S(2)}, u32[]{:S(2)}) collective-permute-start(f32[]{:T(128)} %add.69), channel_id=1, source_target_pairs={{0,8},{4,12},{8,0},{12,4},{16,24},{20,28},{24,16},{28,20},{1,9},{5... | collective-permute-start | bytes 20 | tf_op jit(solution)/shard_map/ppermute | solution.py:35
  19.3 1.7 %collective-permute-done.7 = f32[]{:T(128)} collective-permute-done((f32[]{:T(128)}, f32[]{:T(128)}, u32[]{:S(2)}, u32[]{:S(2)}) %collective-permute-start.7) | collective-permute-done | bytes 36 | tf_op jit(solution)/shard_map/ppermute | solution.py:35
  21.7 2.9 %collective-permute-start.8 = (f32[]{:T(128)}, f32[]{:T(128)}, u32[]{:S(2)}, u32[]{:S(2)}) collective-permute-start(f32[]{:T(128)} %add.70), channel_id=1, source_target_pairs={{0,16},{4,20},{8,24},{12,28},{16,0},{20,4},{24,8},{28,12},{1,17},{... | collective-permute-start | bytes 20 | tf_op jit(solution)/shard_map/ppermute | solution.py:35
  25.2 4.3 %collective-permute-start.23 = (bf16[3,128,128]{2,1,0:T(8,128)(2,1)S(1)}, bf16[3,128,128]{2,1,0:T(8,128)(2,1)S(1)}, u32[]{:S(2)}, u32[]{:S(2)}) collective-permute-start(bf16[3,128,128]{2,1,0:T(8,128)(2,1)S(1)} %pad_maximum_fusion.8), channel_id=1, source_target_pairs={{0,3},{1,0},{2,1},{3,2},{4,7},{5,4},{6,5},{7,6},{8,11},{9,8},{10,9... | collective-permute-start | bytes 294920 | tf_op jit(solution)/shard_map/ppermute | solution.py:199
  30.2 1.5 %collective-permute-start.15 = (bf16[3,128,128]{2,1,0:T(8,128)(2,1)S(1)}, bf16[3,128,128]{2,1,0:T(8,128)(2,1)S(1)}, u32[]{:S(2)}, u32[]{:S(2)}) collective-permute-start(bf16[3,128,128]{2,1,0:T(8,128)(2,1)S(1)} %pad_maximum_fusion.3), channel_id=1, source_target_pairs={{0,1},{1,2},{2,3},{3,0},{4,5},{5,6},{6,7},{7,4},{8,9},{9,10},{10,1... | collective-permute-start | bytes 294920 | tf_op jit(solution)/shard_map/ppermute | solution.py:199
  31.7 1.3 %collective-permute-start.3 = (bf16[32,3584]{1,0:T(8,128)(2,1)S(1)}, bf16[32,3584]{1,0:T(8,128)(2,1)S(1)}, u32[]{:S(2)}, u32[]{:S(2)}) collective-permute-start(bf16[32,3584]{1,0:T(8,128)(2,1)S(1)} %collective-permute-done.2), channel_id=1, source_target_pairs={{1,0},{5,4},{9,8},{13,12},{17,16},{21,20},{25,24},{29,28}} | collective-permute-start | bytes 688136 | tf_op jit(solution)/shard_map/ppermute | solution.py:47
  33.0 6.6 %collective-permute-done.3 = bf16[32,3584]{1,0:T(8,128)(2,1)S(1)} collective-permute-done((bf16[32,3584]{1,0:T(8,128)(2,1)S(1)}, bf16[32,3584]{1,0:T(8,128)(2,1)S(1)}, u32[]{:S(2)}, u32[]{:S(2)}) %collective-permute-start.3) | collective-permute-done | bytes 229408 | tf_op jit(solution)/shard_map/ppermute | solution.py:47
  40.8 2.0 %collective-permute-start.17 = (bf16[3,128,128]{2,1,0:T(8,128)(2,1)S(1)}, bf16[3,128,128]{2,1,0:T(8,128)(2,1)S(1)}, u32[]{:S(2)}, u32[]{:S(2)}) collective-permute-start(bf16[3,128,128]{2,1,0:T(8,128)(2,1)S(1)} %pad_maximum_fusion.5), channel_id=1, source_target_pairs={{0,3},{1,0},{2,1},{3,2},{4,7},{5,4},{6,5},{7,6},{8,11},{9,8},{10,9... | collective-permute-start | bytes 294920 | tf_op jit(solution)/shard_map/ppermute | solution.py:199
  42.8 2.0 %collective-permute-start.10 = (bf16[3,128,256]{2,1,0:T(8,128)(2,1)S(1)}, bf16[3,128,256]{2,1,0:T(8,128)(2,1)S(1)}, u32[]{:S(2)}, u32[]{:S(2)}) collective-permute-start(bf16[3,128,256]{2,1,0:T(8,128)(2,1)S(1)} %pad_maximum_fusion.1), channel_id=1, source_target_pairs={{0,2},{1,3},{2,0},{3,1},{4,6},{5,7},{6,4},{7,5},{8,10},{9,11},{10,... | collective-permute-start | bytes 589832 | tf_op jit(solution)/shard_map/ppermute | solution.py:199
  44.8 1.0 collective-permute-start.11
  45.8 1.0 collective-permute-start.9
  46.9 3.3 %fusion.refs_1_ = bf16[128,512]{1,0:T(8,128)(2,1)} fusion(bf16[3584,512]{1,0:T(8,128)(2,1)} %param.16, bf16[32,3584]{1,0:T(8,128)(2,1)S(1)} %broadcast_select_fusion.2, bf16[32,3584]{1,0:T(8,128)(2,1)S(1)} %broadcast_select_fusion.3, bf16[32,3584]{1,0:T(8,128)(2,1)S(1)} %broadcast_select_fusion.4, bf16[32,3584]{1,0:T(8,128)(2,1)S(1)} %fusion.13, f32[]{:T(128)S(6)} %div.11), kind=kOutput, calls=%fused_computation.3 | convolution fusion | flops 473563136 | bytes 4718596 | tf_op jit(solution)/shard_map/dot_general | solution.py:218
  50.2 3.8 %shard_map.114 = (bf16[3,128,128]{2,1,0:T(8,128)(2,1)}, bf16[3,128,128]{2,1,0:T(8,128)(2,1)}, bf16[3,128,128]{2,1,0:T(8,128)(2,1)}, bf16[3,128,128]{2,1,0:T(8,128)(2,1)}) custom-call(s32[1]{0:T(128)} %bitcast.refs_0_, bf16[128,512]{1,0:T(8,128)(2,1)} %fusion.refs_1_, bf16[1,128,2048]{2,1,0:T(8,128)(2,1)} %refs_2_.5, bf16[1,128,2048]{2,1,0:T(8,128)(2,1)} %refs_3_.5, ...), custom_call_target="tpu_custom_call" | custom-call | flops 335544320 | bytes 786432 | tf_op jit(solution)/shard_map/pallas_call | solution.py:119
  54.0 4.0 %collective-permute-start.24 = (bf16[3,128,128]{2,1,0:T(8,128)(2,1)}, bf16[3,128,128]{2,1,0:T(8,128)(2,1)S(1)}, u32[]{:S(2)}, u32[]{:S(2)}) collective-permute-start(bf16[3,128,128]{2,1,0:T(8,128)(2,1)} %get-tuple-element.31), channel_id=1, source_target_pairs={{0,3},{1,0},{2,1},{3,2},{4,7},{5,4},{6,5},{7,6},{8,11},{9,8},{10,9... | collective-permute-start | bytes 294920 | tf_op jit(solution)/shard_map/ppermute | solution.py:230
  58.6 3.8 %shard_map.113 = (bf16[3,128,128]{2,1,0:T(8,128)(2,1)}, bf16[3,128,128]{2,1,0:T(8,128)(2,1)}, bf16[3,128,128]{2,1,0:T(8,128)(2,1)}, bf16[3,128,128]{2,1,0:T(8,128)(2,1)}) custom-call(s32[1]{0:T(128)} %bitcast.refs_0_, bf16[128,512]{1,0:T(8,128)(2,1)} %fusion.refs_1_, bf16[1,128,2048]{2,1,0:T(8,128)(2,1)} %refs_2_.5, bf16[1,128,2048]{2,1,0:T(8,128)(2,1)} %refs_3_.5, ...), custom_call_target="tpu_custom_call" | custom-call | flops 335544320 | bytes 786432 | tf_op jit(solution)/shard_map/pallas_call | solution.py:119
  62.4 1.2 %collective-permute-done.10.refs_6_ = bf16[3,128,256]{2,1,0:T(8,128)(2,1)S(1)} collective-permute-done((bf16[3,128,256]{2,1,0:T(8,128)(2,1)S(1)}, bf16[3,128,256]{2,1,0:T(8,128)(2,1)S(1)}, u32[]{:S(2)}, u32[]{:S(2)}) %collective-permute-start.10) | collective-permute-done | bytes 196640 | tf_op jit(solution)/shard_map/ppermute | solution.py:199
  63.6 3.8 %collective-permute-start.18 = (bf16[3,128,128]{2,1,0:T(8,128)(2,1)}, bf16[3,128,128]{2,1,0:T(8,128)(2,1)S(1)}, u32[]{:S(2)}, u32[]{:S(2)}) collective-permute-start(bf16[3,128,128]{2,1,0:T(8,128)(2,1)} %get-tuple-element.27), channel_id=1, source_target_pairs={{0,3},{1,0},{2,1},{3,2},{4,7},{5,4},{6,5},{7,6},{8,11},{9,8},{10,9... | collective-permute-start | bytes 294920 | tf_op jit(solution)/shard_map/ppermute | solution.py:230
  68.1 5.9 %shard_map.112 = (bf16[3,128,256]{2,1,0:T(8,128)(2,1)}, bf16[3,128,256]{2,1,0:T(8,128)(2,1)}, bf16[3,128,256]{2,1,0:T(8,128)(2,1)}, bf16[3,128,256]{2,1,0:T(8,128)(2,1)}) custom-call(s32[1]{0:T(128)} %bitcast.refs_0_, bf16[128,512]{1,0:T(8,128)(2,1)} %fusion.refs_1_, bf16[1,128,2048]{2,1,0:T(8,128)(2,1)} %refs_2_.5, bf16[1,128,2048]{2,1,0:T(8,128)(2,1)} %refs_3_.5, ...), custom_call_target="tpu_custom_call" | custom-call | flops 671088640 | bytes 1572864 | tf_op jit(solution)/shard_map/pallas_call | solution.py:119
  74.0 2.5 %collective-permute-start.12 = (bf16[3,128,256]{2,1,0:T(8,128)(2,1)}, bf16[3,128,256]{2,1,0:T(8,128)(2,1)S(1)}, u32[]{:S(2)}, u32[]{:S(2)}) collective-permute-start(bf16[3,128,256]{2,1,0:T(8,128)(2,1)} %get-tuple-element.23), channel_id=1, source_target_pairs={{0,3},{1,0},{2,1},{3,2},{4,7},{5,4},{6,5},{7,6},{8,11},{9,8},{10,9... | collective-permute-start | bytes 589832 | tf_op jit(solution)/shard_map/ppermute | solution.py:230
  76.5 1.7 %collective-permute-start.13 = (bf16[3,128,256]{2,1,0:T(8,128)(2,1)}, bf16[3,128,256]{2,1,0:T(8,128)(2,1)S(1)}, u32[]{:S(2)}, u32[]{:S(2)}) collective-permute-start(bf16[3,128,256]{2,1,0:T(8,128)(2,1)} %get-tuple-element.24), channel_id=1, source_target_pairs={{0,2},{1,3},{2,0},{3,1},{4,6},{5,7},{6,4},{7,5},{8,10},{9,11},{10,... | collective-permute-start | bytes 589832 | tf_op jit(solution)/shard_map/ppermute | solution.py:230
  78.1 1.4 %collective-permute-start.14 = (bf16[3,128,256]{2,1,0:T(8,128)(2,1)}, bf16[3,128,256]{2,1,0:T(8,128)(2,1)S(1)}, u32[]{:S(2)}, u32[]{:S(2)}) collective-permute-start(bf16[3,128,256]{2,1,0:T(8,128)(2,1)} %get-tuple-element.25), channel_id=1, source_target_pairs={{0,1},{1,2},{2,3},{3,0},{4,5},{5,6},{6,7},{7,4},{8,9},{9,10},{10,1... | collective-permute-start | bytes 589832 | tf_op jit(solution)/shard_map/ppermute | solution.py:230
  79.8 2.9 %collective-permute-start.20 = (bf16[3,128,128]{2,1,0:T(8,128)(2,1)S(1)}, bf16[3,128,128]{2,1,0:T(8,128)(2,1)S(1)}, u32[]{:S(2)}, u32[]{:S(2)}) collective-permute-start(bf16[3,128,128]{2,1,0:T(8,128)(2,1)S(1)} %copy-done.22), channel_id=1, source_target_pairs={{0,1},{1,2},{2,3},{3,0},{4,5},{5,6},{6,7},{7,4},{8,9},{9,10},{10,1... | collective-permute-start | bytes 294920 | tf_op jit(solution)/shard_map/ppermute | solution.py:230
  82.7 1.9 %shard_map.115 = (bf16[1,128,2048]{2,1,0:T(8,128)(2,1)}, bf16[1,128,2048]{2,1,0:T(8,128)(2,1)}, bf16[1,128,2048]{2,1,0:T(8,128)(2,1)}) custom-call(s32[1]{0:T(128)} %bitcast.refs_0_, bf16[3,128,128]{2,1,0:T(8,128)(2,1)} %get-tuple-element.30.refs_1_, bf16[3,128,128]{2,1,0:T(8,128)(2,1)} %copy-done.15, bf16[3,128,128]{2,1,0:T(8,128)(2,1)} %copy-done.16, ...), custom_call_target="tpu_custom_call" | custom-call | bytes 786432 | tf_op jit(solution)/shard_map/pallas_call | solution.py:166
  84.5 15.5 %collective-permute-done.19.refs_3_ = bf16[3,128,128]{2,1,0:T(8,128)(2,1)S(1)} collective-permute-done((bf16[3,128,128]{2,1,0:T(8,128)(2,1)S(1)}, bf16[3,128,128]{2,1,0:T(8,128)(2,1)S(1)}, u32[]{:S(2)}, u32[]{:S(2)}) %collective-permute-start.19) | collective-permute-done | bytes 98336 | tf_op jit(solution)/shard_map/ppermute | solution.py:230
  100.7 1.9 %shard_map.116 = (bf16[1,128,2048]{2,1,0:T(8,128)(2,1)}, bf16[1,128,2048]{2,1,0:T(8,128)(2,1)}, bf16[1,128,2048]{2,1,0:T(8,128)(2,1)}) custom-call(s32[1]{0:T(128)} %bitcast.refs_0_, bf16[3,128,128]{2,1,0:T(8,128)(2,1)} %get-tuple-element.26.refs_1_, bf16[3,128,128]{2,1,0:T(8,128)(2,1)} %copy-done.10, ...), custom_call_target="tpu_custom_call", output_to_operand_aliasing={{0}: (5, {}), {1}: (6, {}), {2}: (7, {})} | custom-call | bytes 786432 | tf_op jit(solution)/shard_map/pallas_call | solution.py:166
  103.5 2.2 %shard_map.117 = (bf16[1,128,2048]{2,1,0:T(8,128)(2,1)}, bf16[1,128,2048]{2,1,0:T(8,128)(2,1)}, bf16[1,128,2048]{2,1,0:T(8,128)(2,1)}) custom-call(s32[1]{0:T(128)} %bitcast.refs_0_, bf16[3,128,256]{2,1,0:T(8,128)(2,1)} %get-tuple-element.22.refs_1_, bf16[3,128,256]{2,1,0:T(8,128)(2,1)} %copy-done.5, ...), custom_call_target="tpu_custom_call", output_to_operand_aliasing={{0}: (5, {}), {1}: (6, {}), {2}: (7, {})} | custom-call | bytes 1572864 | tf_op jit(solution)/shard_map/pallas_call | solution.py:166
  (102 shorter events, 9.8 us)
Async XLA Ops:
  2.4 7.4 %copy-start.3 = (bf16[1,128,2048]{2,1,0:T(8,128)(2,1)S(1)}, bf16[1,128,2048]{2,1,0:T(8,128)(2,1)}, u32[]{:S(2)}) copy-start(bf16[1,128,2048]{2,1,0:T(8,128)(2,1)} %refs_3_.5) | copy-start | bytes 1572868
  3.7 11.1 %collective-permute-start.1 = (bf16[32,3584]{1,0:T(8,128)(2,1)S(1)}, bf16[32,3584]{1,0:T(8,128)(2,1)S(1)}, u32[]{:S(2)}, u32[]{:S(2)}) collective-permute-start(bf16[32,3584]{1,0:T(8,128)(2,1)S(1)} %fusion.13), channel_id=1, source_target_pairs={{1,0},{2,1},{3,2},{5,4},{6,5},{7,6},{9,8},{10,9},{11,10},{13,12},{... | collective-permute-start | bytes 688136 | tf_op jit(solution)/shard_map/ppermute | solution.py:47
  5.0 11.1 %collective-permute-start = (bf16[32,3584]{1,0:T(8,128)(2,1)S(1)}, bf16[32,3584]{1,0:T(8,128)(2,1)S(1)}, u32[]{:S(2)}, u32[]{:S(2)}) collective-permute-start(bf16[32,3584]{1,0:T(8,128)(2,1)S(1)} %fusion.13), channel_id=1, source_target_pairs={{0,1},{1,2},{2,3},{4,5},{5,6},{6,7},{8,9},{9,10},{10,11},{12,13},{... | collective-permute-start | bytes 688136 | tf_op jit(solution)/shard_map/ppermute | solution.py:46
  9.6 7.2 %collective-permute-start.6 = (f32[]{:T(128)}, f32[]{:T(128)}, u32[]{:S(2)}, u32[]{:S(2)}) collective-permute-start(f32[]{:T(128)} %bitcast.4), channel_id=1, source_target_pairs={{0,4},{4,0},{8,12},{12,8},{16,20},{20,16},{24,28},{28,24},{1,5},{5... | collective-permute-start | bytes 20 | tf_op jit(solution)/shard_map/ppermute | solution.py:35
  10.6 30.3 %collective-permute-start.21 = (bf16[3,128,128]{2,1,0:T(8,128)(2,1)}, bf16[3,128,128]{2,1,0:T(8,128)(2,1)}, u32[]{:S(2)}, u32[]{:S(2)}) collective-permute-start(bf16[3,128,128]{2,1,0:T(8,128)(2,1)} %pad_maximum_fusion.6), channel_id=1, source_target_pairs={{0,1},{1,2},{2,3},{3,0},{4,5},{5,6},{6,7},{7,4},{8,9},{9,10},{10,1... | collective-permute-start | bytes 294920 | tf_op jit(solution)/shard_map/ppermute | solution.py:199
  12.8 30.0 %collective-permute-start.22 = (bf16[3,128,128]{2,1,0:T(8,128)(2,1)}, bf16[3,128,128]{2,1,0:T(8,128)(2,1)}, u32[]{:S(2)}, u32[]{:S(2)}) collective-permute-start(bf16[3,128,128]{2,1,0:T(8,128)(2,1)} %pad_maximum_fusion.7), channel_id=1, source_target_pairs={{0,2},{1,3},{2,0},{3,1},{4,6},{5,7},{6,4},{7,5},{8,10},{9,11},{10,... | collective-permute-start | bytes 294920 | tf_op jit(solution)/shard_map/ppermute | solution.py:199
  14.8 15.4 %collective-permute-start.2 = (bf16[32,3584]{1,0:T(8,128)(2,1)S(1)}, bf16[32,3584]{1,0:T(8,128)(2,1)S(1)}, u32[]{:S(2)}, u32[]{:S(2)}) collective-permute-start(bf16[32,3584]{1,0:T(8,128)(2,1)S(1)} %collective-permute-done.1), channel_id=1, source_target_pairs={{1,0},{2,1},{5,4},{6,5},{9,8},{10,9},{13,12},{14,13},{17,16},{18,1... | collective-permute-start | bytes 688136 | tf_op jit(solution)/shard_map/ppermute | solution.py:47
  16.1 15.6 %collective-permute-start.4 = (bf16[32,3584]{1,0:T(8,128)(2,1)S(1)}, bf16[32,3584]{1,0:T(8,128)(2,1)S(1)}, u32[]{:S(2)}, u32[]{:S(2)}) collective-permute-start(bf16[32,3584]{1,0:T(8,128)(2,1)S(1)} %collective-permute-done), channel_id=1, source_target_pairs={{1,2},{2,3},{5,6},{6,7},{9,10},{10,11},{13,14},{14,15},{17,18},{18... | collective-permute-start | bytes 688136 | tf_op jit(solution)/shard_map/ppermute | solution.py:46
  17.4 3.6 %collective-permute-start.7 = (f32[]{:T(128)}, f32[]{:T(128)}, u32[]{:S(2)}, u32[]{:S(2)}) collective-permute-start(f32[]{:T(128)} %add.69), channel_id=1, source_target_pairs={{0,8},{4,12},{8,0},{12,4},{16,24},{20,28},{24,16},{28,20},{1,9},{5... | collective-permute-start | bytes 20 | tf_op jit(solution)/shard_map/ppermute | solution.py:35
  21.7 3.6 %collective-permute-start.8 = (f32[]{:T(128)}, f32[]{:T(128)}, u32[]{:S(2)}, u32[]{:S(2)}) collective-permute-start(f32[]{:T(128)} %add.70), channel_id=1, source_target_pairs={{0,16},{4,20},{8,24},{12,28},{16,0},{20,4},{24,8},{28,12},{1,17},{... | collective-permute-start | bytes 20 | tf_op jit(solution)/shard_map/ppermute | solution.py:35
  25.2 19.6 %collective-permute-start.23 = (bf16[3,128,128]{2,1,0:T(8,128)(2,1)S(1)}, bf16[3,128,128]{2,1,0:T(8,128)(2,1)S(1)}, u32[]{:S(2)}, u32[]{:S(2)}) collective-permute-start(bf16[3,128,128]{2,1,0:T(8,128)(2,1)S(1)} %pad_maximum_fusion.8), channel_id=1, source_target_pairs={{0,3},{1,0},{2,1},{3,2},{4,7},{5,4},{6,5},{7,6},{8,11},{9,8},{10,9... | collective-permute-start | bytes 294920 | tf_op jit(solution)/shard_map/ppermute | solution.py:199
  30.2 15.6 %collective-permute-start.15 = (bf16[3,128,128]{2,1,0:T(8,128)(2,1)S(1)}, bf16[3,128,128]{2,1,0:T(8,128)(2,1)S(1)}, u32[]{:S(2)}, u32[]{:S(2)}) collective-permute-start(bf16[3,128,128]{2,1,0:T(8,128)(2,1)S(1)} %pad_maximum_fusion.3), channel_id=1, source_target_pairs={{0,1},{1,2},{2,3},{3,0},{4,5},{5,6},{6,7},{7,4},{8,9},{9,10},{10,1... | collective-permute-start | bytes 294920 | tf_op jit(solution)/shard_map/ppermute | solution.py:199
  31.7 7.9 %collective-permute-start.3 = (bf16[32,3584]{1,0:T(8,128)(2,1)S(1)}, bf16[32,3584]{1,0:T(8,128)(2,1)S(1)}, u32[]{:S(2)}, u32[]{:S(2)}) collective-permute-start(bf16[32,3584]{1,0:T(8,128)(2,1)S(1)} %collective-permute-done.2), channel_id=1, source_target_pairs={{1,0},{5,4},{9,8},{13,12},{17,16},{21,20},{25,24},{29,28}} | collective-permute-start | bytes 688136 | tf_op jit(solution)/shard_map/ppermute | solution.py:47
  39.6 0.7 collective-permute-start.5
  40.3 13.7 %collective-permute-start.16 = (bf16[3,128,128]{2,1,0:T(8,128)(2,1)S(1)}, bf16[3,128,128]{2,1,0:T(8,128)(2,1)S(1)}, u32[]{:S(2)}, u32[]{:S(2)}) collective-permute-start(bf16[3,128,128]{2,1,0:T(8,128)(2,1)S(1)} %pad_maximum_fusion.4), channel_id=1, source_target_pairs={{0,2},{1,3},{2,0},{3,1},{4,6},{5,7},{6,4},{7,5},{8,10},{9,11},{10,... | collective-permute-start | bytes 294920 | tf_op jit(solution)/shard_map/ppermute | solution.py:199
  40.8 17.1 %collective-permute-start.17 = (bf16[3,128,128]{2,1,0:T(8,128)(2,1)S(1)}, bf16[3,128,128]{2,1,0:T(8,128)(2,1)S(1)}, u32[]{:S(2)}, u32[]{:S(2)}) collective-permute-start(bf16[3,128,128]{2,1,0:T(8,128)(2,1)S(1)} %pad_maximum_fusion.5), channel_id=1, source_target_pairs={{0,3},{1,0},{2,1},{3,2},{4,7},{5,4},{6,5},{7,6},{8,11},{9,8},{10,9... | collective-permute-start | bytes 294920 | tf_op jit(solution)/shard_map/ppermute | solution.py:199
  42.8 20.8 %collective-permute-start.10 = (bf16[3,128,256]{2,1,0:T(8,128)(2,1)S(1)}, bf16[3,128,256]{2,1,0:T(8,128)(2,1)S(1)}, u32[]{:S(2)}, u32[]{:S(2)}) collective-permute-start(bf16[3,128,256]{2,1,0:T(8,128)(2,1)S(1)} %pad_maximum_fusion.1), channel_id=1, source_target_pairs={{0,2},{1,3},{2,0},{3,1},{4,6},{5,7},{6,4},{7,5},{8,10},{9,11},{10,... | collective-permute-start | bytes 589832 | tf_op jit(solution)/shard_map/ppermute | solution.py:199
  44.8 18.7 %collective-permute-start.11 = (bf16[3,128,256]{2,1,0:T(8,128)(2,1)S(1)}, bf16[3,128,256]{2,1,0:T(8,128)(2,1)S(1)}, u32[]{:S(2)}, u32[]{:S(2)}) collective-permute-start(bf16[3,128,256]{2,1,0:T(8,128)(2,1)S(1)} %pad_maximum_fusion.2), channel_id=1, source_target_pairs={{0,3},{1,0},{2,1},{3,2},{4,7},{5,4},{6,5},{7,6},{8,11},{9,8},{10,9... | collective-permute-start | bytes 589832 | tf_op jit(solution)/shard_map/ppermute | solution.py:199
  45.8 21.6 %collective-permute-start.9 = (bf16[3,128,256]{2,1,0:T(8,128)(2,1)S(1)}, bf16[3,128,256]{2,1,0:T(8,128)(2,1)S(1)}, u32[]{:S(2)}, u32[]{:S(2)}) collective-permute-start(bf16[3,128,256]{2,1,0:T(8,128)(2,1)S(1)} %pad_maximum_fusion), channel_id=1, source_target_pairs={{0,1},{1,2},{2,3},{3,0},{4,5},{5,6},{6,7},{7,4},{8,9},{9,10},{10,1... | collective-permute-start | bytes 589832 | tf_op jit(solution)/shard_map/ppermute | solution.py:199
  54.0 9.6 %copy-start.24 = (bf16[3,128,128]{2,1,0:T(8,128)(2,1)S(1)}, bf16[3,128,128]{2,1,0:T(8,128)(2,1)}, u32[]{:S(2)}) copy-start(bf16[3,128,128]{2,1,0:T(8,128)(2,1)} %get-tuple-element.33) | copy-start | bytes 294916
  54.0 22.4 %collective-permute-start.24 = (bf16[3,128,128]{2,1,0:T(8,128)(2,1)}, bf16[3,128,128]{2,1,0:T(8,128)(2,1)S(1)}, u32[]{:S(2)}, u32[]{:S(2)}) collective-permute-start(bf16[3,128,128]{2,1,0:T(8,128)(2,1)} %get-tuple-element.31), channel_id=1, source_target_pairs={{0,3},{1,0},{2,1},{3,2},{4,7},{5,4},{6,5},{7,6},{8,11},{9,8},{10,9... | collective-permute-start | bytes 294920 | tf_op jit(solution)/shard_map/ppermute | solution.py:230
  58.0 20.2 %collective-permute-start.25 = (bf16[3,128,128]{2,1,0:T(8,128)(2,1)}, bf16[3,128,128]{2,1,0:T(8,128)(2,1)S(1)}, u32[]{:S(2)}, u32[]{:S(2)}) collective-permute-start(bf16[3,128,128]{2,1,0:T(8,128)(2,1)} %get-tuple-element.32), channel_id=1, source_target_pairs={{0,2},{1,3},{2,0},{3,1},{4,6},{5,7},{6,4},{7,5},{8,10},{9,11},{10,... | collective-permute-start | bytes 294920 | tf_op jit(solution)/shard_map/ppermute | solution.py:230
  62.4 17.1 %copy-start.23 = (bf16[3,128,128]{2,1,0:T(8,128)(2,1)S(1)}, bf16[3,128,128]{2,1,0:T(8,128)(2,1)}, u32[]{:S(2)}) copy-start(bf16[3,128,128]{2,1,0:T(8,128)(2,1)} %get-tuple-element.28) | copy-start | bytes 294916
  62.4 17.4 %copy-start.22 = (bf16[3,128,128]{2,1,0:T(8,128)(2,1)S(1)}, bf16[3,128,128]{2,1,0:T(8,128)(2,1)}, u32[]{:S(2)}) copy-start(bf16[3,128,128]{2,1,0:T(8,128)(2,1)} %get-tuple-element.29) | copy-start | bytes 294916
  63.6 15.9 %collective-permute-start.26 = (bf16[3,128,128]{2,1,0:T(8,128)(2,1)S(1)}, bf16[3,128,128]{2,1,0:T(8,128)(2,1)S(1)}, u32[]{:S(2)}, u32[]{:S(2)}) collective-permute-start(bf16[3,128,128]{2,1,0:T(8,128)(2,1)S(1)} %copy-done.24), channel_id=1, source_target_pairs={{0,1},{1,2},{2,3},{3,0},{4,5},{5,6},{6,7},{7,4},{8,9},{9,10},{10,1... | collective-permute-start | bytes 294920 | tf_op jit(solution)/shard_map/ppermute | solution.py:230
  63.6 16.2 %collective-permute-start.18 = (bf16[3,128,128]{2,1,0:T(8,128)(2,1)}, bf16[3,128,128]{2,1,0:T(8,128)(2,1)S(1)}, u32[]{:S(2)}, u32[]{:S(2)}) collective-permute-start(bf16[3,128,128]{2,1,0:T(8,128)(2,1)} %get-tuple-element.27), channel_id=1, source_target_pairs={{0,3},{1,0},{2,1},{3,2},{4,7},{5,4},{6,5},{7,6},{8,11},{9,8},{10,9... | collective-permute-start | bytes 294920 | tf_op jit(solution)/shard_map/ppermute | solution.py:230
  74.0 28.6 %collective-permute-start.12 = (bf16[3,128,256]{2,1,0:T(8,128)(2,1)}, bf16[3,128,256]{2,1,0:T(8,128)(2,1)S(1)}, u32[]{:S(2)}, u32[]{:S(2)}) collective-permute-start(bf16[3,128,256]{2,1,0:T(8,128)(2,1)} %get-tuple-element.23), channel_id=1, source_target_pairs={{0,3},{1,0},{2,1},{3,2},{4,7},{5,4},{6,5},{7,6},{8,11},{9,8},{10,9... | collective-permute-start | bytes 589832 | tf_op jit(solution)/shard_map/ppermute | solution.py:230
  76.5 26.2 %collective-permute-start.13 = (bf16[3,128,256]{2,1,0:T(8,128)(2,1)}, bf16[3,128,256]{2,1,0:T(8,128)(2,1)S(1)}, u32[]{:S(2)}, u32[]{:S(2)}) collective-permute-start(bf16[3,128,256]{2,1,0:T(8,128)(2,1)} %get-tuple-element.24), channel_id=1, source_target_pairs={{0,2},{1,3},{2,0},{3,1},{4,6},{5,7},{6,4},{7,5},{8,10},{9,11},{10,... | collective-permute-start | bytes 589832 | tf_op jit(solution)/shard_map/ppermute | solution.py:230
  78.1 24.5 %collective-permute-start.14 = (bf16[3,128,256]{2,1,0:T(8,128)(2,1)}, bf16[3,128,256]{2,1,0:T(8,128)(2,1)S(1)}, u32[]{:S(2)}, u32[]{:S(2)}) collective-permute-start(bf16[3,128,256]{2,1,0:T(8,128)(2,1)} %get-tuple-element.25), channel_id=1, source_target_pairs={{0,1},{1,2},{2,3},{3,0},{4,5},{5,6},{6,7},{7,4},{8,9},{9,10},{10,1... | collective-permute-start | bytes 589832 | tf_op jit(solution)/shard_map/ppermute | solution.py:230
  79.5 20.5 %collective-permute-start.19 = (bf16[3,128,128]{2,1,0:T(8,128)(2,1)S(1)}, bf16[3,128,128]{2,1,0:T(8,128)(2,1)S(1)}, u32[]{:S(2)}, u32[]{:S(2)}) collective-permute-start(bf16[3,128,128]{2,1,0:T(8,128)(2,1)S(1)} %copy-done.23), channel_id=1, source_target_pairs={{0,2},{1,3},{2,0},{3,1},{4,6},{5,7},{6,4},{7,5},{8,10},{9,11},{10,... | collective-permute-start | bytes 294920 | tf_op jit(solution)/shard_map/ppermute | solution.py:230
  79.8 20.3 %copy-start.10 = (bf16[3,128,128]{2,1,0:T(8,128)(2,1)}, bf16[3,128,128]{2,1,0:T(8,128)(2,1)S(1)}, u32[]{:S(2)}) copy-start(bf16[3,128,128]{2,1,0:T(8,128)(2,1)S(1)} %collective-permute-done.18.refs_2_) | copy-start | bytes 294916
  79.8 20.3 %collective-permute-start.20 = (bf16[3,128,128]{2,1,0:T(8,128)(2,1)S(1)}, bf16[3,128,128]{2,1,0:T(8,128)(2,1)S(1)}, u32[]{:S(2)}, u32[]{:S(2)}) collective-permute-start(bf16[3,128,128]{2,1,0:T(8,128)(2,1)S(1)} %copy-done.22), channel_id=1, source_target_pairs={{0,1},{1,2},{2,3},{3,0},{4,5},{5,6},{6,7},{7,4},{8,9},{9,10},{10,1... | collective-permute-start | bytes 294920 | tf_op jit(solution)/shard_map/ppermute | solution.py:230
  (20 other events, 59.1 us)

commit v2 on v1

--- a/solution.py
+++ b/solution.py
@@ -10,46 +10,101 @@
 
 HD = 128
 GW = 64
-
-
-def norm_backward(hidden, cotangent, gain):
-    hidden_f = hidden.astype(jnp.float32)
-    scaled_cot = cotangent.astype(jnp.float32) * gain
-    inv_rms = lax.rsqrt(jnp.mean(hidden_f * hidden_f, axis=-1, keepdims=True) + 1e-06)
-    mixed = jnp.mean(hidden_f * scaled_cot, axis=-1, keepdims=True)
-    return (inv_rms * scaled_cot - hidden_f * inv_rms * inv_rms * inv_rms * mixed).astype(
+IN_HEADS = (2, 2)
+OUT_HEADS = (2, 1, 1)
+
+
+def visual_kernel(here_ref, pos_ref, hidden_ref, cot_ref, gain_ref, out_ref):
+    rows = hidden_ref.shape[1]
+    picked = out_ref.shape[0]
+    row = lax.broadcasted_iota(jnp.int32, (rows, picked), 0) + here_ref[0] * rows
+    pick = jnp.where(row == pos_ref[...], 1.0, 0.0).astype(jnp.bfloat16)
+    first_both = (((0,), (0,)), ((), ()))
+    hidden = lax.dot_general(pick, hidden_ref[0], first_both, preferred_element_type=jnp.float32)
+    cot = lax.dot_general(pick, cot_ref[0], first_both, preferred_element_type=jnp.float32)
+    scaled_cot = cot * gain_ref[...]
+    inv_rms = lax.rsqrt(jnp.mean(hidden * hidden, axis=-1, keepdims=True) + 1e-06)
+    mixed = jnp.mean(hidden * scaled_cot, axis=-1, keepdims=True)
+    out_ref[...] = (inv_rms * scaled_cot - hidden * (inv_rms * inv_rms * inv_rms * mixed)).astype(
         jnp.bfloat16
     )
 
 
-def head_groups(heads):
-    return (1, 1, heads - 2) if heads > 2 else (heads,)
+def visual_grads(here, positions, hidden, cotangent, gain):
+    picked, depth = positions.shape[1], hidden.shape[2]
+    vmem = pl.BlockSpec(memory_space=pltpu.VMEM)
+    return pl.pallas_call(
+        visual_kernel,
+        in_specs=[pl.BlockSpec(memory_space=pltpu.SMEM)] + [vmem] * 4,
+        out_specs=vmem,
+        out_shape=jax.ShapeDtypeStruct((picked, depth), jnp.bfloat16),
+        cost_estimate=pl.CostEstimate(
+            flops=4 * picked * hidden.size, bytes_accessed=4 * hidden.size, transcendentals=0
+        ),
+        name="visual",
+    )(here, positions, hidden, cotangent, gain[None])
+
+
+def pack_kernel(count, first, here_ref, *refs):
+    sources, outs, sems = refs[:3], refs[3:-1], refs[-1]
+    width = outs[0].shape[2]
+    own_width = sources[0].shape[2] // count
+    copies = []
+    for k, out in enumerate(outs, 1):
+        column = pl.multiple_of((here_ref[0] ^ k) * own_width + first, HD)
+        for i, source in enumerate(sources):
+            copies.append(
+                pltpu.make_async_copy(
+                    source.at[0, :, pl.ds(column, width)], out.at[i], sems.at[3 * k - 3 + i]
+                )
+            )
+    for copy in copies:
+        copy.start()
+    for copy in copies:
+        copy.wait()
+
+
+def pack(here, sources, first, width, count):
+    rows = sources[0].shape[1]
+    return pl.pallas_call(
+        functools.partial(pack_kernel, count, first),
+        in_specs=[pl.BlockSpec(memory_space=pltpu.SMEM)]
+        + [pl.BlockSpec(memory_space=pl.ANY)] * 3,
+        out_specs=[pl.BlockSpec(memory_space=pltpu.VMEM)] * (count - 1),
+        out_shape=[jax.ShapeDtypeStruct((3, rows, width), jnp.bfloat16)] * (count - 1),
+        scratch_shapes=[pltpu.SemaphoreType.DMA((3 * count - 3,))],
+        cost_estimate=pl.CostEstimate(
+            flops=0, bytes_accessed=12 * count * rows * width, transcendentals=0
+        ),
+    )(here, *sources)
+
+
+def split(heads, parts):
+    return parts if sum(parts) == heads else (heads,)
+
+
+def partners(size, k):
+    return [(i, i ^ k) for i in range(size)]
 
 
 def total_over(value, axis):
     size = lax.axis_size(axis)
-    if size & (size - 1):
-        return lax.psum(value, axis)
     step = 1
     while step < size:
-        value = value + lax.ppermute(value, axis, [(i, i ^ step) for i in range(size)])
+        value = value + lax.ppermute(value, axis, partners(size, step))
         step *= 2
     return value
 
 
-def relayed_blocks(block, axis):
+def gathered(block, axis):
     size = lax.axis_size(axis)
-    here = lax.axis_index(axis)
-    upward, downward = [], []
-    up = down = block
-    for step in range(size - 1):
-        up = lax.ppermute(up, axis, [(i, i + 1) for i in range(step, size - 1)])
-        down = lax.ppermute(down, axis, [(i + 1, i) for i in range(size - 1 - step)])
-        upward.append(up)
-        downward.append(down)
-    return [block] + [
-        jnp.where(here >= k, upward[k - 1], downward[size - k - 1]) for k in range(1, size)
-    ]
+    held = {0: block}
+    step = size // 2
+    while step:
+        for k in sorted(held):
+            held[k ^ step] = lax.ppermute(held[k], axis, partners(size, step))
+        step //= 2
+    return [held[k] for k in range(size)]
 
 
 def attend_kernel(count, scale, chunk, *refs):
@@ -108,13 +163,14 @@
         out[2] = dv_s[at].astype(jnp.bfloat16)
 
 
-def attend(here, handed, own, blocks, first, heads, count):
+def attend(here, handed, own, blocks, first, skip, heads, count):
     rows = own[0].shape[1]
     local_heads = handed.shape[1] // HD
     length = rows * count
     chunk = min(256, length)
     own_spec = pl.BlockSpec((1, rows, HD), lambda h, t: (0, 0, t[0] * local_heads + first + h))
-    block_spec = pl.BlockSpec((3, rows, HD), lambda h, t: (0, 0, h))
+    out_spec = pl.BlockSpec((3, rows, HD), lambda h, t: (0, 0, h))
+    block_spec = pl.BlockSpec((3, rows, HD), lambda h, t: (0, 0, skip + h))
     flops = 10 * heads * length * length * HD
     return pl.pallas_call(
         functools.partial(attend_kernel, count, HD**-0.5, chunk),
@@ -124,7 +180,7 @@
             in_specs=[pl.BlockSpec((handed.shape[0], HD), lambda h, t: (0, first + h))]
             + [own_spec] * 3
             + [block_spec] * (count - 1),
-            out_specs=[block_spec] * count,
+            out_specs=[out_spec] * count,
             scratch_shapes=[pltpu.VMEM((length, HD), jnp.bfloat16)] * 5
             + [pltpu.VMEM((length, HD), jnp.float32)] * 2,
         ),
@@ -146,7 +202,7 @@
     own_width = outs[0].shape[2] // count
     copies = []
     for k, part in enumerate(parts):
-        column = pl.multiple_of(lax.rem(here + k, count) * own_width + first, HD)
+        column = pl.multiple_of((here ^ k) * own_width + first, HD)
         for i, out in enumerate(outs):
             copies.append(
                 pltpu.make_async_copy(
@@ -185,35 +241,22 @@
     here = lax.axis_index("tensor")
     place_of = here[None].astype(jnp.int32)
     own_width = img_query.shape[2] // count
-    groups = head_groups(own_width // HD)
-    starts = [sum(groups[:g]) for g in range(len(groups))]
-
-    def columns(array, k, g):
-        first = lax.rem(here + k, count) * own_width + starts[g] * HD
-        return lax.dynamic_slice_in_dim(array[0], first, groups[g] * HD, 1)
+    own = (img_query, img_key, img_value)
+    visual_grad = visual_grads(place_of, visual_pos, rm_hidden, rm_cotangent, rm_gain)
+    visual_blocks = gathered(visual_grad, "tensor")
 
     arrived = []
-    for g in range(len(groups)):
-        arrived.append(
-            [
-                lax.ppermute(
-                    jnp.stack([columns(a, k, g) for a in (img_query, img_key, img_value)]),
-                    "tensor",
-                    [(i, (i + k) % count) for i in range(count)],
-                )
-                for k in range(1, count)
-            ]
-        )
+    for heads in split(own_width // HD, IN_HEADS):
+        packed = pack(place_of, own, len(arrived) * HD, heads * HD, count)
+        blocks = [
+            lax.ppermute(packed[k - 1], "tensor", partners(count, k))
+            for k in range(1, count)
+        ]
+        arrived += [(blocks, skip) for skip in range(heads)]
 
     reward_sum = total_over(jnp.sum(rewards), "dp")
     sample_count = lax.axis_size("dp") * rewards.shape[0]
     reward_weight = rewards[0] * sample_count / reward_sum
-    row_offset = here * rm_hidden.shape[1]
-    local_rows = visual_pos[0] - row_offset
-    vis_hidden = jnp.take(rm_hidden[0], local_rows, axis=0)
-    vis_cot = jnp.take(rm_cotangent[0], local_rows, axis=0)
-    visual_grad = norm_backward(vis_hidden, vis_cot, rm_gain)
-    visual_blocks = relayed_blocks(visual_grad, "tensor")
     handed = (
         jnp.dot(
             jnp.concatenate(visual_blocks, axis=0), bridge, preferred_element_type=jnp.float32
@@ -222,15 +265,15 @@
     ).astype(jnp.bfloat16)
 
     outs = ()
-    for g, heads in enumerate(groups):
-        grads = attend(
-            place_of, handed, (img_query, img_key, img_value), arrived[g], starts[g], heads, count
-        )
+    first = 0
+    for heads in split(own_width // HD, OUT_HEADS):
+        blocks, skip = arrived[first]
+        grads = attend(place_of, handed, own, blocks, first, skip, heads, count)
         parts = [grads[0]] + [
-            lax.ppermute(grads[k], "tensor", [(i, (i - k) % count) for i in range(count)])
-            for k in range(1, count)
+            lax.ppermute(grads[k], "tensor", partners(count, k)) for k in range(1, count)
         ]
-        outs = place(place_of, parts, outs, img_query.shape, starts[g] * HD)
+        outs = place(place_of, parts, outs, img_query.shape, first * HD)
+        first += heads
     return tuple(outs)
 
 

time: 108 us -> 118 us (1.093)
  waiting for transfers between devices: 25.7 us -> 44.5 us
  starting transfers between devices: 45.9 us -> 33.7 us
  Pallas kernels: 19.4 us -> 25.7 us
  other arithmetic: 2.86 us -> 0 us
    ppermute x27 -> x21, waiting for transfers between devices: 25.7 us -> 44.5 us  [the longest x6 21.1 us: work(): lax.ppermute(packed[k - 1], 'tensor', partners(count, k))]
    ppermute x27 -> x21, starting transfers between devices: 45.9 us -> 33.7 us  [the longest x9 14.7 us: work(): lax.ppermute(grads[k], 'tensor', partners(count, k))]
    pallas_call x0 -> x3, Pallas kernels: none -> 6.32 us  [the longest x2 4.02 us: pack(): pl.pallas_call(functools.partial(pack_kernel, count, first), in_specs=[pl...]
    another operation x9 -> x0, other arithmetic: 1.44 us -> none  [work(): jnp.stack([columns(a, k, g) for a in (img_query, img_key, img_value)])]
    gather x2 -> x0, local copies, waits for them, and re-layouts: 1.37 us -> none  [the longest x1 0.69 us: work(): vis_cot = jnp.take(rm_cotangent[0], local_rows, axis=0)]
    broadcast_in_dim x0 -> x1, local copies, waits for them, and re-layouts: none -> 1.33 us  [visual_grads(): gain[None]]
    unnamed x50 -> x34, local copies, waits for them, and re-layouts: 3.12 us -> 4.08 us
  transfers between devices with their start and end apart: 27 -> 21, of which waited for: 5 -> 8; matrix products, arithmetic and copies ran while one was open for 5% -> 3% of each run, Pallas kernels for 16% -> 19%
where the time goes in v2:
time: 118 us; the launch traced here: 116 us
  waiting for transfers between devices  44.5 us (38%)
  starting transfers between devices  33.7 us (29%)
  Pallas kernels  25.7 us (22%)
  local copies, waits for them, and re-layouts  5.41 us (5%)
  between operations  3.38 us (3%)
  matrix products  3.35 us (3%)
    ppermute x6, waiting for transfers between devices, work(): lax.ppermute(packed[k - 1], 'tensor', partners(count, k))  21.1 us
    ppermute x9, starting transfers between devices, work(): lax.ppermute(grads[k], 'tensor', partners(count, k))  14.7 us
    pallas_call x3, Pallas kernels, attend(): pl.pallas_call(functools.partial(attend_kernel, count, HD ** (-0.5), chun...  13.4 us
    ppermute x9, waiting for transfers between devices, work(): lax.ppermute(grads[k], 'tensor', partners(count, k))  11.4 us
    ppermute x6, starting transfers between devices, work(): lax.ppermute(packed[k - 1], 'tensor', partners(count, k))  9.39 us
    ppermute x3, waiting for transfers between devices, gathered(): held[k ^ step] = lax.ppermute(held[k], axis, partners(size, step))  9.33 us
    pallas_call x3, Pallas kernels, place(): pl.pallas_call(functools.partial(place_kernel, count, first), in_specs=[p...  5.93 us
    ppermute x3, starting transfers between devices, gathered(): held[k ^ step] = lax.ppermute(held[k], axis, partners(size, step))  4.82 us
  transfers between devices with their start and end apart: 21, of which 8 were waited for; matrix products, arithmetic and copies ran while one was open for 3% of the time, Pallas kernels for 19%

profile of v2, /device:TPU:2, one launch (start us, length us, event | category | flops | bytes accessed | tf_op | source)
XLA Modules:
  0.0 116.0 jit_solution(12523550955211337342)
XLA Ops:
  0.6 1.3 %broadcast_in_dim.7.gain_ref = f32[1,3584]{1,0:T(1,128)} reshape(f32[3584]{0:T(1024)} %param.11) | data formatting | bytes 28672 | tf_op jit(solution)/shard_map/broadcast_in_dim | solution.py:45
  2.0 2.3 %visual.1 = bf16[32,3584]{1,0:T(8,128)(2,1)} custom-call(s32[1]{0:T(128)} %bitcast.here_ref.refs_0_, s32[1,32]{1,0:T(1,128)} %pos_ref.1, bf16[1,64,3584]{2,1,0:T(8,128)(2,1)} %hidden_ref.1, bf16[1,64,3584]{2,1,0:T(8,128)(2,1)} %cot_ref.1, f32[1,3584]{1,0:T(1,128)} %broadcast_in_dim.7.gain_ref), custom_call_target="tpu_custom_call" | custom-call | flops 29360128 | bytes 917504 | tf_op jit(solution)/shard_map/visual/pallas_call | solution.py:36
  4.3 2.6 %collective-permute-start.1 = (bf16[32,3584]{1,0:T(8,128)(2,1)}, bf16[32,3584]{1,0:T(8,128)(2,1)S(1)}, u32[]{:S(2)}, u32[]{:S(2)}) collective-permute-start(bf16[32,3584]{1,0:T(8,128)(2,1)} %visual.1), channel_id=1, source_target_pairs={{0,2},{1,3},{2,0},{3,1},{4,6},{5,7},{6,4},{7,5},{8,10},{9,11},{10,... | collective-permute-start | bytes 688136 | tf_op jit(solution)/shard_map/ppermute | solution.py:105
  6.9 1.6 %collective-permute-start = (bf16[32,3584]{1,0:T(8,128)(2,1)}, bf16[32,3584]{1,0:T(8,128)(2,1)S(1)}, u32[]{:S(2)}, u32[]{:S(2)}) collective-permute-start(bf16[32,3584]{1,0:T(8,128)(2,1)} %visual.1), channel_id=1, source_target_pairs={{0,1},{1,0},{2,3},{3,2},{4,5},{5,4},{6,7},{7,6},{8,9},{9,8},{10,11... | collective-permute-start | bytes 688136 | tf_op jit(solution)/shard_map/ppermute | solution.py:105
  8.4 9.3 %collective-permute-done.1 = bf16[32,3584]{1,0:T(8,128)(2,1)S(1)} collective-permute-done((bf16[32,3584]{1,0:T(8,128)(2,1)}, bf16[32,3584]{1,0:T(8,128)(2,1)S(1)}, u32[]{:S(2)}, u32[]{:S(2)}) %collective-permute-start.1) | collective-permute-done | bytes 229408 | tf_op jit(solution)/shard_map/ppermute | solution.py:105
  18.4 2.0 %shard_map.115 = (bf16[3,128,256]{2,1,0:T(8,128)(2,1)}, bf16[3,128,256]{2,1,0:T(8,128)(2,1)}, bf16[3,128,256]{2,1,0:T(8,128)(2,1)}) custom-call(s32[1]{0:T(128)} %bitcast.here_ref.refs_0_, bf16[1,128,2048]{2,1,0:T(8,128)(2,1)} %refs_2_.9, bf16[1,128,2048]{2,1,0:T(8,128)(2,1)} %refs_3_.5, bf16[1,128,2048]{2,1,0:T(8,128)(2,1)} %refs_4_.5), custom_call_target="tpu_custom_call" | custom-call | bytes 1572864 | tf_op jit(solution)/shard_map/pallas_call | solution.py:69
  20.4 1.4 %collective-permute-start.15 = (bf16[3,128,256]{2,1,0:T(8,128)(2,1)}, bf16[3,128,256]{2,1,0:T(8,128)(2,1)S(1)}, u32[]{:S(2)}, u32[]{:S(2)}) collective-permute-start(bf16[3,128,256]{2,1,0:T(8,128)(2,1)} %get-tuple-element.38), channel_id=1, source_target_pairs={{0,1},{1,0},{2,3},{3,2},{4,5},{5,4},{6,7},{7,6},{8,9},{9,8},{10,11... | collective-permute-start | bytes 589832 | tf_op jit(solution)/shard_map/ppermute | solution.py:252
  21.9 2.0 %shard_map.112 = (bf16[3,128,256]{2,1,0:T(8,128)(2,1)}, bf16[3,128,256]{2,1,0:T(8,128)(2,1)}, bf16[3,128,256]{2,1,0:T(8,128)(2,1)}) custom-call(s32[1]{0:T(128)} %bitcast.here_ref.refs_0_, bf16[1,128,2048]{2,1,0:T(8,128)(2,1)} %refs_2_.9, bf16[1,128,2048]{2,1,0:T(8,128)(2,1)} %refs_3_.5, bf16[1,128,2048]{2,1,0:T(8,128)(2,1)} %refs_4_.5), custom_call_target="tpu_custom_call" | custom-call | bytes 1572864 | tf_op jit(solution)/shard_map/pallas_call | solution.py:69
  25.9 1.9 %collective-permute-start.4 = (f32[]{:T(128)}, f32[]{:T(128)}, u32[]{:S(2)}, u32[]{:S(2)}) collective-permute-start(f32[]{:T(128)} %add.9), channel_id=1, source_target_pairs={{0,8},{4,12},{8,0},{12,4},{16,24},{20,28},{24,16},{28,20},{1,9},{5... | collective-permute-start | bytes 20 | tf_op jit(solution)/shard_map/ppermute | solution.py:94
  27.8 1.8 %collective-permute-done.4 = f32[]{:T(128)} collective-permute-done((f32[]{:T(128)}, f32[]{:T(128)}, u32[]{:S(2)}, u32[]{:S(2)}) %collective-permute-start.4) | collective-permute-done | bytes 36 | tf_op jit(solution)/shard_map/ppermute | solution.py:94
  30.3 2.9 %collective-permute-start.5 = (f32[]{:T(128)}, f32[]{:T(128)}, u32[]{:S(2)}, u32[]{:S(2)}) collective-permute-start(f32[]{:T(128)} %add.10), channel_id=1, source_target_pairs={{0,16},{4,20},{8,24},{12,28},{16,0},{20,4},{24,8},{28,12},{1,17},{... | collective-permute-start | bytes 20 | tf_op jit(solution)/shard_map/ppermute | solution.py:94
  34.0 3.3 %collective-permute-start.7 = (bf16[3,128,256]{2,1,0:T(8,128)(2,1)}, bf16[3,128,256]{2,1,0:T(8,128)(2,1)S(1)}, u32[]{:S(2)}, u32[]{:S(2)}) collective-permute-start(bf16[3,128,256]{2,1,0:T(8,128)(2,1)} %get-tuple-element.28), channel_id=1, source_target_pairs={{0,2},{1,3},{2,0},{3,1},{4,6},{5,7},{6,4},{7,5},{8,10},{9,11},{10,... | collective-permute-start | bytes 589832 | tf_op jit(solution)/shard_map/ppermute | solution.py:252
  38.5 1.1 collective-permute-start.16
  39.6 2.3 %collective-permute-start.17 = (bf16[3,128,256]{2,1,0:T(8,128)(2,1)}, bf16[3,128,256]{2,1,0:T(8,128)(2,1)S(1)}, u32[]{:S(2)}, u32[]{:S(2)}) collective-permute-start(bf16[3,128,256]{2,1,0:T(8,128)(2,1)} %get-tuple-element.40), channel_id=1, source_target_pairs={{0,3},{1,2},{2,1},{3,0},{4,7},{5,6},{6,5},{7,4},{8,11},{9,10},{10,... | collective-permute-start | bytes 589832 | tf_op jit(solution)/shard_map/ppermute | solution.py:252
  42.0 3.4 %fusion.refs_1_ = bf16[128,512]{1,0:T(8,128)(2,1)} fusion(bf16[3584,512]{1,0:T(8,128)(2,1)} %param.14, bf16[32,3584]{1,0:T(8,128)(2,1)S(1)} %collective-permute-done.2, bf16[32,3584]{1,0:T(8,128)(2,1)S(1)} %collective-permute-done.1, bf16[32,3584]{1,0:T(8,128)(2,1)S(1)} %collective-permute-done, bf16[32,3584]{1,0:T(8,128)(2,1)S(1)} %copy-done.3, f32[]{:T(128)S(6)} %div.3), kind=kOutput, calls=%fused_computation.1 | convolution fusion | flops 473563136 | bytes 4718596 | tf_op jit(solution)/shard_map/dot_general | solution.py:261
  45.3 21.1 %collective-permute-done.16.refs_6_ = bf16[3,128,256]{2,1,0:T(8,128)(2,1)S(1)} collective-permute-done((bf16[3,128,256]{2,1,0:T(8,128)(2,1)}, bf16[3,128,256]{2,1,0:T(8,128)(2,1)S(1)}, u32[]{:S(2)}, u32[]{:S(2)}) %collective-permute-start.16) | collective-permute-done | bytes 196640 | tf_op jit(solution)/shard_map/ppermute | solution.py:252
  67.8 5.9 %shard_map.116 = (bf16[3,128,256]{2,1,0:T(8,128)(2,1)}, bf16[3,128,256]{2,1,0:T(8,128)(2,1)}, bf16[3,128,256]{2,1,0:T(8,128)(2,1)}, bf16[3,128,256]{2,1,0:T(8,128)(2,1)}) custom-call(s32[1]{0:T(128)} %bitcast.here_ref.refs_0_, bf16[128,512]{1,0:T(8,128)(2,1)} %fusion.refs_1_, bf16[1,128,2048]{2,1,0:T(8,128)(2,1)} %refs_2_.9, bf16[1,128,2048]{2,1,0:T(8,128)(2,1)} %refs_3_.5, ...), custom_call_target="tpu_custom_call" | custom-call | flops 671088640 | bytes 1572864 | tf_op jit(solution)/shard_map/pallas_call | solution.py:175
  73.7 3.9 %collective-permute-start.18 = (bf16[3,128,256]{2,1,0:T(8,128)(2,1)}, bf16[3,128,256]{2,1,0:T(8,128)(2,1)S(1)}, u32[]{:S(2)}, u32[]{:S(2)}) collective-permute-start(bf16[3,128,256]{2,1,0:T(8,128)(2,1)} %get-tuple-element.42), channel_id=1, source_target_pairs={{0,1},{1,0},{2,3},{3,2},{4,5},{5,4},{6,7},{7,6},{8,9},{9,8},{10,11... | collective-permute-start | bytes 589832 | tf_op jit(solution)/shard_map/ppermute | solution.py:273
  78.5 1.5 %collective-permute-start.20 = (bf16[3,128,256]{2,1,0:T(8,128)(2,1)}, bf16[3,128,256]{2,1,0:T(8,128)(2,1)S(1)}, u32[]{:S(2)}, u32[]{:S(2)}) collective-permute-start(bf16[3,128,256]{2,1,0:T(8,128)(2,1)} %get-tuple-element.44), channel_id=1, source_target_pairs={{0,3},{1,2},{2,1},{3,0},{4,7},{5,6},{6,5},{7,4},{8,11},{9,10},{10,... | collective-permute-start | bytes 589832 | tf_op jit(solution)/shard_map/ppermute | solution.py:273
  81.4 3.8 %shard_map.114 = (bf16[3,128,128]{2,1,0:T(8,128)(2,1)}, bf16[3,128,128]{2,1,0:T(8,128)(2,1)}, bf16[3,128,128]{2,1,0:T(8,128)(2,1)}, bf16[3,128,128]{2,1,0:T(8,128)(2,1)}) custom-call(s32[1]{0:T(128)} %bitcast.here_ref.refs_0_, bf16[128,512]{1,0:T(8,128)(2,1)} %fusion.refs_1_, bf16[1,128,2048]{2,1,0:T(8,128)(2,1)} %refs_2_.9, bf16[1,128,2048]{2,1,0:T(8,128)(2,1)} %refs_3_.5, ...), custom_call_target="tpu_custom_call" | custom-call | flops 335544320 | bytes 786432 | tf_op jit(solution)/shard_map/pallas_call | solution.py:175
  85.1 1.0 collective-permute-start.12
  86.2 1.9 %collective-permute-start.13 = (bf16[3,128,128]{2,1,0:T(8,128)(2,1)}, bf16[3,128,128]{2,1,0:T(8,128)(2,1)S(1)}, u32[]{:S(2)}, u32[]{:S(2)}) collective-permute-start(bf16[3,128,128]{2,1,0:T(8,128)(2,1)} %get-tuple-element.36), channel_id=1, source_target_pairs={{0,2},{1,3},{2,0},{3,1},{4,6},{5,7},{6,4},{7,5},{8,10},{9,11},{10,... | collective-permute-start | bytes 294920 | tf_op jit(solution)/shard_map/ppermute | solution.py:273
  88.0 3.8 %shard_map.113 = (bf16[3,128,128]{2,1,0:T(8,128)(2,1)}, bf16[3,128,128]{2,1,0:T(8,128)(2,1)}, bf16[3,128,128]{2,1,0:T(8,128)(2,1)}, bf16[3,128,128]{2,1,0:T(8,128)(2,1)}) custom-call(s32[1]{0:T(128)} %bitcast.here_ref.refs_0_, bf16[128,512]{1,0:T(8,128)(2,1)} %fusion.refs_1_, bf16[1,128,2048]{2,1,0:T(8,128)(2,1)} %refs_2_.9, bf16[1,128,2048]{2,1,0:T(8,128)(2,1)} %refs_3_.5, ...), custom_call_target="tpu_custom_call" | custom-call | flops 335544320 | bytes 786432 | tf_op jit(solution)/shard_map/pallas_call | solution.py:175
  91.8 2.0 %collective-permute-done.12.refs_2_ = bf16[3,128,128]{2,1,0:T(8,128)(2,1)S(1)} collective-permute-done((bf16[3,128,128]{2,1,0:T(8,128)(2,1)}, bf16[3,128,128]{2,1,0:T(8,128)(2,1)S(1)}, u32[]{:S(2)}, u32[]{:S(2)}) %collective-permute-start.12) | collective-permute-done | bytes 98336 | tf_op jit(solution)/shard_map/ppermute | solution.py:273
  93.8 2.4 %collective-permute-start.14 = (bf16[3,128,128]{2,1,0:T(8,128)(2,1)S(1)}, bf16[3,128,128]{2,1,0:T(8,128)(2,1)S(1)}, u32[]{:S(2)}, u32[]{:S(2)}) collective-permute-start(bf16[3,128,128]{2,1,0:T(8,128)(2,1)S(1)} %copy-done.16), channel_id=1, source_target_pairs={{0,3},{1,2},{2,1},{3,0},{4,7},{5,6},{6,5},{7,4},{8,11},{9,10},{10,... | collective-permute-start | bytes 294920 | tf_op jit(solution)/shard_map/ppermute | solution.py:273
  96.5 1.2 %collective-permute-done.19.refs_3_ = bf16[3,128,256]{2,1,0:T(8,128)(2,1)S(1)} collective-permute-done((bf16[3,128,256]{2,1,0:T(8,128)(2,1)}, bf16[3,128,256]{2,1,0:T(8,128)(2,1)S(1)}, u32[]{:S(2)}, u32[]{:S(2)}) %collective-permute-start.19) | collective-permute-done | bytes 196640 | tf_op jit(solution)/shard_map/ppermute | solution.py:273
  98.2 2.4 %collective-permute-start.11 = (bf16[3,128,128]{2,1,0:T(8,128)(2,1)}, bf16[3,128,128]{2,1,0:T(8,128)(2,1)S(1)}, u32[]{:S(2)}, u32[]{:S(2)}) collective-permute-start(bf16[3,128,128]{2,1,0:T(8,128)(2,1)} %get-tuple-element.33), channel_id=1, source_target_pairs={{0,3},{1,2},{2,1},{3,0},{4,7},{5,6},{6,5},{7,4},{8,11},{9,10},{10,... | collective-permute-start | bytes 294920 | tf_op jit(solution)/shard_map/ppermute | solution.py:273
  100.6 2.2 %shard_map.117 = (bf16[1,128,2048]{2,1,0:T(8,128)(2,1)}, bf16[1,128,2048]{2,1,0:T(8,128)(2,1)}, bf16[1,128,2048]{2,1,0:T(8,128)(2,1)}) custom-call(s32[1]{0:T(128)} %bitcast.here_ref.refs_0_, bf16[3,128,256]{2,1,0:T(8,128)(2,1)} %get-tuple-element.41.refs_1_, bf16[3,128,256]{2,1,0:T(8,128)(2,1)} %copy-done.4, bf16[3,128,256]{2,1,0:T(8,128)(2,1)} %copy-done.5, ...), custom_call_target="tpu_custom_call" | custom-call | bytes 1572864 | tf_op jit(solution)/shard_map/pallas_call | solution.py:222
  102.8 6.5 %collective-permute-done.13.refs_3_ = bf16[3,128,128]{2,1,0:T(8,128)(2,1)S(1)} collective-permute-done((bf16[3,128,128]{2,1,0:T(8,128)(2,1)}, bf16[3,128,128]{2,1,0:T(8,128)(2,1)S(1)}, u32[]{:S(2)}, u32[]{:S(2)}) %collective-permute-start.13) | collective-permute-done | bytes 98336 | tf_op jit(solution)/shard_map/ppermute | solution.py:273
  110.0 1.9 %shard_map.118 = (bf16[1,128,2048]{2,1,0:T(8,128)(2,1)}, bf16[1,128,2048]{2,1,0:T(8,128)(2,1)}, bf16[1,128,2048]{2,1,0:T(8,128)(2,1)}) custom-call(s32[1]{0:T(128)} %bitcast.here_ref.refs_0_, bf16[3,128,128]{2,1,0:T(8,128)(2,1)} %get-tuple-element.34.refs_1_, ...), custom_call_target="tpu_custom_call", output_to_operand_aliasing={{0}: (5, {}), {1}: (6, {}), {2}: (7, {})} | custom-call | bytes 786432 | tf_op jit(solution)/shard_map/pallas_call | solution.py:222
  111.9 1.6 %collective-permute-done.10.refs_3_ = bf16[3,128,128]{2,1,0:T(8,128)(2,1)S(1)} collective-permute-done((bf16[3,128,128]{2,1,0:T(8,128)(2,1)}, bf16[3,128,128]{2,1,0:T(8,128)(2,1)S(1)}, u32[]{:S(2)}, u32[]{:S(2)}) %collective-permute-start.10) | collective-permute-done | bytes 98336 | tf_op jit(solution)/shard_map/ppermute | solution.py:273
  114.2 1.9 %shard_map.119 = (bf16[1,128,2048]{2,1,0:T(8,128)(2,1)}, bf16[1,128,2048]{2,1,0:T(8,128)(2,1)}, bf16[1,128,2048]{2,1,0:T(8,128)(2,1)}) custom-call(s32[1]{0:T(128)} %bitcast.here_ref.refs_0_, bf16[3,128,128]{2,1,0:T(8,128)(2,1)} %get-tuple-element.30.refs_1_, ...), custom_call_target="tpu_custom_call", output_to_operand_aliasing={{0}: (5, {}), {1}: (6, {}), {2}: (7, {})} | custom-call | bytes 786432 | tf_op jit(solution)/shard_map/pallas_call | solution.py:222
  (55 shorter events, 8.6 us)
Async XLA Ops:
  4.3 37.7 %copy-start.3 = (bf16[32,3584]{1,0:T(8,128)(2,1)S(1)}, bf16[32,3584]{1,0:T(8,128)(2,1)}, u32[]{:S(2)}) copy-start(bf16[32,3584]{1,0:T(8,128)(2,1)} %visual.1) | copy-start | bytes 688132
  4.3 13.5 %collective-permute-start.1 = (bf16[32,3584]{1,0:T(8,128)(2,1)}, bf16[32,3584]{1,0:T(8,128)(2,1)S(1)}, u32[]{:S(2)}, u32[]{:S(2)}) collective-permute-start(bf16[32,3584]{1,0:T(8,128)(2,1)} %visual.1), channel_id=1, source_target_pairs={{0,2},{1,3},{2,0},{3,1},{4,6},{5,7},{6,4},{7,5},{8,10},{9,11},{10,... | collective-permute-start | bytes 688136 | tf_op jit(solution)/shard_map/ppermute | solution.py:105
  6.9 31.7 %collective-permute-start = (bf16[32,3584]{1,0:T(8,128)(2,1)}, bf16[32,3584]{1,0:T(8,128)(2,1)S(1)}, u32[]{:S(2)}, u32[]{:S(2)}) collective-permute-start(bf16[32,3584]{1,0:T(8,128)(2,1)} %visual.1), channel_id=1, source_target_pairs={{0,1},{1,0},{2,3},{3,2},{4,5},{5,4},{6,7},{7,6},{8,9},{9,8},{10,11... | collective-permute-start | bytes 688136 | tf_op jit(solution)/shard_map/ppermute | solution.py:105
  17.8 21.9 %collective-permute-start.2 = (bf16[32,3584]{1,0:T(8,128)(2,1)S(1)}, bf16[32,3584]{1,0:T(8,128)(2,1)S(1)}, u32[]{:S(2)}, u32[]{:S(2)}) collective-permute-start(bf16[32,3584]{1,0:T(8,128)(2,1)S(1)} %collective-permute-done.1), channel_id=1, source_target_pairs={{0,1},{1,0},{2,3},{3,2},{4,5},{5,4},{6,7},{7,6},{8,9},{9,8},{10,11... | collective-permute-start | bytes 688136 | tf_op jit(solution)/shard_map/ppermute | solution.py:105
  20.4 17.5 %collective-permute-start.15 = (bf16[3,128,256]{2,1,0:T(8,128)(2,1)}, bf16[3,128,256]{2,1,0:T(8,128)(2,1)S(1)}, u32[]{:S(2)}, u32[]{:S(2)}) collective-permute-start(bf16[3,128,256]{2,1,0:T(8,128)(2,1)} %get-tuple-element.38), channel_id=1, source_target_pairs={{0,1},{1,0},{2,3},{3,2},{4,5},{5,4},{6,7},{7,6},{8,9},{9,8},{10,11... | collective-permute-start | bytes 589832 | tf_op jit(solution)/shard_map/ppermute | solution.py:252
  21.9 3.4 %collective-permute-start.3 = (f32[]{:T(128)}, f32[]{:T(128)}, u32[]{:S(2)}, u32[]{:S(2)}) collective-permute-start(f32[]{:T(128)} %bitcast.1), channel_id=1, source_target_pairs={{0,4},{4,0},{8,12},{12,8},{16,20},{20,16},{24,28},{28,24},{1,5},{5... | collective-permute-start | bytes 20 | tf_op jit(solution)/shard_map/ppermute | solution.py:94
  23.9 54.7 %collective-permute-start.6 = (bf16[3,128,256]{2,1,0:T(8,128)(2,1)}, bf16[3,128,256]{2,1,0:T(8,128)(2,1)S(1)}, u32[]{:S(2)}, u32[]{:S(2)}) collective-permute-start(bf16[3,128,256]{2,1,0:T(8,128)(2,1)} %get-tuple-element.27), channel_id=1, source_target_pairs={{0,1},{1,0},{2,3},{3,2},{4,5},{5,4},{6,7},{7,6},{8,9},{9,8},{10,11... | collective-permute-start | bytes 589832 | tf_op jit(solution)/shard_map/ppermute | solution.py:252
  25.9 3.7 %collective-permute-start.4 = (f32[]{:T(128)}, f32[]{:T(128)}, u32[]{:S(2)}, u32[]{:S(2)}) collective-permute-start(f32[]{:T(128)} %add.9), channel_id=1, source_target_pairs={{0,8},{4,12},{8,0},{12,4},{16,24},{20,28},{24,16},{28,20},{1,9},{5... | collective-permute-start | bytes 20 | tf_op jit(solution)/shard_map/ppermute | solution.py:94
  30.3 3.7 %collective-permute-start.5 = (f32[]{:T(128)}, f32[]{:T(128)}, u32[]{:S(2)}, u32[]{:S(2)}) collective-permute-start(f32[]{:T(128)} %add.10), channel_id=1, source_target_pairs={{0,16},{4,20},{8,24},{12,28},{16,0},{20,4},{24,8},{28,12},{1,17},{... | collective-permute-start | bytes 20 | tf_op jit(solution)/shard_map/ppermute | solution.py:94
  34.0 46.0 %collective-permute-start.7 = (bf16[3,128,256]{2,1,0:T(8,128)(2,1)}, bf16[3,128,256]{2,1,0:T(8,128)(2,1)S(1)}, u32[]{:S(2)}, u32[]{:S(2)}) collective-permute-start(bf16[3,128,256]{2,1,0:T(8,128)(2,1)} %get-tuple-element.28), channel_id=1, source_target_pairs={{0,2},{1,3},{2,0},{3,1},{4,6},{5,7},{6,4},{7,5},{8,10},{9,11},{10,... | collective-permute-start | bytes 589832 | tf_op jit(solution)/shard_map/ppermute | solution.py:252
  38.0 7.3 %copy-start.13 = (bf16[3,128,256]{2,1,0:T(8,128)(2,1)}, bf16[3,128,256]{2,1,0:T(8,128)(2,1)S(1)}, u32[]{:S(2)}) copy-start(bf16[3,128,256]{2,1,0:T(8,128)(2,1)S(1)} %collective-permute-done.15.refs_5_) | copy-start | bytes 589828
  38.0 42.0 %collective-permute-start.8 = (bf16[3,128,256]{2,1,0:T(8,128)(2,1)}, bf16[3,128,256]{2,1,0:T(8,128)(2,1)S(1)}, u32[]{:S(2)}, u32[]{:S(2)}) collective-permute-start(bf16[3,128,256]{2,1,0:T(8,128)(2,1)} %get-tuple-element.29), channel_id=1, source_target_pairs={{0,3},{1,2},{2,1},{3,0},{4,7},{5,6},{6,5},{7,4},{8,11},{9,10},{10,... | collective-permute-start | bytes 589832 | tf_op jit(solution)/shard_map/ppermute | solution.py:252
  38.5 27.9 %collective-permute-start.16 = (bf16[3,128,256]{2,1,0:T(8,128)(2,1)}, bf16[3,128,256]{2,1,0:T(8,128)(2,1)S(1)}, u32[]{:S(2)}, u32[]{:S(2)}) collective-permute-start(bf16[3,128,256]{2,1,0:T(8,128)(2,1)} %get-tuple-element.39), channel_id=1, source_target_pairs={{0,2},{1,3},{2,0},{3,1},{4,6},{5,7},{6,4},{7,5},{8,10},{9,11},{10,... | collective-permute-start | bytes 589832 | tf_op jit(solution)/shard_map/ppermute | solution.py:252
  39.6 26.8 %collective-permute-start.17 = (bf16[3,128,256]{2,1,0:T(8,128)(2,1)}, bf16[3,128,256]{2,1,0:T(8,128)(2,1)S(1)}, u32[]{:S(2)}, u32[]{:S(2)}) collective-permute-start(bf16[3,128,256]{2,1,0:T(8,128)(2,1)} %get-tuple-element.40), channel_id=1, source_target_pairs={{0,3},{1,2},{2,1},{3,0},{4,7},{5,6},{6,5},{7,4},{8,11},{9,10},{10,... | collective-permute-start | bytes 589832 | tf_op jit(solution)/shard_map/ppermute | solution.py:252
  73.7 22.5 %collective-permute-start.18 = (bf16[3,128,256]{2,1,0:T(8,128)(2,1)}, bf16[3,128,256]{2,1,0:T(8,128)(2,1)S(1)}, u32[]{:S(2)}, u32[]{:S(2)}) collective-permute-start(bf16[3,128,256]{2,1,0:T(8,128)(2,1)} %get-tuple-element.42), channel_id=1, source_target_pairs={{0,1},{1,0},{2,3},{3,2},{4,5},{5,4},{6,7},{7,6},{8,9},{9,8},{10,11... | collective-permute-start | bytes 589832 | tf_op jit(solution)/shard_map/ppermute | solution.py:273
  77.6 20.1 %collective-permute-start.19 = (bf16[3,128,256]{2,1,0:T(8,128)(2,1)}, bf16[3,128,256]{2,1,0:T(8,128)(2,1)S(1)}, u32[]{:S(2)}, u32[]{:S(2)}) collective-permute-start(bf16[3,128,256]{2,1,0:T(8,128)(2,1)} %get-tuple-element.43), channel_id=1, source_target_pairs={{0,2},{1,3},{2,0},{3,1},{4,6},{5,7},{6,4},{7,5},{8,10},{9,11},{10,... | collective-permute-start | bytes 589832 | tf_op jit(solution)/shard_map/ppermute | solution.py:273
  78.5 1.5 %copy-start = (bf16[3,128,256]{2,1,0:T(8,128)(2,1)}, bf16[3,128,256]{2,1,0:T(8,128)(2,1)S(1)}, u32[]{:S(2)}) copy-start(bf16[3,128,256]{2,1,0:T(8,128)(2,1)S(1)} %collective-permute-done.6.refs_5_) | copy-start | bytes 589828
  78.5 19.6 %collective-permute-start.20 = (bf16[3,128,256]{2,1,0:T(8,128)(2,1)}, bf16[3,128,256]{2,1,0:T(8,128)(2,1)S(1)}, u32[]{:S(2)}, u32[]{:S(2)}) collective-permute-start(bf16[3,128,256]{2,1,0:T(8,128)(2,1)} %get-tuple-element.44), channel_id=1, source_target_pairs={{0,3},{1,2},{2,1},{3,0},{4,7},{5,6},{6,5},{7,4},{8,11},{9,10},{10,... | collective-permute-start | bytes 589832 | tf_op jit(solution)/shard_map/ppermute | solution.py:273
  80.0 0.7 copy-start.1
  85.1 8.7 %copy-start.16 = (bf16[3,128,128]{2,1,0:T(8,128)(2,1)S(1)}, bf16[3,128,128]{2,1,0:T(8,128)(2,1)}, u32[]{:S(2)}) copy-start(bf16[3,128,128]{2,1,0:T(8,128)(2,1)} %get-tuple-element.37) | copy-start | bytes 294916
  85.1 8.7 %collective-permute-start.12 = (bf16[3,128,128]{2,1,0:T(8,128)(2,1)}, bf16[3,128,128]{2,1,0:T(8,128)(2,1)S(1)}, u32[]{:S(2)}, u32[]{:S(2)}) collective-permute-start(bf16[3,128,128]{2,1,0:T(8,128)(2,1)} %get-tuple-element.35), channel_id=1, source_target_pairs={{0,1},{1,0},{2,3},{3,2},{4,5},{5,4},{6,7},{7,6},{8,9},{9,8},{10,11... | collective-permute-start | bytes 294920 | tf_op jit(solution)/shard_map/ppermute | solution.py:273
  86.2 23.1 %collective-permute-start.13 = (bf16[3,128,128]{2,1,0:T(8,128)(2,1)}, bf16[3,128,128]{2,1,0:T(8,128)(2,1)S(1)}, u32[]{:S(2)}, u32[]{:S(2)}) collective-permute-start(bf16[3,128,128]{2,1,0:T(8,128)(2,1)} %get-tuple-element.36), channel_id=1, source_target_pairs={{0,2},{1,3},{2,0},{3,1},{4,6},{5,7},{6,4},{7,5},{8,10},{9,11},{10,... | collective-permute-start | bytes 294920 | tf_op jit(solution)/shard_map/ppermute | solution.py:273
  93.8 15.5 %copy-start.7 = (bf16[3,128,128]{2,1,0:T(8,128)(2,1)}, bf16[3,128,128]{2,1,0:T(8,128)(2,1)S(1)}, u32[]{:S(2)}) copy-start(bf16[3,128,128]{2,1,0:T(8,128)(2,1)S(1)} %collective-permute-done.12.refs_2_) | copy-start | bytes 294916
  93.8 15.5 %collective-permute-start.14 = (bf16[3,128,128]{2,1,0:T(8,128)(2,1)S(1)}, bf16[3,128,128]{2,1,0:T(8,128)(2,1)S(1)}, u32[]{:S(2)}, u32[]{:S(2)}) collective-permute-start(bf16[3,128,128]{2,1,0:T(8,128)(2,1)S(1)} %copy-done.16), channel_id=1, source_target_pairs={{0,3},{1,2},{2,1},{3,0},{4,7},{5,6},{6,5},{7,4},{8,11},{9,10},{10,... | collective-permute-start | bytes 294920 | tf_op jit(solution)/shard_map/ppermute | solution.py:273
  96.2 4.4 %copy-start.4 = (bf16[3,128,256]{2,1,0:T(8,128)(2,1)}, bf16[3,128,256]{2,1,0:T(8,128)(2,1)S(1)}, u32[]{:S(2)}) copy-start(bf16[3,128,256]{2,1,0:T(8,128)(2,1)S(1)} %collective-permute-done.18.refs_2_) | copy-start | bytes 589828
  96.2 15.7 %collective-permute-start.9 = (bf16[3,128,128]{2,1,0:T(8,128)(2,1)}, bf16[3,128,128]{2,1,0:T(8,128)(2,1)S(1)}, u32[]{:S(2)}, u32[]{:S(2)}) collective-permute-start(bf16[3,128,128]{2,1,0:T(8,128)(2,1)} %get-tuple-element.31), channel_id=1, source_target_pairs={{0,1},{1,0},{2,3},{3,2},{4,5},{5,4},{6,7},{7,6},{8,9},{9,8},{10,11... | collective-permute-start | bytes 294920 | tf_op jit(solution)/shard_map/ppermute | solution.py:273
  97.7 2.9 %copy-start.5 = (bf16[3,128,256]{2,1,0:T(8,128)(2,1)}, bf16[3,128,256]{2,1,0:T(8,128)(2,1)S(1)}, u32[]{:S(2)}) copy-start(bf16[3,128,256]{2,1,0:T(8,128)(2,1)S(1)} %collective-permute-done.19.refs_3_) | copy-start | bytes 589828
  97.7 15.7 %collective-permute-start.10 = (bf16[3,128,128]{2,1,0:T(8,128)(2,1)}, bf16[3,128,128]{2,1,0:T(8,128)(2,1)S(1)}, u32[]{:S(2)}, u32[]{:S(2)}) collective-permute-start(bf16[3,128,128]{2,1,0:T(8,128)(2,1)} %get-tuple-element.32), channel_id=1, source_target_pairs={{0,2},{1,3},{2,0},{3,1},{4,6},{5,7},{6,4},{7,5},{8,10},{9,11},{10,... | collective-permute-start | bytes 294920 | tf_op jit(solution)/shard_map/ppermute | solution.py:273
  98.2 2.4 %copy-start.6 = (bf16[3,128,256]{2,1,0:T(8,128)(2,1)}, bf16[3,128,256]{2,1,0:T(8,128)(2,1)S(1)}, u32[]{:S(2)}) copy-start(bf16[3,128,256]{2,1,0:T(8,128)(2,1)S(1)} %collective-permute-done.20.refs_4_) | copy-start | bytes 589828
  98.2 15.3 %collective-permute-start.11 = (bf16[3,128,128]{2,1,0:T(8,128)(2,1)}, bf16[3,128,128]{2,1,0:T(8,128)(2,1)S(1)}, u32[]{:S(2)}, u32[]{:S(2)}) collective-permute-start(bf16[3,128,128]{2,1,0:T(8,128)(2,1)} %get-tuple-element.33), channel_id=1, source_target_pairs={{0,3},{1,2},{2,1},{3,0},{4,7},{5,6},{6,5},{7,4},{8,11},{9,10},{10,... | collective-permute-start | bytes 294920 | tf_op jit(solution)/shard_map/ppermute | solution.py:273
  111.9 1.6 %copy-start.9 = (bf16[3,128,128]{2,1,0:T(8,128)(2,1)}, bf16[3,128,128]{2,1,0:T(8,128)(2,1)S(1)}, u32[]{:S(2)}) copy-start(bf16[3,128,128]{2,1,0:T(8,128)(2,1)S(1)} %collective-permute-done.9.refs_2_) | copy-start | bytes 294916
  113.5 0.7 copy-start.11
  (6 other events, 4.0 us)

commit v3 on v2

--- a/solution.py
+++ b/solution.py
@@ -22,7 +22,14 @@
     first_both = (((0,), (0,)), ((), ()))
     hidden = lax.dot_general(pick, hidden_ref[0], first_both, preferred_element_type=jnp.float32)
     cot = lax.dot_general(pick, cot_ref[0], first_both, preferred_element_type=jnp.float32)
-    scaled_cot = cot * gain_ref[...]
+    lanes = gain_ref.shape[1]
+    scaled_cot = jnp.concatenate(
+        [
+            cot[:, j * lanes : (j + 1) * lanes] * gain_ref[pl.ds(j, 1)]
+            for j in range(gain_ref.shape[0])
+        ],
+        axis=1,
+    )
     inv_rms = lax.rsqrt(jnp.mean(hidden * hidden, axis=-1, keepdims=True) + 1e-06)
     mixed = jnp.mean(hidden * scaled_cot, axis=-1, keepdims=True)
     out_ref[...] = (inv_rms * scaled_cot - hidden * (inv_rms * inv_rms * inv_rms * mixed)).astype(
@@ -41,8 +48,9 @@
         cost_estimate=pl.CostEstimate(
             flops=4 * picked * hidden.size, bytes_accessed=4 * hidden.size, transcendentals=0
         ),
+        compiler_params=pltpu.CompilerParams(vmem_limit_bytes=(8 << 20) + 12 * hidden.size),
         name="visual",
-    )(here, positions, hidden, cotangent, gain[None])
+    )(here, positions, hidden, cotangent, gain.reshape(-1, HD))
 
 
 def pack_kernel(count, first, here_ref, *refs):
@@ -50,12 +58,12 @@
     width = outs[0].shape[2]
     own_width = sources[0].shape[2] // count
     copies = []
-    for k, out in enumerate(outs, 1):
+    for k, out in enumerate(outs):
         column = pl.multiple_of((here_ref[0] ^ k) * own_width + first, HD)
         for i, source in enumerate(sources):
             copies.append(
                 pltpu.make_async_copy(
-                    source.at[0, :, pl.ds(column, width)], out.at[i], sems.at[3 * k - 3 + i]
+                    source.at[0, :, pl.ds(column, width)], out.at[i], sems.at[3 * k + i]
                 )
             )
     for copy in copies:
@@ -70,11 +78,14 @@
         functools.partial(pack_kernel, count, first),
         in_specs=[pl.BlockSpec(memory_space=pltpu.SMEM)]
         + [pl.BlockSpec(memory_space=pl.ANY)] * 3,
-        out_specs=[pl.BlockSpec(memory_space=pltpu.VMEM)] * (count - 1),
-        out_shape=[jax.ShapeDtypeStruct((3, rows, width), jnp.bfloat16)] * (count - 1),
-        scratch_shapes=[pltpu.SemaphoreType.DMA((3 * count - 3,))],
+        out_specs=[pl.BlockSpec(memory_space=pltpu.VMEM)] * count,
+        out_shape=[jax.ShapeDtypeStruct((3, rows, width), jnp.bfloat16)] * count,
+        scratch_shapes=[pltpu.SemaphoreType.DMA((3 * count,))],
         cost_estimate=pl.CostEstimate(
             flops=0, bytes_accessed=12 * count * rows * width, transcendentals=0
+        ),
+        compiler_params=pltpu.CompilerParams(
+            vmem_limit_bytes=(1 << 20) + 6 * count * rows * width
         ),
     )(here, *sources)
 
@@ -108,17 +119,14 @@
 
 
 def attend_kernel(count, scale, chunk, *refs):
-    _, handed_ref, query_ref, key_ref, value_ref = refs[:5]
-    blocks = refs[5 : 4 + count]
-    outs = refs[4 + count : 4 + 2 * count]
-    q_s, k_s, v_s, g_s, dq_s, dk_s, dv_s = refs[4 + 2 * count :]
-    rows = query_ref.shape[1]
+    handed_ref = refs[0]
+    blocks = refs[1 : 1 + count]
+    outs = refs[1 + count : 1 + 2 * count]
+    q_s, k_s, v_s, g_s, dq_s, dk_s, dv_s = refs[1 + 2 * count :]
+    rows = blocks[0].shape[1]
     length = rows * count
     seen = handed_ref.shape[0] // count
-    q_s[pl.ds(0, rows)] = query_ref[0]
-    k_s[pl.ds(0, rows)] = key_ref[0]
-    v_s[pl.ds(0, rows)] = value_ref[0]
-    for j, block in enumerate(blocks, 1):
+    for j, block in enumerate(blocks):
         at = pl.ds(j * rows, rows)
         q_s[at] = block[0]
         k_s[at] = block[1]
@@ -163,34 +171,31 @@
         out[2] = dv_s[at].astype(jnp.bfloat16)
 
 
-def attend(here, handed, own, blocks, first, skip, heads, count):
-    rows = own[0].shape[1]
-    local_heads = handed.shape[1] // HD
+def attend(handed, blocks, first, skip, heads):
+    count = len(blocks)
+    rows = blocks[0].shape[1]
     length = rows * count
     chunk = min(256, length)
-    own_spec = pl.BlockSpec((1, rows, HD), lambda h, t: (0, 0, t[0] * local_heads + first + h))
-    out_spec = pl.BlockSpec((3, rows, HD), lambda h, t: (0, 0, h))
-    block_spec = pl.BlockSpec((3, rows, HD), lambda h, t: (0, 0, skip + h))
-    flops = 10 * heads * length * length * HD
+    out_spec = pl.BlockSpec((3, rows, HD), lambda h: (0, 0, h))
+    block_spec = pl.BlockSpec((3, rows, HD), lambda h: (0, 0, skip + h))
     return pl.pallas_call(
         functools.partial(attend_kernel, count, HD**-0.5, chunk),
-        grid_spec=pltpu.PrefetchScalarGridSpec(
-            num_scalar_prefetch=1,
-            grid=(heads,),
-            in_specs=[pl.BlockSpec((handed.shape[0], HD), lambda h, t: (0, first + h))]
-            + [own_spec] * 3
-            + [block_spec] * (count - 1),
-            out_specs=[out_spec] * count,
-            scratch_shapes=[pltpu.VMEM((length, HD), jnp.bfloat16)] * 5
-            + [pltpu.VMEM((length, HD), jnp.float32)] * 2,
-        ),
+        grid=(heads,),
+        in_specs=[pl.BlockSpec((handed.shape[0], HD), lambda h: (0, first + h))]
+        + [block_spec] * count,
+        out_specs=[out_spec] * count,
+        scratch_shapes=[pltpu.VMEM((length, HD), jnp.bfloat16)] * 5
+        + [pltpu.VMEM((length, HD), jnp.float32)] * 2,
         out_shape=[jax.ShapeDtypeStruct((3, rows, heads * HD), jnp.bfloat16)] * count,
         cost_estimate=pl.CostEstimate(
-            flops=flops,
+            flops=10 * heads * length * length * HD,
             bytes_accessed=12 * length * heads * HD,
             transcendentals=heads * length * length,
         ),
-    )(here, handed, *own, *blocks)
+        compiler_params=pltpu.CompilerParams(
+            vmem_limit_bytes=(4 << 20) + 48 * length * chunk
+        ),
+    )(handed, *blocks)
 
 
 def place_kernel(count, first, *refs):
@@ -231,6 +236,9 @@
         cost_estimate=pl.CostEstimate(
             flops=0, bytes_accessed=4 * count * parts[0].size, transcendentals=0
         ),
+        compiler_params=pltpu.CompilerParams(
+            vmem_limit_bytes=(1 << 20) + 2 * count * parts[0].size
+        ),
     )(here, *parts, *outs)
 
 
@@ -248,9 +256,8 @@
     arrived = []
     for heads in split(own_width // HD, IN_HEADS):
         packed = pack(place_of, own, len(arrived) * HD, heads * HD, count)
-        blocks = [
-            lax.ppermute(packed[k - 1], "tensor", partners(count, k))
-            for k in range(1, count)
+        blocks = [packed[0]] + [
+            lax.ppermute(packed[k], "tensor", partners(count, k)) for k in range(1, count)
         ]
         arrived += [(blocks, skip) for skip in range(heads)]
 
@@ -268,7 +275,7 @@
     first = 0
     for heads in split(own_width // HD, OUT_HEADS):
         blocks, skip = arrived[first]
-        grads = attend(place_of, handed, own, blocks, first, skip, heads, count)
+        grads = attend(handed, blocks, first, skip, heads)
         parts = [grads[0]] + [
             lax.ppermute(grads[k], "tensor", partners(count, k)) for k in range(1, count)
         ]

time: 118 us -> 97.6 us (0.83)
  waiting for transfers between devices: 44.5 us -> 22.7 us
  starting transfers between devices: 33.7 us -> 48.1 us
  Pallas kernels: 25.7 us -> 11.9 us
  local copies, waits for them, and re-layouts: 5.41 us -> 6.62 us
    ppermute x6, waiting for transfers between devices: 21.1 us -> 1.23 us  [work(): lax.ppermute(packed[k], 'tensor', partners(count, k))]
    ppermute x9, starting transfers between devices: 14.7 us -> 28.9 us  [work(): lax.ppermute(grads[k], 'tensor', partners(count, k))]
    pallas_call x3, Pallas kernels: 13.4 us -> 8.32 us  [attend(): pl.pallas_call(functools.partial(attend_kernel, count, HD ** (-0.5), chun...]
    pallas_call x2, Pallas kernels: 4.02 us -> 0.51 us  [pack(): pl.pallas_call(functools.partial(pack_kernel, count, first), in_specs=[pl...]
    pallas_call x3, Pallas kernels: 5.93 us -> 2.64 us  [place(): pl.pallas_call(functools.partial(place_kernel, count, first), in_specs=[p...]
    unnamed x34 -> x20, local copies, waits for them, and re-layouts: 4.08 us -> 6.62 us
    pallas_call x1, Pallas kernels: 2.3 us -> 0.44 us  [visual_grads(): pl.pallas_call(visual_kernel, in_specs=[pl.BlockSpec(memory_space=pltpu.S...]
    ppermute x9, waiting for transfers between devices: 11.4 us -> 9.96 us  [work(): lax.ppermute(grads[k], 'tensor', partners(count, k))]
  transfers between devices with their start and end apart: 21 -> 21, of which waited for: 8 -> 7; matrix products, arithmetic and copies ran while one was open for 3% -> 3% of each run, Pallas kernels for 19% -> 11%
where the time goes in v3:
time: 97.6 us; the launch traced here: 95.7 us
  starting transfers between devices  48.1 us (49%)
  waiting for transfers between devices  22.7 us (23%)
  Pallas kernels  11.9 us (12%)
  local copies, waits for them, and re-layouts  6.62 us (7%)
  between operations  3.42 us (4%)
  matrix products  2.92 us (3%)
    ppermute x9, starting transfers between devices, work(): lax.ppermute(grads[k], 'tensor', partners(count, k))  28.9 us
    ppermute x9, waiting for transfers between devices, work(): lax.ppermute(grads[k], 'tensor', partners(count, k))  9.96 us
    ppermute x6, starting transfers between devices, work(): lax.ppermute(packed[k], 'tensor', partners(count, k))  9.67 us
    ppermute x3, waiting for transfers between devices, gathered(): held[k ^ step] = lax.ppermute(held[k], axis, partners(size, step))  9.09 us
    pallas_call x3, Pallas kernels, attend(): pl.pallas_call(functools.partial(attend_kernel, count, HD ** (-0.5), chun...  8.32 us
    unnamed x20, local copies, waits for them, and re-layouts  6.62 us
    ppermute x3, starting transfers between devices, gathered(): held[k ^ step] = lax.ppermute(held[k], axis, partners(size, step))  4.8 us
    ppermute x3, starting transfers between devices, total_over(): value = value + lax.ppermute(value, axis, partners(size, step))  4.78 us
  transfers between devices with their start and end apart: 21, of which 7 were waited for; matrix products, arithmetic and copies ran while one was open for 3% of the time, Pallas kernels for 11%

profile of v3, /device:TPU:2, one launch (start us, length us, event | category | flops | bytes accessed | tf_op | source)
XLA Modules:
  0.0 95.7 jit_solution(6448872076827501633)
XLA Ops:
  0.7 1.1 %copy-done.6 = bf16[1,64,3584]{2,1,0:T(8,128)(2,1)S(1)} copy-done((bf16[1,64,3584]{2,1,0:T(8,128)(2,1)S(1)}, bf16[1,64,3584]{2,1,0:T(8,128)(2,1)}, u32[]{:S(2)}) %copy-start.6) | copy-done | bytes 458776
  1.8 1.0 %copy-done.7 = bf16[1,64,3584]{2,1,0:T(8,128)(2,1)S(1)} copy-done((bf16[1,64,3584]{2,1,0:T(8,128)(2,1)S(1)}, bf16[1,64,3584]{2,1,0:T(8,128)(2,1)}, u32[]{:S(2)}) %copy-start.7) | copy-done | bytes 458776
  4.6 2.7 %collective-permute-start.1 = (bf16[32,3584]{1,0:T(8,128)(2,1)S(1)}, bf16[32,3584]{1,0:T(8,128)(2,1)S(1)}, u32[]{:S(2)}, u32[]{:S(2)}) collective-permute-start(bf16[32,3584]{1,0:T(8,128)(2,1)S(1)} %visual.1), channel_id=1, source_target_pairs={{0,2},{1,3},{2,0},{3,1},{4,6},{5,7},{6,4},{7,5},{8,10},{9,11},{10,... | collective-permute-start | bytes 688136 | tf_op jit(solution)/shard_map/ppermute | solution.py:116
  7.3 1.6 %collective-permute-start = (bf16[32,3584]{1,0:T(8,128)(2,1)S(1)}, bf16[32,3584]{1,0:T(8,128)(2,1)}, u32[]{:S(2)}, u32[]{:S(2)}) collective-permute-start(bf16[32,3584]{1,0:T(8,128)(2,1)S(1)} %visual.1), channel_id=1, source_target_pairs={{0,1},{1,0},{2,3},{3,2},{4,5},{5,4},{6,7},{7,6},{8,9},{9,8},{10,11... | collective-permute-start | bytes 688136 | tf_op jit(solution)/shard_map/ppermute | solution.py:116
  8.8 9.1 %collective-permute-done.1 = bf16[32,3584]{1,0:T(8,128)(2,1)S(1)} collective-permute-done((bf16[32,3584]{1,0:T(8,128)(2,1)S(1)}, bf16[32,3584]{1,0:T(8,128)(2,1)S(1)}, u32[]{:S(2)}, u32[]{:S(2)}) %collective-permute-start.1) | collective-permute-done | bytes 229408 | tf_op jit(solution)/shard_map/ppermute | solution.py:116
  18.5 1.0 %copy-done = bf16[1,128,2048]{2,1,0:T(8,128)(2,1)S(1)} copy-done((bf16[1,128,2048]{2,1,0:T(8,128)(2,1)S(1)}, bf16[1,128,2048]{2,1,0:T(8,128)(2,1)}, u32[]{:S(2)}) %copy-start) | copy-done | bytes 524312
  19.5 1.0 %copy-done.2 = bf16[1,128,2048]{2,1,0:T(8,128)(2,1)S(1)} copy-done((bf16[1,128,2048]{2,1,0:T(8,128)(2,1)S(1)}, bf16[1,128,2048]{2,1,0:T(8,128)(2,1)}, u32[]{:S(2)}) %copy-start.2) | copy-done | bytes 524312
  20.6 1.0 %copy-done.4 = bf16[1,128,2048]{2,1,0:T(8,128)(2,1)S(1)} copy-done((bf16[1,128,2048]{2,1,0:T(8,128)(2,1)S(1)}, bf16[1,128,2048]{2,1,0:T(8,128)(2,1)}, u32[]{:S(2)}) %copy-start.4) | copy-done | bytes 524312
  21.9 1.5 %collective-permute-start.15 = (bf16[3,128,256]{2,1,0:T(8,128)(2,1)S(1)}, bf16[3,128,256]{2,1,0:T(8,128)(2,1)S(1)}, u32[]{:S(2)}, u32[]{:S(2)}) collective-permute-start(bf16[3,128,256]{2,1,0:T(8,128)(2,1)S(1)} %get-tuple-element.42), channel_id=1, source_target_pairs={{0,1},{1,0},{2,3},{3,2},{4,5},{5,4},{6,7},{7,6},{8,9},{9,8},{10,11... | collective-permute-start | bytes 589832 | tf_op jit(solution)/shard_map/ppermute | solution.py:260
  23.4 2.1 %collective-permute-start.16 = (bf16[3,128,256]{2,1,0:T(8,128)(2,1)S(1)}, bf16[3,128,256]{2,1,0:T(8,128)(2,1)S(1)}, u32[]{:S(2)}, u32[]{:S(2)}) collective-permute-start(bf16[3,128,256]{2,1,0:T(8,128)(2,1)S(1)} %get-tuple-element.43), channel_id=1, source_target_pairs={{0,2},{1,3},{2,0},{3,1},{4,6},{5,7},{6,4},{7,5},{8,10},{9,11},{10,... | collective-permute-start | bytes 589832 | tf_op jit(solution)/shard_map/ppermute | solution.py:260
  27.1 1.9 %collective-permute-start.4 = (f32[]{:T(128)}, f32[]{:T(128)}, u32[]{:S(2)}, u32[]{:S(2)}) collective-permute-start(f32[]{:T(128)} %add.9), channel_id=1, source_target_pairs={{0,8},{4,12},{8,0},{12,4},{16,24},{20,28},{24,16},{28,20},{1,9},{5... | collective-permute-start | bytes 20 | tf_op jit(solution)/shard_map/ppermute | solution.py:105
  29.0 1.7 %collective-permute-done.4 = f32[]{:T(128)} collective-permute-done((f32[]{:T(128)}, f32[]{:T(128)}, u32[]{:S(2)}, u32[]{:S(2)}) %collective-permute-start.4) | collective-permute-done | bytes 36 | tf_op jit(solution)/shard_map/ppermute | solution.py:105
  31.3 2.9 %collective-permute-start.5 = (f32[]{:T(128)}, f32[]{:T(128)}, u32[]{:S(2)}, u32[]{:S(2)}) collective-permute-start(f32[]{:T(128)} %add.10), channel_id=1, source_target_pairs={{0,16},{4,20},{8,24},{12,28},{16,0},{20,4},{24,8},{28,12},{1,17},{... | collective-permute-start | bytes 20 | tf_op jit(solution)/shard_map/ppermute | solution.py:105
  34.9 1.6 %collective-permute-start.17 = (bf16[3,128,256]{2,1,0:T(8,128)(2,1)S(1)}, bf16[3,128,256]{2,1,0:T(8,128)(2,1)S(1)}, u32[]{:S(2)}, u32[]{:S(2)}) collective-permute-start(bf16[3,128,256]{2,1,0:T(8,128)(2,1)S(1)} %get-tuple-element.44), channel_id=1, source_target_pairs={{0,3},{1,2},{2,1},{3,0},{4,7},{5,6},{6,5},{7,4},{8,11},{9,10},{10,... | collective-permute-start | bytes 589832 | tf_op jit(solution)/shard_map/ppermute | solution.py:260
  37.5 2.5 %collective-permute-start.7 = (bf16[3,128,256]{2,1,0:T(8,128)(2,1)S(1)}, bf16[3,128,256]{2,1,0:T(8,128)(2,1)S(1)}, u32[]{:S(2)}, u32[]{:S(2)}) collective-permute-start(bf16[3,128,256]{2,1,0:T(8,128)(2,1)S(1)} %get-tuple-element.31), channel_id=1, source_target_pairs={{0,2},{1,3},{2,0},{3,1},{4,6},{5,7},{6,4},{7,5},{8,10},{9,11},{10,... | collective-permute-start | bytes 589832 | tf_op jit(solution)/shard_map/ppermute | solution.py:260
  40.0 1.6 %collective-permute-start.8 = (bf16[3,128,256]{2,1,0:T(8,128)(2,1)S(1)}, bf16[3,128,256]{2,1,0:T(8,128)(2,1)S(1)}, u32[]{:S(2)}, u32[]{:S(2)}) collective-permute-start(bf16[3,128,256]{2,1,0:T(8,128)(2,1)S(1)} %get-tuple-element.32), channel_id=1, source_target_pairs={{0,3},{1,2},{2,1},{3,0},{4,7},{5,6},{6,5},{7,4},{8,11},{9,10},{10,... | collective-permute-start | bytes 589832 | tf_op jit(solution)/shard_map/ppermute | solution.py:260
  41.7 2.9 %fusion.refs_0_ = bf16[128,512]{1,0:T(8,128)(2,1)S(1)} fusion(bf16[3584,512]{1,0:T(8,128)(2,1)} %param.14, bf16[32,3584]{1,0:T(8,128)(2,1)} %collective-permute-done.2, bf16[32,3584]{1,0:T(8,128)(2,1)S(1)} %collective-permute-done.1, bf16[32,3584]{1,0:T(8,128)(2,1)} %collective-permute-done, bf16[32,3584]{1,0:T(8,128)(2,1)S(1)} %visual.1, f32[]{:T(128)S(6)} %div.3), kind=kOutput, calls=%fused_computation.1 | convolution fusion | flops 473563136 | bytes 4718596 | tf_op jit(solution)/shard_map/dot_general | solution.py:268
  44.6 4.3 %shard_map.116 = (bf16[3,128,256]{2,1,0:T(8,128)(2,1)S(1)}, bf16[3,128,256]{2,1,0:T(8,128)(2,1)S(1)}, bf16[3,128,256]{2,1,0:T(8,128)(2,1)S(1)}, bf16[3,128,256]{2,1,0:T(8,128)(2,1)S(1)}) custom-call(bf16[128,512]{1,0:T(8,128)(2,1)S(1)} %fusion.refs_0_, bf16[3,128,256]{2,1,0:T(8,128)(2,1)S(1)} %get-tuple-element.41.refs_1_, ...), custom_call_target="tpu_custom_call" | custom-call | flops 671088640 | bytes 1572864 | tf_op jit(solution)/shard_map/pallas_call | solution.py:181
  48.9 10.7 %collective-permute-start.18 = (bf16[3,128,256]{2,1,0:T(8,128)(2,1)S(1)}, bf16[3,128,256]{2,1,0:T(8,128)(2,1)S(1)}, u32[]{:S(2)}, u32[]{:S(2)}) collective-permute-start(bf16[3,128,256]{2,1,0:T(8,128)(2,1)S(1)} %get-tuple-element.46), channel_id=1, source_target_pairs={{0,1},{1,0},{2,3},{3,2},{4,5},{5,4},{6,7},{7,6},{8,9},{9,8},{10,11... | collective-permute-start | bytes 589832 | tf_op jit(solution)/shard_map/ppermute | solution.py:280
  59.6 2.4 %collective-permute-start.20 = (bf16[3,128,256]{2,1,0:T(8,128)(2,1)S(1)}, bf16[3,128,256]{2,1,0:T(8,128)(2,1)S(1)}, u32[]{:S(2)}, u32[]{:S(2)}) collective-permute-start(bf16[3,128,256]{2,1,0:T(8,128)(2,1)S(1)} %get-tuple-element.48), channel_id=1, source_target_pairs={{0,3},{1,2},{2,1},{3,0},{4,7},{5,6},{6,5},{7,4},{8,11},{9,10},{10,... | collective-permute-start | bytes 589832 | tf_op jit(solution)/shard_map/ppermute | solution.py:280
  62.0 1.2 %collective-permute-done.7.refs_3_ = bf16[3,128,256]{2,1,0:T(8,128)(2,1)S(1)} collective-permute-done((bf16[3,128,256]{2,1,0:T(8,128)(2,1)S(1)}, bf16[3,128,256]{2,1,0:T(8,128)(2,1)S(1)}, u32[]{:S(2)}, u32[]{:S(2)}) %collective-permute-start.7) | collective-permute-done | bytes 196640 | tf_op jit(solution)/shard_map/ppermute | solution.py:260
  63.3 2.0 %shard_map.114 = (bf16[3,128,128]{2,1,0:T(8,128)(2,1)S(1)}, bf16[3,128,128]{2,1,0:T(8,128)(2,1)S(1)}, bf16[3,128,128]{2,1,0:T(8,128)(2,1)S(1)}, bf16[3,128,128]{2,1,0:T(8,128)(2,1)S(1)}) custom-call(bf16[128,512]{1,0:T(8,128)(2,1)S(1)} %fusion.refs_0_, bf16[3,128,256]{2,1,0:T(8,128)(2,1)S(1)} %get-tuple-element.29.refs_1_, ...), custom_call_target="tpu_custom_call" | custom-call | flops 335544320 | bytes 786432 | tf_op jit(solution)/shard_map/pallas_call | solution.py:181
  65.3 9.0 %collective-permute-start.12 = (bf16[3,128,128]{2,1,0:T(8,128)(2,1)S(1)}, bf16[3,128,128]{2,1,0:T(8,128)(2,1)S(1)}, u32[]{:S(2)}, u32[]{:S(2)}) collective-permute-start(bf16[3,128,128]{2,1,0:T(8,128)(2,1)S(1)} %get-tuple-element.38), channel_id=1, source_target_pairs={{0,1},{1,0},{2,3},{3,2},{4,5},{5,4},{6,7},{7,6},{8,9},{9,8},{10,11... | collective-permute-start | bytes 294920 | tf_op jit(solution)/shard_map/ppermute | solution.py:280
  74.6 2.0 %shard_map.113 = (bf16[3,128,128]{2,1,0:T(8,128)(2,1)S(1)}, bf16[3,128,128]{2,1,0:T(8,128)(2,1)S(1)}, bf16[3,128,128]{2,1,0:T(8,128)(2,1)S(1)}, bf16[3,128,128]{2,1,0:T(8,128)(2,1)S(1)}) custom-call(bf16[128,512]{1,0:T(8,128)(2,1)S(1)} %fusion.refs_0_, bf16[3,128,256]{2,1,0:T(8,128)(2,1)S(1)} %get-tuple-element.29.refs_1_, ...), custom_call_target="tpu_custom_call" | custom-call | flops 335544320 | bytes 786432 | tf_op jit(solution)/shard_map/pallas_call | solution.py:181
  77.3 2.0 %collective-permute-start.14 = (bf16[3,128,128]{2,1,0:T(8,128)(2,1)S(1)}, bf16[3,128,128]{2,1,0:T(8,128)(2,1)S(1)}, u32[]{:S(2)}, u32[]{:S(2)}) collective-permute-start(bf16[3,128,128]{2,1,0:T(8,128)(2,1)S(1)} %get-tuple-element.40), channel_id=1, source_target_pairs={{0,3},{1,2},{2,1},{3,0},{4,7},{5,6},{6,5},{7,4},{8,11},{9,10},{10,... | collective-permute-start | bytes 294920 | tf_op jit(solution)/shard_map/ppermute | solution.py:280
  79.3 0.9 collective-permute-start.9
  80.2 1.4 %collective-permute-start.10 = (bf16[3,128,128]{2,1,0:T(8,128)(2,1)S(1)}, bf16[3,128,128]{2,1,0:T(8,128)(2,1)S(1)}, u32[]{:S(2)}, u32[]{:S(2)}) collective-permute-start(bf16[3,128,128]{2,1,0:T(8,128)(2,1)S(1)} %get-tuple-element.35), channel_id=1, source_target_pairs={{0,2},{1,3},{2,0},{3,1},{4,6},{5,7},{6,4},{7,5},{8,10},{9,11},{10,... | collective-permute-start | bytes 294920 | tf_op jit(solution)/shard_map/ppermute | solution.py:280
  81.7 2.0 %collective-permute-start.11 = (bf16[3,128,128]{2,1,0:T(8,128)(2,1)S(1)}, bf16[3,128,128]{2,1,0:T(8,128)(2,1)S(1)}, u32[]{:S(2)}, u32[]{:S(2)}) collective-permute-start(bf16[3,128,128]{2,1,0:T(8,128)(2,1)S(1)} %get-tuple-element.36), channel_id=1, source_target_pairs={{0,3},{1,2},{2,1},{3,0},{4,7},{5,6},{6,5},{7,4},{8,11},{9,10},{10,... | collective-permute-start | bytes 294920 | tf_op jit(solution)/shard_map/ppermute | solution.py:280
  83.7 1.0 %shard_map.117 = (bf16[1,128,2048]{2,1,0:T(8,128)(2,1)}, bf16[1,128,2048]{2,1,0:T(8,128)(2,1)}, bf16[1,128,2048]{2,1,0:T(8,128)(2,1)}) custom-call(s32[1]{0:T(128)} %bitcast.here_ref.refs_0_, bf16[3,128,256]{2,1,0:T(8,128)(2,1)S(1)} %get-tuple-element.45.refs_1_, bf16[3,128,256]{2,1,0:T(8,128)(2,1)S(1)} %collective-permute-done.18.refs_2_, ...), custom_call_target="tpu_custom_call" | custom-call | bytes 1572864 | tf_op jit(solution)/shard_map/pallas_call | solution.py:227
  84.7 6.0 %collective-permute-done.13.refs_3_ = bf16[3,128,128]{2,1,0:T(8,128)(2,1)S(1)} collective-permute-done((bf16[3,128,128]{2,1,0:T(8,128)(2,1)S(1)}, bf16[3,128,128]{2,1,0:T(8,128)(2,1)S(1)}, u32[]{:S(2)}, u32[]{:S(2)}) %collective-permute-start.13) | collective-permute-done | bytes 98336 | tf_op jit(solution)/shard_map/ppermute | solution.py:280
  90.6 0.8 shard_map.118
  91.5 3.4 %collective-permute-done.10.refs_3_ = bf16[3,128,128]{2,1,0:T(8,128)(2,1)S(1)} collective-permute-done((bf16[3,128,128]{2,1,0:T(8,128)(2,1)S(1)}, bf16[3,128,128]{2,1,0:T(8,128)(2,1)S(1)}, u32[]{:S(2)}, u32[]{:S(2)}) %collective-permute-start.10) | collective-permute-done | bytes 98336 | tf_op jit(solution)/shard_map/ppermute | solution.py:280
  (40 shorter events, 5.7 us)
Async XLA Ops:
  0.6 25.5 %copy-start.3 = (bf16[1,128,2048]{2,1,0:T(8,128)(2,1)S(1)}, bf16[1,128,2048]{2,1,0:T(8,128)(2,1)}, u32[]{:S(2)}) copy-start(bf16[1,128,2048]{2,1,0:T(8,128)(2,1)} %refs_1_.3) | copy-start | bytes 1572868
  0.6 25.5 %copy-start.1 = (bf16[1,128,2048]{2,1,0:T(8,128)(2,1)S(1)}, bf16[1,128,2048]{2,1,0:T(8,128)(2,1)}, u32[]{:S(2)}) copy-start(bf16[1,128,2048]{2,1,0:T(8,128)(2,1)} %refs_0_.3) | copy-start | bytes 1572868
  0.7 1.1 %copy-start.6 = (bf16[1,64,3584]{2,1,0:T(8,128)(2,1)S(1)}, bf16[1,64,3584]{2,1,0:T(8,128)(2,1)}, u32[]{:S(2)}) copy-start(bf16[1,64,3584]{2,1,0:T(8,128)(2,1)} %hidden_ref.1) | copy-start | bytes 1376260
  1.8 1.0 %copy-start.7 = (bf16[1,64,3584]{2,1,0:T(8,128)(2,1)S(1)}, bf16[1,64,3584]{2,1,0:T(8,128)(2,1)}, u32[]{:S(2)}) copy-start(bf16[1,64,3584]{2,1,0:T(8,128)(2,1)} %cot_ref.1) | copy-start | bytes 1376260
  2.8 0.7 copy-start.8
  3.5 0.7 copy-start.9
  4.6 13.3 %collective-permute-start.1 = (bf16[32,3584]{1,0:T(8,128)(2,1)S(1)}, bf16[32,3584]{1,0:T(8,128)(2,1)S(1)}, u32[]{:S(2)}, u32[]{:S(2)}) collective-permute-start(bf16[32,3584]{1,0:T(8,128)(2,1)S(1)} %visual.1), channel_id=1, source_target_pairs={{0,2},{1,3},{2,0},{3,1},{4,6},{5,7},{6,4},{7,5},{8,10},{9,11},{10,... | collective-permute-start | bytes 688136 | tf_op jit(solution)/shard_map/ppermute | solution.py:116
  7.3 30.3 %collective-permute-start = (bf16[32,3584]{1,0:T(8,128)(2,1)S(1)}, bf16[32,3584]{1,0:T(8,128)(2,1)}, u32[]{:S(2)}, u32[]{:S(2)}) collective-permute-start(bf16[32,3584]{1,0:T(8,128)(2,1)S(1)} %visual.1), channel_id=1, source_target_pairs={{0,1},{1,0},{2,3},{3,2},{4,5},{5,4},{6,7},{7,6},{8,9},{9,8},{10,11... | collective-permute-start | bytes 688136 | tf_op jit(solution)/shard_map/ppermute | solution.py:116
  17.9 22.1 %collective-permute-start.2 = (bf16[32,3584]{1,0:T(8,128)(2,1)S(1)}, bf16[32,3584]{1,0:T(8,128)(2,1)}, u32[]{:S(2)}, u32[]{:S(2)}) collective-permute-start(bf16[32,3584]{1,0:T(8,128)(2,1)S(1)} %collective-permute-done.1), channel_id=1, source_target_pairs={{0,1},{1,0},{2,3},{3,2},{4,5},{5,4},{6,7},{7,6},{8,9},{9,8},{10,11... | collective-permute-start | bytes 688136 | tf_op jit(solution)/shard_map/ppermute | solution.py:116
  18.5 1.0 %copy-start = (bf16[1,128,2048]{2,1,0:T(8,128)(2,1)S(1)}, bf16[1,128,2048]{2,1,0:T(8,128)(2,1)}, u32[]{:S(2)}) copy-start(bf16[1,128,2048]{2,1,0:T(8,128)(2,1)} %refs_0_.3) | copy-start | bytes 1572868
  19.5 1.0 %copy-start.2 = (bf16[1,128,2048]{2,1,0:T(8,128)(2,1)S(1)}, bf16[1,128,2048]{2,1,0:T(8,128)(2,1)}, u32[]{:S(2)}) copy-start(bf16[1,128,2048]{2,1,0:T(8,128)(2,1)} %refs_1_.3) | copy-start | bytes 1572868
  20.6 1.0 %copy-start.4 = (bf16[1,128,2048]{2,1,0:T(8,128)(2,1)S(1)}, bf16[1,128,2048]{2,1,0:T(8,128)(2,1)}, u32[]{:S(2)}) copy-start(bf16[1,128,2048]{2,1,0:T(8,128)(2,1)} %refs_2_.3) | copy-start | bytes 1572868
  21.6 4.5 %copy-start.5 = (bf16[1,128,2048]{2,1,0:T(8,128)(2,1)S(1)}, bf16[1,128,2048]{2,1,0:T(8,128)(2,1)}, u32[]{:S(2)}) copy-start(bf16[1,128,2048]{2,1,0:T(8,128)(2,1)} %refs_2_.3) | copy-start | bytes 1572868
  21.9 15.3 %collective-permute-start.15 = (bf16[3,128,256]{2,1,0:T(8,128)(2,1)S(1)}, bf16[3,128,256]{2,1,0:T(8,128)(2,1)S(1)}, u32[]{:S(2)}, u32[]{:S(2)}) collective-permute-start(bf16[3,128,256]{2,1,0:T(8,128)(2,1)S(1)} %get-tuple-element.42), channel_id=1, source_target_pairs={{0,1},{1,0},{2,3},{3,2},{4,5},{5,4},{6,7},{7,6},{8,9},{9,8},{10,11... | collective-permute-start | bytes 589832 | tf_op jit(solution)/shard_map/ppermute | solution.py:260
  23.4 3.0 %collective-permute-start.3 = (f32[]{:T(128)}, f32[]{:T(128)}, u32[]{:S(2)}, u32[]{:S(2)}) collective-permute-start(f32[]{:T(128)} %bitcast.2), channel_id=1, source_target_pairs={{0,4},{4,0},{8,12},{12,8},{16,20},{20,16},{24,28},{28,24},{1,5},{5... | collective-permute-start | bytes 20 | tf_op jit(solution)/shard_map/ppermute | solution.py:105
  23.4 21.2 %collective-permute-start.16 = (bf16[3,128,256]{2,1,0:T(8,128)(2,1)S(1)}, bf16[3,128,256]{2,1,0:T(8,128)(2,1)S(1)}, u32[]{:S(2)}, u32[]{:S(2)}) collective-permute-start(bf16[3,128,256]{2,1,0:T(8,128)(2,1)S(1)} %get-tuple-element.43), channel_id=1, source_target_pairs={{0,2},{1,3},{2,0},{3,1},{4,6},{5,7},{6,4},{7,5},{8,10},{9,11},{10,... | collective-permute-start | bytes 589832 | tf_op jit(solution)/shard_map/ppermute | solution.py:260
  27.1 3.6 %collective-permute-start.4 = (f32[]{:T(128)}, f32[]{:T(128)}, u32[]{:S(2)}, u32[]{:S(2)}) collective-permute-start(f32[]{:T(128)} %add.9), channel_id=1, source_target_pairs={{0,8},{4,12},{8,0},{12,4},{16,24},{20,28},{24,16},{28,20},{1,9},{5... | collective-permute-start | bytes 20 | tf_op jit(solution)/shard_map/ppermute | solution.py:105
  31.3 3.6 %collective-permute-start.5 = (f32[]{:T(128)}, f32[]{:T(128)}, u32[]{:S(2)}, u32[]{:S(2)}) collective-permute-start(f32[]{:T(128)} %add.10), channel_id=1, source_target_pairs={{0,16},{4,20},{8,24},{12,28},{16,0},{20,4},{24,8},{28,12},{1,17},{... | collective-permute-start | bytes 20 | tf_op jit(solution)/shard_map/ppermute | solution.py:105
  34.9 9.7 %collective-permute-start.17 = (bf16[3,128,256]{2,1,0:T(8,128)(2,1)S(1)}, bf16[3,128,256]{2,1,0:T(8,128)(2,1)S(1)}, u32[]{:S(2)}, u32[]{:S(2)}) collective-permute-start(bf16[3,128,256]{2,1,0:T(8,128)(2,1)S(1)} %get-tuple-element.44), channel_id=1, source_target_pairs={{0,3},{1,2},{2,1},{3,0},{4,7},{5,6},{6,5},{7,4},{8,11},{9,10},{10,... | collective-permute-start | bytes 589832 | tf_op jit(solution)/shard_map/ppermute | solution.py:260
  37.2 22.4 %collective-permute-start.6 = (bf16[3,128,256]{2,1,0:T(8,128)(2,1)S(1)}, bf16[3,128,256]{2,1,0:T(8,128)(2,1)S(1)}, u32[]{:S(2)}, u32[]{:S(2)}) collective-permute-start(bf16[3,128,256]{2,1,0:T(8,128)(2,1)S(1)} %get-tuple-element.30), channel_id=1, source_target_pairs={{0,1},{1,0},{2,3},{3,2},{4,5},{5,4},{6,7},{7,6},{8,9},{9,8},{10,11... | collective-permute-start | bytes 589832 | tf_op jit(solution)/shard_map/ppermute | solution.py:260
  37.5 25.7 %collective-permute-start.7 = (bf16[3,128,256]{2,1,0:T(8,128)(2,1)S(1)}, bf16[3,128,256]{2,1,0:T(8,128)(2,1)S(1)}, u32[]{:S(2)}, u32[]{:S(2)}) collective-permute-start(bf16[3,128,256]{2,1,0:T(8,128)(2,1)S(1)} %get-tuple-element.31), channel_id=1, source_target_pairs={{0,2},{1,3},{2,0},{3,1},{4,6},{5,7},{6,4},{7,5},{8,10},{9,11},{10,... | collective-permute-start | bytes 589832 | tf_op jit(solution)/shard_map/ppermute | solution.py:260
  40.0 23.2 %collective-permute-start.8 = (bf16[3,128,256]{2,1,0:T(8,128)(2,1)S(1)}, bf16[3,128,256]{2,1,0:T(8,128)(2,1)S(1)}, u32[]{:S(2)}, u32[]{:S(2)}) collective-permute-start(bf16[3,128,256]{2,1,0:T(8,128)(2,1)S(1)} %get-tuple-element.32), channel_id=1, source_target_pairs={{0,3},{1,2},{2,1},{3,0},{4,7},{5,6},{6,5},{7,4},{8,11},{9,10},{10,... | collective-permute-start | bytes 589832 | tf_op jit(solution)/shard_map/ppermute | solution.py:260
  48.9 30.4 %collective-permute-start.18 = (bf16[3,128,256]{2,1,0:T(8,128)(2,1)S(1)}, bf16[3,128,256]{2,1,0:T(8,128)(2,1)S(1)}, u32[]{:S(2)}, u32[]{:S(2)}) collective-permute-start(bf16[3,128,256]{2,1,0:T(8,128)(2,1)S(1)} %get-tuple-element.46), channel_id=1, source_target_pairs={{0,1},{1,0},{2,3},{3,2},{4,5},{5,4},{6,7},{7,6},{8,9},{9,8},{10,11... | collective-permute-start | bytes 589832 | tf_op jit(solution)/shard_map/ppermute | solution.py:280
  59.6 20.6 %collective-permute-start.19 = (bf16[3,128,256]{2,1,0:T(8,128)(2,1)S(1)}, bf16[3,128,256]{2,1,0:T(8,128)(2,1)S(1)}, u32[]{:S(2)}, u32[]{:S(2)}) collective-permute-start(bf16[3,128,256]{2,1,0:T(8,128)(2,1)S(1)} %get-tuple-element.47), channel_id=1, source_target_pairs={{0,2},{1,3},{2,0},{3,1},{4,6},{5,7},{6,4},{7,5},{8,10},{9,11},{10,... | collective-permute-start | bytes 589832 | tf_op jit(solution)/shard_map/ppermute | solution.py:280
  59.6 22.1 %collective-permute-start.20 = (bf16[3,128,256]{2,1,0:T(8,128)(2,1)S(1)}, bf16[3,128,256]{2,1,0:T(8,128)(2,1)S(1)}, u32[]{:S(2)}, u32[]{:S(2)}) collective-permute-start(bf16[3,128,256]{2,1,0:T(8,128)(2,1)S(1)} %get-tuple-element.48), channel_id=1, source_target_pairs={{0,3},{1,2},{2,1},{3,0},{4,7},{5,6},{6,5},{7,4},{8,11},{9,10},{10,... | collective-permute-start | bytes 589832 | tf_op jit(solution)/shard_map/ppermute | solution.py:280
  65.3 12.0 %collective-permute-start.12 = (bf16[3,128,128]{2,1,0:T(8,128)(2,1)S(1)}, bf16[3,128,128]{2,1,0:T(8,128)(2,1)S(1)}, u32[]{:S(2)}, u32[]{:S(2)}) collective-permute-start(bf16[3,128,128]{2,1,0:T(8,128)(2,1)S(1)} %get-tuple-element.38), channel_id=1, source_target_pairs={{0,1},{1,0},{2,3},{3,2},{4,5},{5,4},{6,7},{7,6},{8,9},{9,8},{10,11... | collective-permute-start | bytes 294920 | tf_op jit(solution)/shard_map/ppermute | solution.py:280
  74.3 16.3 %collective-permute-start.13 = (bf16[3,128,128]{2,1,0:T(8,128)(2,1)S(1)}, bf16[3,128,128]{2,1,0:T(8,128)(2,1)S(1)}, u32[]{:S(2)}, u32[]{:S(2)}) collective-permute-start(bf16[3,128,128]{2,1,0:T(8,128)(2,1)S(1)} %get-tuple-element.39), channel_id=1, source_target_pairs={{0,2},{1,3},{2,0},{3,1},{4,6},{5,7},{6,4},{7,5},{8,10},{9,11},{10,... | collective-permute-start | bytes 294920 | tf_op jit(solution)/shard_map/ppermute | solution.py:280
  77.3 13.4 %collective-permute-start.14 = (bf16[3,128,128]{2,1,0:T(8,128)(2,1)S(1)}, bf16[3,128,128]{2,1,0:T(8,128)(2,1)S(1)}, u32[]{:S(2)}, u32[]{:S(2)}) collective-permute-start(bf16[3,128,128]{2,1,0:T(8,128)(2,1)S(1)} %get-tuple-element.40), channel_id=1, source_target_pairs={{0,3},{1,2},{2,1},{3,0},{4,7},{5,6},{6,5},{7,4},{8,11},{9,10},{10,... | collective-permute-start | bytes 294920 | tf_op jit(solution)/shard_map/ppermute | solution.py:280
  79.3 12.2 %collective-permute-start.9 = (bf16[3,128,128]{2,1,0:T(8,128)(2,1)S(1)}, bf16[3,128,128]{2,1,0:T(8,128)(2,1)S(1)}, u32[]{:S(2)}, u32[]{:S(2)}) collective-permute-start(bf16[3,128,128]{2,1,0:T(8,128)(2,1)S(1)} %get-tuple-element.34), channel_id=1, source_target_pairs={{0,1},{1,0},{2,3},{3,2},{4,5},{5,4},{6,7},{7,6},{8,9},{9,8},{10,11... | collective-permute-start | bytes 294920 | tf_op jit(solution)/shard_map/ppermute | solution.py:280
  80.2 14.6 %collective-permute-start.10 = (bf16[3,128,128]{2,1,0:T(8,128)(2,1)S(1)}, bf16[3,128,128]{2,1,0:T(8,128)(2,1)S(1)}, u32[]{:S(2)}, u32[]{:S(2)}) collective-permute-start(bf16[3,128,128]{2,1,0:T(8,128)(2,1)S(1)} %get-tuple-element.35), channel_id=1, source_target_pairs={{0,2},{1,3},{2,0},{3,1},{4,6},{5,7},{6,4},{7,5},{8,10},{9,11},{10,... | collective-permute-start | bytes 294920 | tf_op jit(solution)/shard_map/ppermute | solution.py:280
  81.7 13.2 %collective-permute-start.11 = (bf16[3,128,128]{2,1,0:T(8,128)(2,1)S(1)}, bf16[3,128,128]{2,1,0:T(8,128)(2,1)S(1)}, u32[]{:S(2)}, u32[]{:S(2)}) collective-permute-start(bf16[3,128,128]{2,1,0:T(8,128)(2,1)S(1)} %get-tuple-element.36), channel_id=1, source_target_pairs={{0,3},{1,2},{2,1},{3,0},{4,7},{5,6},{6,5},{7,4},{8,11},{9,10},{10,... | collective-permute-start | bytes 294920 | tf_op jit(solution)/shard_map/ppermute | solution.py:280

commit v4 on v3

--- a/solution.py
+++ b/solution.py
@@ -10,18 +10,35 @@
 
 HD = 128
 GW = 64
-IN_HEADS = (2, 2)
+IN_HEADS = (2, 1, 1)
 OUT_HEADS = (2, 1, 1)
 
 
-def visual_kernel(here_ref, pos_ref, hidden_ref, cot_ref, gain_ref, out_ref):
-    rows = hidden_ref.shape[1]
+def in_hbm(array):
+    return pltpu.with_memory_space_constraint(array, pltpu.HBM)
+
+
+def visual_kernel(here_ref, pos_ref, gain_ref, hidden_hbm, cot_hbm, out_ref, held, sems):
+    rows = hidden_hbm.shape[1]
     picked = out_ref.shape[0]
+    pieces = sems.shape[1]
+    piece = rows // pieces
+    copies = []
+    for i, source in enumerate((hidden_hbm, cot_hbm)):
+        for j in range(pieces):
+            at = pl.ds(j * piece, piece)
+            copies.append(
+                pltpu.make_async_copy(source.at[0, at], held.at[i, at], sems.at[i, j])
+            )
+    for copy in copies:
+        copy.start()
     row = lax.broadcasted_iota(jnp.int32, (rows, picked), 0) + here_ref[0] * rows
     pick = jnp.where(row == pos_ref[...], 1.0, 0.0).astype(jnp.bfloat16)
     first_both = (((0,), (0,)), ((), ()))
-    hidden = lax.dot_general(pick, hidden_ref[0], first_both, preferred_element_type=jnp.float32)
-    cot = lax.dot_general(pick, cot_ref[0], first_both, preferred_element_type=jnp.float32)
+    for copy in copies:
+        copy.wait()
+    hidden = lax.dot_general(pick, held[0], first_both, preferred_element_type=jnp.float32)
+    cot = lax.dot_general(pick, held[1], first_both, preferred_element_type=jnp.float32)
     lanes = gain_ref.shape[1]
     scaled_cot = jnp.concatenate(
         [
@@ -39,18 +56,25 @@
 
 def visual_grads(here, positions, hidden, cotangent, gain):
     picked, depth = positions.shape[1], hidden.shape[2]
+    rows = hidden.shape[1]
+    pieces = 8 if rows % 64 == 0 else 1
     vmem = pl.BlockSpec(memory_space=pltpu.VMEM)
+    hbm = pl.BlockSpec(memory_space=pltpu.HBM)
     return pl.pallas_call(
         visual_kernel,
-        in_specs=[pl.BlockSpec(memory_space=pltpu.SMEM)] + [vmem] * 4,
+        in_specs=[pl.BlockSpec(memory_space=pltpu.SMEM), vmem, vmem, hbm, hbm],
         out_specs=vmem,
+        scratch_shapes=[
+            pltpu.VMEM((2, rows, depth), jnp.bfloat16),
+            pltpu.SemaphoreType.DMA((2, pieces)),
+        ],
         out_shape=jax.ShapeDtypeStruct((picked, depth), jnp.bfloat16),
         cost_estimate=pl.CostEstimate(
             flops=4 * picked * hidden.size, bytes_accessed=4 * hidden.size, transcendentals=0
         ),
         compiler_params=pltpu.CompilerParams(vmem_limit_bytes=(8 << 20) + 12 * hidden.size),
         name="visual",
-    )(here, positions, hidden, cotangent, gain.reshape(-1, HD))
+    )(here, positions, gain.reshape(-1, HD), in_hbm(hidden), in_hbm(cotangent))
 
 
 def pack_kernel(count, first, here_ref, *refs):
@@ -77,7 +101,7 @@
     return pl.pallas_call(
         functools.partial(pack_kernel, count, first),
         in_specs=[pl.BlockSpec(memory_space=pltpu.SMEM)]
-        + [pl.BlockSpec(memory_space=pl.ANY)] * 3,
+        + [pl.BlockSpec(memory_space=pltpu.HBM)] * 3,
         out_specs=[pl.BlockSpec(memory_space=pltpu.VMEM)] * count,
         out_shape=[jax.ShapeDtypeStruct((3, rows, width), jnp.bfloat16)] * count,
         scratch_shapes=[pltpu.SemaphoreType.DMA((3 * count,))],
@@ -87,7 +111,7 @@
         compiler_params=pltpu.CompilerParams(
             vmem_limit_bytes=(1 << 20) + 6 * count * rows * width
         ),
-    )(here, *sources)
+    )(here, *map(in_hbm, sources))
 
 
 def split(heads, parts):

time: 97.6 us -> 97.3 us (level)
  the two profiles are of different devices: /device:TPU:2 before, /device:TPU:0 now
where the time goes in v4:
time: 97.3 us; the launch traced here: 96.7 us
  starting transfers between devices  49 us (50%)
  waiting for transfers between devices  24.3 us (25%)
  Pallas kernels  16 us (16%)
  between operations  3.37 us (3%)
  matrix products  2.68 us (3%)
  local copies, waits for them, and re-layouts  1.37 us (1%)
    ppermute x9, starting transfers between devices, work(): lax.ppermute(packed[k], 'tensor', partners(count, k))  18.5 us
    ppermute x9, starting transfers between devices, work(): lax.ppermute(grads[k], 'tensor', partners(count, k))  18.4 us
    ppermute x3, waiting for transfers between devices, gathered(): held[k ^ step] = lax.ppermute(held[k], axis, partners(size, step))  9.04 us
    pallas_call x3, Pallas kernels, attend(): pl.pallas_call(functools.partial(attend_kernel, count, HD ** (-0.5), chun...  8.19 us
    ppermute x9, waiting for transfers between devices, work(): lax.ppermute(packed[k], 'tensor', partners(count, k))  8.02 us
    ppermute x3, starting transfers between devices, gathered(): held[k ^ step] = lax.ppermute(held[k], axis, partners(size, step))  6.33 us
    ppermute x9, waiting for transfers between devices, work(): lax.ppermute(grads[k], 'tensor', partners(count, k))  5.85 us
    ppermute x3, starting transfers between devices, total_over(): value = value + lax.ppermute(value, axis, partners(size, step))  5.75 us
  transfers between devices with their start and end apart: 24, of which 6 were waited for; matrix products, arithmetic and copies ran while one was open for 3% of the time, Pallas kernels for 14%

profile of v4, /device:TPU:0, one launch (start us, length us, event | category | flops | bytes accessed | tf_op | source)
XLA Modules:
  0.0 96.7 jit_solution(3739296179069987724)
XLA Ops:
  2.0 1.8 %visual.1 = bf16[32,3584]{1,0:T(8,128)(2,1)S(1)} custom-call(s32[1]{0:T(128)} %bitcast.here_ref.refs_0_, s32[1,32]{1,0:T(1,128)S(1)} %copy-done.1, f32[28,128]{1,0:T(8,128)S(1)} %bitcast.6, bf16[1,64,3584]{2,1,0:T(8,128)(2,1)} %hidden_hbm.1, bf16[1,64,3584]{2,1,0:T(8,128)(2,1)} %cot_hbm.1), custom_call_target="tpu_custom_call" | custom-call | flops 29360128 | bytes 917504 | tf_op jit(solution)/shard_map/visual/pallas_call | solution.py:63
  3.8 4.1 %collective-permute-start.1 = (bf16[32,3584]{1,0:T(8,128)(2,1)S(1)}, bf16[32,3584]{1,0:T(8,128)(2,1)S(1)}, u32[]{:S(2)}, u32[]{:S(2)}) collective-permute-start(bf16[32,3584]{1,0:T(8,128)(2,1)S(1)} %visual.1), channel_id=1, source_target_pairs={{0,2},{1,3},{2,0},{3,1},{4,6},{5,7},{6,4},{7,5},{8,10},{9,11},{10,... | collective-permute-start | bytes 688136 | tf_op jit(solution)/shard_map/ppermute | solution.py:140
  7.9 1.6 %collective-permute-start = (bf16[32,3584]{1,0:T(8,128)(2,1)S(1)}, bf16[32,3584]{1,0:T(8,128)(2,1)S(1)}, u32[]{:S(2)}, u32[]{:S(2)}) collective-permute-start(bf16[32,3584]{1,0:T(8,128)(2,1)S(1)} %visual.1), channel_id=1, source_target_pairs={{0,1},{1,0},{2,3},{3,2},{4,5},{5,4},{6,7},{7,6},{8,9},{9,8},{10,11... | collective-permute-start | bytes 688136 | tf_op jit(solution)/shard_map/ppermute | solution.py:140
  9.5 9.0 %collective-permute-done.1 = bf16[32,3584]{1,0:T(8,128)(2,1)S(1)} collective-permute-done((bf16[32,3584]{1,0:T(8,128)(2,1)S(1)}, bf16[32,3584]{1,0:T(8,128)(2,1)S(1)}, u32[]{:S(2)}, u32[]{:S(2)}) %collective-permute-start.1) | collective-permute-done | bytes 229408 | tf_op jit(solution)/shard_map/ppermute | solution.py:140
  19.1 1.3 %shard_map.116 = (bf16[3,128,256]{2,1,0:T(8,128)(2,1)S(1)}, bf16[3,128,256]{2,1,0:T(8,128)(2,1)S(1)}, bf16[3,128,256]{2,1,0:T(8,128)(2,1)S(1)}, bf16[3,128,256]{2,1,0:T(8,128)(2,1)S(1)}) custom-call(s32[1]{0:T(128)} %bitcast.here_ref.refs_0_, bf16[1,128,2048]{2,1,0:T(8,128)(2,1)} %refs_0_.5, bf16[1,128,2048]{2,1,0:T(8,128)(2,1)} %refs_1_.5, ...), custom_call_target="tpu_custom_call" | custom-call | bytes 1572864 | tf_op jit(solution)/shard_map/pallas_call | solution.py:101
  20.4 1.5 %collective-permute-start.18 = (bf16[3,128,256]{2,1,0:T(8,128)(2,1)S(1)}, bf16[3,128,256]{2,1,0:T(8,128)(2,1)S(1)}, u32[]{:S(2)}, u32[]{:S(2)}) collective-permute-start(bf16[3,128,256]{2,1,0:T(8,128)(2,1)S(1)} %get-tuple-element.50), channel_id=1, source_target_pairs={{0,1},{1,0},{2,3},{3,2},{4,5},{5,4},{6,7},{7,6},{8,9},{9,8},{10,11... | collective-permute-start | bytes 589832 | tf_op jit(solution)/shard_map/ppermute | solution.py:284
  21.9 2.1 %collective-permute-start.19 = (bf16[3,128,256]{2,1,0:T(8,128)(2,1)S(1)}, bf16[3,128,256]{2,1,0:T(8,128)(2,1)S(1)}, u32[]{:S(2)}, u32[]{:S(2)}) collective-permute-start(bf16[3,128,256]{2,1,0:T(8,128)(2,1)S(1)} %get-tuple-element.51), channel_id=1, source_target_pairs={{0,2},{1,3},{2,0},{3,1},{4,6},{5,7},{6,4},{7,5},{8,10},{9,11},{10,... | collective-permute-start | bytes 589832 | tf_op jit(solution)/shard_map/ppermute | solution.py:284
  24.7 1.1 %shard_map.114 = (bf16[3,128,128]{2,1,0:T(8,128)(2,1)S(1)}, bf16[3,128,128]{2,1,0:T(8,128)(2,1)S(1)}, bf16[3,128,128]{2,1,0:T(8,128)(2,1)S(1)}, bf16[3,128,128]{2,1,0:T(8,128)(2,1)S(1)}) custom-call(s32[1]{0:T(128)} %bitcast.here_ref.refs_0_, bf16[1,128,2048]{2,1,0:T(8,128)(2,1)} %refs_0_.5, bf16[1,128,2048]{2,1,0:T(8,128)(2,1)} %refs_1_.5, ...), custom_call_target="tpu_custom_call" | custom-call | bytes 786432 | tf_op jit(solution)/shard_map/pallas_call | solution.py:101
  25.7 1.1 %shard_map.112 = (bf16[3,128,128]{2,1,0:T(8,128)(2,1)S(1)}, bf16[3,128,128]{2,1,0:T(8,128)(2,1)S(1)}, bf16[3,128,128]{2,1,0:T(8,128)(2,1)S(1)}, bf16[3,128,128]{2,1,0:T(8,128)(2,1)S(1)}) custom-call(s32[1]{0:T(128)} %bitcast.here_ref.refs_0_, bf16[1,128,2048]{2,1,0:T(8,128)(2,1)} %refs_0_.5, bf16[1,128,2048]{2,1,0:T(8,128)(2,1)} %refs_1_.5, ...), custom_call_target="tpu_custom_call" | custom-call | bytes 786432 | tf_op jit(solution)/shard_map/pallas_call | solution.py:101
  27.4 2.9 %collective-permute-start.4 = (f32[]{:T(128)}, f32[]{:T(128)}, u32[]{:S(2)}, u32[]{:S(2)}) collective-permute-start(f32[]{:T(128)} %add.9), channel_id=1, source_target_pairs={{0,8},{4,12},{8,0},{12,4},{16,24},{20,28},{24,16},{28,20},{1,9},{5... | collective-permute-start | bytes 20 | tf_op jit(solution)/shard_map/ppermute | solution.py:129
  30.3 0.7 collective-permute-done.4
  31.6 2.9 %collective-permute-start.5 = (f32[]{:T(128)}, f32[]{:T(128)}, u32[]{:S(2)}, u32[]{:S(2)}) collective-permute-start(f32[]{:T(128)} %add.10), channel_id=1, source_target_pairs={{0,16},{4,20},{8,24},{12,28},{16,0},{20,4},{24,8},{28,12},{1,17},{... | collective-permute-start | bytes 20 | tf_op jit(solution)/shard_map/ppermute | solution.py:129
  35.2 1.3 %collective-permute-start.20 = (bf16[3,128,256]{2,1,0:T(8,128)(2,1)S(1)}, bf16[3,128,256]{2,1,0:T(8,128)(2,1)S(1)}, u32[]{:S(2)}, u32[]{:S(2)}) collective-permute-start(bf16[3,128,256]{2,1,0:T(8,128)(2,1)S(1)} %get-tuple-element.52), channel_id=1, source_target_pairs={{0,3},{1,2},{2,1},{3,0},{4,7},{5,6},{6,5},{7,4},{8,11},{9,10},{10,... | collective-permute-start | bytes 589832 | tf_op jit(solution)/shard_map/ppermute | solution.py:284
  37.8 2.5 %collective-permute-start.13 = (bf16[3,128,128]{2,1,0:T(8,128)(2,1)S(1)}, bf16[3,128,128]{2,1,0:T(8,128)(2,1)S(1)}, u32[]{:S(2)}, u32[]{:S(2)}) collective-permute-start(bf16[3,128,128]{2,1,0:T(8,128)(2,1)S(1)} %get-tuple-element.43), channel_id=1, source_target_pairs={{0,2},{1,3},{2,0},{3,1},{4,6},{5,7},{6,4},{7,5},{8,10},{9,11},{10,... | collective-permute-start | bytes 294920 | tf_op jit(solution)/shard_map/ppermute | solution.py:284
  40.3 1.3 %collective-permute-start.14 = (bf16[3,128,128]{2,1,0:T(8,128)(2,1)S(1)}, bf16[3,128,128]{2,1,0:T(8,128)(2,1)S(1)}, u32[]{:S(2)}, u32[]{:S(2)}) collective-permute-start(bf16[3,128,128]{2,1,0:T(8,128)(2,1)S(1)} %get-tuple-element.44), channel_id=1, source_target_pairs={{0,3},{1,2},{2,1},{3,0},{4,7},{5,6},{6,5},{7,4},{8,11},{9,10},{10,... | collective-permute-start | bytes 294920 | tf_op jit(solution)/shard_map/ppermute | solution.py:284
  41.6 2.7 %fusion.refs_0_ = bf16[128,512]{1,0:T(8,128)(2,1)S(1)} fusion(bf16[3584,512]{1,0:T(8,128)(2,1)} %param.14, bf16[32,3584]{1,0:T(8,128)(2,1)S(1)} %collective-permute-done.2, bf16[32,3584]{1,0:T(8,128)(2,1)S(1)} %collective-permute-done.1, bf16[32,3584]{1,0:T(8,128)(2,1)S(1)} %collective-permute-done, bf16[32,3584]{1,0:T(8,128)(2,1)S(1)} %visual.1, f32[]{:T(128)S(6)} %div.3), kind=kOutput, calls=%fused_computation.1 | convolution fusion | flops 473563136 | bytes 4718596 | tf_op jit(solution)/shard_map/dot_general | solution.py:292
  44.8 7.9 %collective-permute-start.7 = (bf16[3,128,128]{2,1,0:T(8,128)(2,1)S(1)}, bf16[3,128,128]{2,1,0:T(8,128)(2,1)S(1)}, u32[]{:S(2)}, u32[]{:S(2)}) collective-permute-start(bf16[3,128,128]{2,1,0:T(8,128)(2,1)S(1)} %get-tuple-element.35), channel_id=1, source_target_pairs={{0,2},{1,3},{2,0},{3,1},{4,6},{5,7},{6,4},{7,5},{8,10},{9,11},{10,... | collective-permute-start | bytes 294920 | tf_op jit(solution)/shard_map/ppermute | solution.py:284
  52.7 4.3 %shard_map.117 = (bf16[3,128,256]{2,1,0:T(8,128)(2,1)S(1)}, bf16[3,128,256]{2,1,0:T(8,128)(2,1)S(1)}, bf16[3,128,256]{2,1,0:T(8,128)(2,1)S(1)}, bf16[3,128,256]{2,1,0:T(8,128)(2,1)S(1)}) custom-call(bf16[128,512]{1,0:T(8,128)(2,1)S(1)} %fusion.refs_0_, bf16[3,128,256]{2,1,0:T(8,128)(2,1)S(1)} %get-tuple-element.49.refs_1_, ...), custom_call_target="tpu_custom_call" | custom-call | flops 671088640 | bytes 1572864 | tf_op jit(solution)/shard_map/pallas_call | solution.py:205
  57.1 1.7 %collective-permute-start.22 = (bf16[3,128,256]{2,1,0:T(8,128)(2,1)S(1)}, bf16[3,128,256]{2,1,0:T(8,128)(2,1)S(1)}, u32[]{:S(2)}, u32[]{:S(2)}) collective-permute-start(bf16[3,128,256]{2,1,0:T(8,128)(2,1)S(1)} %get-tuple-element.55), channel_id=1, source_target_pairs={{0,2},{1,3},{2,0},{3,1},{4,6},{5,7},{6,4},{7,5},{8,10},{9,11},{10,... | collective-permute-start | bytes 589832 | tf_op jit(solution)/shard_map/ppermute | solution.py:304
  58.8 2.7 %collective-permute-start.23 = (bf16[3,128,256]{2,1,0:T(8,128)(2,1)S(1)}, bf16[3,128,256]{2,1,0:T(8,128)(2,1)S(1)}, u32[]{:S(2)}, u32[]{:S(2)}) collective-permute-start(bf16[3,128,256]{2,1,0:T(8,128)(2,1)S(1)} %get-tuple-element.56), channel_id=1, source_target_pairs={{0,3},{1,2},{2,1},{3,0},{4,7},{5,6},{6,5},{7,4},{8,11},{9,10},{10,... | collective-permute-start | bytes 589832 | tf_op jit(solution)/shard_map/ppermute | solution.py:304
  61.4 1.2 %collective-permute-start.8 = (bf16[3,128,128]{2,1,0:T(8,128)(2,1)S(1)}, bf16[3,128,128]{2,1,0:T(8,128)(2,1)S(1)}, u32[]{:S(2)}, u32[]{:S(2)}) collective-permute-start(bf16[3,128,128]{2,1,0:T(8,128)(2,1)S(1)} %get-tuple-element.36), channel_id=1, source_target_pairs={{0,3},{1,2},{2,1},{3,0},{4,7},{5,6},{6,5},{7,4},{8,11},{9,10},{10,... | collective-permute-start | bytes 294920 | tf_op jit(solution)/shard_map/ppermute | solution.py:284
  62.6 2.0 %shard_map.115 = (bf16[3,128,128]{2,1,0:T(8,128)(2,1)S(1)}, bf16[3,128,128]{2,1,0:T(8,128)(2,1)S(1)}, bf16[3,128,128]{2,1,0:T(8,128)(2,1)S(1)}, bf16[3,128,128]{2,1,0:T(8,128)(2,1)S(1)}) custom-call(bf16[128,512]{1,0:T(8,128)(2,1)S(1)} %fusion.refs_0_, bf16[3,128,128]{2,1,0:T(8,128)(2,1)S(1)} %get-tuple-element.41.refs_1_, ...), custom_call_target="tpu_custom_call" | custom-call | flops 335544320 | bytes 786432 | tf_op jit(solution)/shard_map/pallas_call | solution.py:205
  64.7 7.6 %collective-permute-done.8.refs_4_ = bf16[3,128,128]{2,1,0:T(8,128)(2,1)S(1)} collective-permute-done((bf16[3,128,128]{2,1,0:T(8,128)(2,1)S(1)}, bf16[3,128,128]{2,1,0:T(8,128)(2,1)S(1)}, u32[]{:S(2)}, u32[]{:S(2)}) %collective-permute-start.8) | collective-permute-done | bytes 98336 | tf_op jit(solution)/shard_map/ppermute | solution.py:284
  72.3 7.7 %collective-permute-start.16 = (bf16[3,128,128]{2,1,0:T(8,128)(2,1)S(1)}, bf16[3,128,128]{2,1,0:T(8,128)(2,1)S(1)}, u32[]{:S(2)}, u32[]{:S(2)}) collective-permute-start(bf16[3,128,128]{2,1,0:T(8,128)(2,1)S(1)} %get-tuple-element.47), channel_id=1, source_target_pairs={{0,2},{1,3},{2,0},{3,1},{4,6},{5,7},{6,4},{7,5},{8,10},{9,11},{10,... | collective-permute-start | bytes 294920 | tf_op jit(solution)/shard_map/ppermute | solution.py:304
  80.0 2.0 %shard_map.113 = (bf16[3,128,128]{2,1,0:T(8,128)(2,1)S(1)}, bf16[3,128,128]{2,1,0:T(8,128)(2,1)S(1)}, bf16[3,128,128]{2,1,0:T(8,128)(2,1)S(1)}, bf16[3,128,128]{2,1,0:T(8,128)(2,1)S(1)}) custom-call(bf16[128,512]{1,0:T(8,128)(2,1)S(1)} %fusion.refs_0_, bf16[3,128,128]{2,1,0:T(8,128)(2,1)S(1)} %get-tuple-element.33.refs_1_, ...), custom_call_target="tpu_custom_call" | custom-call | flops 335544320 | bytes 786432 | tf_op jit(solution)/shard_map/pallas_call | solution.py:205
  82.0 2.7 %collective-permute-start.17 = (bf16[3,128,128]{2,1,0:T(8,128)(2,1)S(1)}, bf16[3,128,128]{2,1,0:T(8,128)(2,1)S(1)}, u32[]{:S(2)}, u32[]{:S(2)}) collective-permute-start(bf16[3,128,128]{2,1,0:T(8,128)(2,1)S(1)} %get-tuple-element.48), channel_id=1, source_target_pairs={{0,3},{1,2},{2,1},{3,0},{4,7},{5,6},{6,5},{7,4},{8,11},{9,10},{10,... | collective-permute-start | bytes 294920 | tf_op jit(solution)/shard_map/ppermute | solution.py:304
  84.7 1.2 %collective-permute-start.11 = (bf16[3,128,128]{2,1,0:T(8,128)(2,1)S(1)}, bf16[3,128,128]{2,1,0:T(8,128)(2,1)S(1)}, u32[]{:S(2)}, u32[]{:S(2)}) collective-permute-start(bf16[3,128,128]{2,1,0:T(8,128)(2,1)S(1)} %get-tuple-element.40), channel_id=1, source_target_pairs={{0,3},{1,2},{2,1},{3,0},{4,7},{5,6},{6,5},{7,4},{8,11},{9,10},{10,... | collective-permute-start | bytes 294920 | tf_op jit(solution)/shard_map/ppermute | solution.py:304
  86.0 2.3 %collective-permute-start.9 = (bf16[3,128,128]{2,1,0:T(8,128)(2,1)S(1)}, bf16[3,128,128]{2,1,0:T(8,128)(2,1)S(1)}, u32[]{:S(2)}, u32[]{:S(2)}) collective-permute-start(bf16[3,128,128]{2,1,0:T(8,128)(2,1)S(1)} %get-tuple-element.38), channel_id=1, source_target_pairs={{0,1},{1,0},{2,3},{3,2},{4,5},{5,4},{6,7},{7,6},{8,9},{9,8},{10,11... | collective-permute-start | bytes 294920 | tf_op jit(solution)/shard_map/ppermute | solution.py:304
  88.2 1.0 shard_map.118
  89.2 0.8 shard_map.119
  90.1 5.8 %collective-permute-done.10.refs_3_ = bf16[3,128,128]{2,1,0:T(8,128)(2,1)S(1)} collective-permute-done((bf16[3,128,128]{2,1,0:T(8,128)(2,1)S(1)}, bf16[3,128,128]{2,1,0:T(8,128)(2,1)S(1)}, u32[]{:S(2)}, u32[]{:S(2)}) %collective-permute-start.10) | collective-permute-done | bytes 98336 | tf_op jit(solution)/shard_map/ppermute | solution.py:304
  95.9 0.8 shard_map.120
  (31 shorter events, 3.9 us)
Async XLA Ops:
  0.6 0.7 copy-start
  1.4 0.7 copy-start.1
  3.8 14.7 %collective-permute-start.1 = (bf16[32,3584]{1,0:T(8,128)(2,1)S(1)}, bf16[32,3584]{1,0:T(8,128)(2,1)S(1)}, u32[]{:S(2)}, u32[]{:S(2)}) collective-permute-start(bf16[32,3584]{1,0:T(8,128)(2,1)S(1)} %visual.1), channel_id=1, source_target_pairs={{0,2},{1,3},{2,0},{3,1},{4,6},{5,7},{6,4},{7,5},{8,10},{9,11},{10,... | collective-permute-start | bytes 688136 | tf_op jit(solution)/shard_map/ppermute | solution.py:140
  7.9 29.9 %collective-permute-start = (bf16[32,3584]{1,0:T(8,128)(2,1)S(1)}, bf16[32,3584]{1,0:T(8,128)(2,1)S(1)}, u32[]{:S(2)}, u32[]{:S(2)}) collective-permute-start(bf16[32,3584]{1,0:T(8,128)(2,1)S(1)} %visual.1), channel_id=1, source_target_pairs={{0,1},{1,0},{2,3},{3,2},{4,5},{5,4},{6,7},{7,6},{8,9},{9,8},{10,11... | collective-permute-start | bytes 688136 | tf_op jit(solution)/shard_map/ppermute | solution.py:140
  18.5 21.8 %collective-permute-start.2 = (bf16[32,3584]{1,0:T(8,128)(2,1)S(1)}, bf16[32,3584]{1,0:T(8,128)(2,1)S(1)}, u32[]{:S(2)}, u32[]{:S(2)}) collective-permute-start(bf16[32,3584]{1,0:T(8,128)(2,1)S(1)} %collective-permute-done.1), channel_id=1, source_target_pairs={{0,1},{1,0},{2,3},{3,2},{4,5},{5,4},{6,7},{7,6},{8,9},{9,8},{10,11... | collective-permute-start | bytes 688136 | tf_op jit(solution)/shard_map/ppermute | solution.py:140
  20.4 16.8 %collective-permute-start.18 = (bf16[3,128,256]{2,1,0:T(8,128)(2,1)S(1)}, bf16[3,128,256]{2,1,0:T(8,128)(2,1)S(1)}, u32[]{:S(2)}, u32[]{:S(2)}) collective-permute-start(bf16[3,128,256]{2,1,0:T(8,128)(2,1)S(1)} %get-tuple-element.50), channel_id=1, source_target_pairs={{0,1},{1,0},{2,3},{3,2},{4,5},{5,4},{6,7},{7,6},{8,9},{9,8},{10,11... | collective-permute-start | bytes 589832 | tf_op jit(solution)/shard_map/ppermute | solution.py:284
  21.9 4.9 %collective-permute-start.3 = (f32[]{:T(128)}, f32[]{:T(128)}, u32[]{:S(2)}, u32[]{:S(2)}) collective-permute-start(f32[]{:T(128)} %bitcast.2), channel_id=1, source_target_pairs={{0,4},{4,0},{8,12},{12,8},{16,20},{20,16},{24,28},{28,24},{1,5},{5... | collective-permute-start | bytes 20 | tf_op jit(solution)/shard_map/ppermute | solution.py:129
  21.9 22.4 %collective-permute-start.19 = (bf16[3,128,256]{2,1,0:T(8,128)(2,1)S(1)}, bf16[3,128,256]{2,1,0:T(8,128)(2,1)S(1)}, u32[]{:S(2)}, u32[]{:S(2)}) collective-permute-start(bf16[3,128,256]{2,1,0:T(8,128)(2,1)S(1)} %get-tuple-element.51), channel_id=1, source_target_pairs={{0,2},{1,3},{2,0},{3,1},{4,6},{5,7},{6,4},{7,5},{8,10},{9,11},{10,... | collective-permute-start | bytes 589832 | tf_op jit(solution)/shard_map/ppermute | solution.py:284
  27.4 3.6 %collective-permute-start.4 = (f32[]{:T(128)}, f32[]{:T(128)}, u32[]{:S(2)}, u32[]{:S(2)}) collective-permute-start(f32[]{:T(128)} %add.9), channel_id=1, source_target_pairs={{0,8},{4,12},{8,0},{12,4},{16,24},{20,28},{24,16},{28,20},{1,9},{5... | collective-permute-start | bytes 20 | tf_op jit(solution)/shard_map/ppermute | solution.py:129
  31.6 3.6 %collective-permute-start.5 = (f32[]{:T(128)}, f32[]{:T(128)}, u32[]{:S(2)}, u32[]{:S(2)}) collective-permute-start(f32[]{:T(128)} %add.10), channel_id=1, source_target_pairs={{0,16},{4,20},{8,24},{12,28},{16,0},{20,4},{24,8},{28,12},{1,17},{... | collective-permute-start | bytes 20 | tf_op jit(solution)/shard_map/ppermute | solution.py:129
  35.2 9.6 %collective-permute-start.20 = (bf16[3,128,256]{2,1,0:T(8,128)(2,1)S(1)}, bf16[3,128,256]{2,1,0:T(8,128)(2,1)S(1)}, u32[]{:S(2)}, u32[]{:S(2)}) collective-permute-start(bf16[3,128,256]{2,1,0:T(8,128)(2,1)S(1)} %get-tuple-element.52), channel_id=1, source_target_pairs={{0,3},{1,2},{2,1},{3,0},{4,7},{5,6},{6,5},{7,4},{8,11},{9,10},{10,... | collective-permute-start | bytes 589832 | tf_op jit(solution)/shard_map/ppermute | solution.py:284
  37.2 19.8 %collective-permute-start.12 = (bf16[3,128,128]{2,1,0:T(8,128)(2,1)S(1)}, bf16[3,128,128]{2,1,0:T(8,128)(2,1)S(1)}, u32[]{:S(2)}, u32[]{:S(2)}) collective-permute-start(bf16[3,128,128]{2,1,0:T(8,128)(2,1)S(1)} %get-tuple-element.42), channel_id=1, source_target_pairs={{0,1},{1,0},{2,3},{3,2},{4,5},{5,4},{6,7},{7,6},{8,9},{9,8},{10,11... | collective-permute-start | bytes 294920 | tf_op jit(solution)/shard_map/ppermute | solution.py:284
  37.8 19.2 %collective-permute-start.13 = (bf16[3,128,128]{2,1,0:T(8,128)(2,1)S(1)}, bf16[3,128,128]{2,1,0:T(8,128)(2,1)S(1)}, u32[]{:S(2)}, u32[]{:S(2)}) collective-permute-start(bf16[3,128,128]{2,1,0:T(8,128)(2,1)S(1)} %get-tuple-element.43), channel_id=1, source_target_pairs={{0,2},{1,3},{2,0},{3,1},{4,6},{5,7},{6,4},{7,5},{8,10},{9,11},{10,... | collective-permute-start | bytes 294920 | tf_op jit(solution)/shard_map/ppermute | solution.py:284
  40.3 18.4 %collective-permute-start.14 = (bf16[3,128,128]{2,1,0:T(8,128)(2,1)S(1)}, bf16[3,128,128]{2,1,0:T(8,128)(2,1)S(1)}, u32[]{:S(2)}, u32[]{:S(2)}) collective-permute-start(bf16[3,128,128]{2,1,0:T(8,128)(2,1)S(1)} %get-tuple-element.44), channel_id=1, source_target_pairs={{0,3},{1,2},{2,1},{3,0},{4,7},{5,6},{6,5},{7,4},{8,11},{9,10},{10,... | collective-permute-start | bytes 294920 | tf_op jit(solution)/shard_map/ppermute | solution.py:284
  44.3 17.1 %collective-permute-start.6 = (bf16[3,128,128]{2,1,0:T(8,128)(2,1)S(1)}, bf16[3,128,128]{2,1,0:T(8,128)(2,1)S(1)}, u32[]{:S(2)}, u32[]{:S(2)}) collective-permute-start(bf16[3,128,128]{2,1,0:T(8,128)(2,1)S(1)} %get-tuple-element.34), channel_id=1, source_target_pairs={{0,1},{1,0},{2,3},{3,2},{4,5},{5,4},{6,7},{7,6},{8,9},{9,8},{10,11... | collective-permute-start | bytes 294920 | tf_op jit(solution)/shard_map/ppermute | solution.py:284
  44.8 19.8 %collective-permute-start.7 = (bf16[3,128,128]{2,1,0:T(8,128)(2,1)S(1)}, bf16[3,128,128]{2,1,0:T(8,128)(2,1)S(1)}, u32[]{:S(2)}, u32[]{:S(2)}) collective-permute-start(bf16[3,128,128]{2,1,0:T(8,128)(2,1)S(1)} %get-tuple-element.35), channel_id=1, source_target_pairs={{0,2},{1,3},{2,0},{3,1},{4,6},{5,7},{6,4},{7,5},{8,10},{9,11},{10,... | collective-permute-start | bytes 294920 | tf_op jit(solution)/shard_map/ppermute | solution.py:284
  57.0 27.8 %collective-permute-start.21 = (bf16[3,128,256]{2,1,0:T(8,128)(2,1)S(1)}, bf16[3,128,256]{2,1,0:T(8,128)(2,1)S(1)}, u32[]{:S(2)}, u32[]{:S(2)}) collective-permute-start(bf16[3,128,256]{2,1,0:T(8,128)(2,1)S(1)} %get-tuple-element.54), channel_id=1, source_target_pairs={{0,1},{1,0},{2,3},{3,2},{4,5},{5,4},{6,7},{7,6},{8,9},{9,8},{10,11... | collective-permute-start | bytes 589832 | tf_op jit(solution)/shard_map/ppermute | solution.py:304
  57.1 27.7 %collective-permute-start.22 = (bf16[3,128,256]{2,1,0:T(8,128)(2,1)S(1)}, bf16[3,128,256]{2,1,0:T(8,128)(2,1)S(1)}, u32[]{:S(2)}, u32[]{:S(2)}) collective-permute-start(bf16[3,128,256]{2,1,0:T(8,128)(2,1)S(1)} %get-tuple-element.55), channel_id=1, source_target_pairs={{0,2},{1,3},{2,0},{3,1},{4,6},{5,7},{6,4},{7,5},{8,10},{9,11},{10,... | collective-permute-start | bytes 589832 | tf_op jit(solution)/shard_map/ppermute | solution.py:304
  58.8 27.2 %collective-permute-start.23 = (bf16[3,128,256]{2,1,0:T(8,128)(2,1)S(1)}, bf16[3,128,256]{2,1,0:T(8,128)(2,1)S(1)}, u32[]{:S(2)}, u32[]{:S(2)}) collective-permute-start(bf16[3,128,256]{2,1,0:T(8,128)(2,1)S(1)} %get-tuple-element.56), channel_id=1, source_target_pairs={{0,3},{1,2},{2,1},{3,0},{4,7},{5,6},{6,5},{7,4},{8,11},{9,10},{10,... | collective-permute-start | bytes 589832 | tf_op jit(solution)/shard_map/ppermute | solution.py:304
  61.4 10.9 %collective-permute-start.8 = (bf16[3,128,128]{2,1,0:T(8,128)(2,1)S(1)}, bf16[3,128,128]{2,1,0:T(8,128)(2,1)S(1)}, u32[]{:S(2)}, u32[]{:S(2)}) collective-permute-start(bf16[3,128,128]{2,1,0:T(8,128)(2,1)S(1)} %get-tuple-element.36), channel_id=1, source_target_pairs={{0,3},{1,2},{2,1},{3,0},{4,7},{5,6},{6,5},{7,4},{8,11},{9,10},{10,... | collective-permute-start | bytes 294920 | tf_op jit(solution)/shard_map/ppermute | solution.py:284
  64.6 17.4 %collective-permute-start.15 = (bf16[3,128,128]{2,1,0:T(8,128)(2,1)S(1)}, bf16[3,128,128]{2,1,0:T(8,128)(2,1)S(1)}, u32[]{:S(2)}, u32[]{:S(2)}) collective-permute-start(bf16[3,128,128]{2,1,0:T(8,128)(2,1)S(1)} %get-tuple-element.46), channel_id=1, source_target_pairs={{0,1},{1,0},{2,3},{3,2},{4,5},{5,4},{6,7},{7,6},{8,9},{9,8},{10,11... | collective-permute-start | bytes 294920 | tf_op jit(solution)/shard_map/ppermute | solution.py:304
  72.3 16.9 %collective-permute-start.16 = (bf16[3,128,128]{2,1,0:T(8,128)(2,1)S(1)}, bf16[3,128,128]{2,1,0:T(8,128)(2,1)S(1)}, u32[]{:S(2)}, u32[]{:S(2)}) collective-permute-start(bf16[3,128,128]{2,1,0:T(8,128)(2,1)S(1)} %get-tuple-element.47), channel_id=1, source_target_pairs={{0,2},{1,3},{2,0},{3,1},{4,6},{5,7},{6,4},{7,5},{8,10},{9,11},{10,... | collective-permute-start | bytes 294920 | tf_op jit(solution)/shard_map/ppermute | solution.py:304
  82.0 7.2 %collective-permute-start.17 = (bf16[3,128,128]{2,1,0:T(8,128)(2,1)S(1)}, bf16[3,128,128]{2,1,0:T(8,128)(2,1)S(1)}, u32[]{:S(2)}, u32[]{:S(2)}) collective-permute-start(bf16[3,128,128]{2,1,0:T(8,128)(2,1)S(1)} %get-tuple-element.48), channel_id=1, source_target_pairs={{0,3},{1,2},{2,1},{3,0},{4,7},{5,6},{6,5},{7,4},{8,11},{9,10},{10,... | collective-permute-start | bytes 294920 | tf_op jit(solution)/shard_map/ppermute | solution.py:304
  84.7 11.2 %collective-permute-start.10 = (bf16[3,128,128]{2,1,0:T(8,128)(2,1)S(1)}, bf16[3,128,128]{2,1,0:T(8,128)(2,1)S(1)}, u32[]{:S(2)}, u32[]{:S(2)}) collective-permute-start(bf16[3,128,128]{2,1,0:T(8,128)(2,1)S(1)} %get-tuple-element.39), channel_id=1, source_target_pairs={{0,2},{1,3},{2,0},{3,1},{4,6},{5,7},{6,4},{7,5},{8,10},{9,11},{10,... | collective-permute-start | bytes 294920 | tf_op jit(solution)/shard_map/ppermute | solution.py:304
  84.7 11.2 %collective-permute-start.11 = (bf16[3,128,128]{2,1,0:T(8,128)(2,1)S(1)}, bf16[3,128,128]{2,1,0:T(8,128)(2,1)S(1)}, u32[]{:S(2)}, u32[]{:S(2)}) collective-permute-start(bf16[3,128,128]{2,1,0:T(8,128)(2,1)S(1)} %get-tuple-element.40), channel_id=1, source_target_pairs={{0,3},{1,2},{2,1},{3,0},{4,7},{5,6},{6,5},{7,4},{8,11},{9,10},{10,... | collective-permute-start | bytes 294920 | tf_op jit(solution)/shard_map/ppermute | solution.py:304
  86.0 10.0 %collective-permute-start.9 = (bf16[3,128,128]{2,1,0:T(8,128)(2,1)S(1)}, bf16[3,128,128]{2,1,0:T(8,128)(2,1)S(1)}, u32[]{:S(2)}, u32[]{:S(2)}) collective-permute-start(bf16[3,128,128]{2,1,0:T(8,128)(2,1)S(1)} %get-tuple-element.38), channel_id=1, source_target_pairs={{0,1},{1,0},{2,3},{3,2},{4,5},{5,4},{6,7},{7,6},{8,9},{9,8},{10,11... | collective-permute-start | bytes 294920 | tf_op jit(solution)/shard_map/ppermute | solution.py:304

commit v5 on v4

--- a/solution.py
+++ b/solution.py
@@ -10,20 +10,22 @@
 
 HD = 128
 GW = 64
-IN_HEADS = (2, 1, 1)
-OUT_HEADS = (2, 1, 1)
 
 
 def in_hbm(array):
     return pltpu.with_memory_space_constraint(array, pltpu.HBM)
 
 
-def visual_kernel(here_ref, pos_ref, gain_ref, hidden_hbm, cot_hbm, out_ref, held, sems):
+def visual_kernel(
+    here_ref, pos_hbm, gain_hbm, hidden_hbm, cot_hbm, out_ref, pos_ref, gain_ref, held, small, sems
+):
     rows = hidden_hbm.shape[1]
     picked = out_ref.shape[0]
     pieces = sems.shape[1]
     piece = rows // pieces
-    copies = []
+    pos_copy = pltpu.make_async_copy(pos_hbm, pos_ref, small.at[0])
+    copies = [pltpu.make_async_copy(gain_hbm, gain_ref, small.at[1])]
+    pos_copy.start()
     for i, source in enumerate((hidden_hbm, cot_hbm)):
         for j in range(pieces):
             at = pl.ds(j * piece, piece)
@@ -32,6 +34,7 @@
             )
     for copy in copies:
         copy.start()
+    pos_copy.wait()
     row = lax.broadcasted_iota(jnp.int32, (rows, picked), 0) + here_ref[0] * rows
     pick = jnp.where(row == pos_ref[...], 1.0, 0.0).astype(jnp.bfloat16)
     first_both = (((0,), (0,)), ((), ()))
@@ -62,10 +65,13 @@
     hbm = pl.BlockSpec(memory_space=pltpu.HBM)
     return pl.pallas_call(
         visual_kernel,
-        in_specs=[pl.BlockSpec(memory_space=pltpu.SMEM), vmem, vmem, hbm, hbm],
+        in_specs=[pl.BlockSpec(memory_space=pltpu.SMEM)] + [hbm] * 4,
         out_specs=vmem,
         scratch_shapes=[
+            pltpu.VMEM(positions.shape, jnp.int32),
+            pltpu.VMEM((depth // HD, HD), jnp.float32),
             pltpu.VMEM((2, rows, depth), jnp.bfloat16),
+            pltpu.SemaphoreType.DMA((2,)),
             pltpu.SemaphoreType.DMA((2, pieces)),
         ],
         out_shape=jax.ShapeDtypeStruct((picked, depth), jnp.bfloat16),
@@ -74,48 +80,50 @@
         ),
         compiler_params=pltpu.CompilerParams(vmem_limit_bytes=(8 << 20) + 12 * hidden.size),
         name="visual",
-    )(here, positions, gain.reshape(-1, HD), in_hbm(hidden), in_hbm(cotangent))
-
-
-def pack_kernel(count, first, here_ref, *refs):
+    )(here, *map(in_hbm, (positions, gain.reshape(-1, HD), hidden, cotangent)))
+
+
+def pack_kernel(count, first, slots, here_ref, *refs):
     sources, outs, sems = refs[:3], refs[3:-1], refs[-1]
-    width = outs[0].shape[2]
+    width = outs[0].shape[2] // len(slots)
     own_width = sources[0].shape[2] // count
     copies = []
     for k, out in enumerate(outs):
-        column = pl.multiple_of((here_ref[0] ^ k) * own_width + first, HD)
-        for i, source in enumerate(sources):
-            copies.append(
-                pltpu.make_async_copy(
-                    source.at[0, :, pl.ds(column, width)], out.at[i], sems.at[3 * k + i]
+        for j, slot in enumerate(slots):
+            column = pl.multiple_of((here_ref[0] ^ k ^ slot) * own_width + first, HD)
+            for i in range(out.shape[0]):
+                copies.append(
+                    pltpu.make_async_copy(
+                        sources[i].at[0, :, pl.ds(column, width)],
+                        out.at[i, :, pl.ds(j * width, width)],
+                        sems.at[len(copies)],
+                    )
                 )
-            )
     for copy in copies:
         copy.start()
     for copy in copies:
         copy.wait()
 
 
-def pack(here, sources, first, width, count):
-    rows = sources[0].shape[1]
+def pack(here, sources, first, width, slots, taken):
+    count, rows = len(taken), sources[0].shape[1]
+    total = sum(taken) * len(slots)
     return pl.pallas_call(
-        functools.partial(pack_kernel, count, first),
+        functools.partial(pack_kernel, count, first, slots),
         in_specs=[pl.BlockSpec(memory_space=pltpu.SMEM)]
         + [pl.BlockSpec(memory_space=pltpu.HBM)] * 3,
         out_specs=[pl.BlockSpec(memory_space=pltpu.VMEM)] * count,
-        out_shape=[jax.ShapeDtypeStruct((3, rows, width), jnp.bfloat16)] * count,
-        scratch_shapes=[pltpu.SemaphoreType.DMA((3 * count,))],
+        out_shape=[
+            jax.ShapeDtypeStruct((n, rows, width * len(slots)), jnp.bfloat16) for n in taken
+        ],
+        scratch_shapes=[pltpu.SemaphoreType.DMA((total,))],
         cost_estimate=pl.CostEstimate(
-            flops=0, bytes_accessed=12 * count * rows * width, transcendentals=0
+            flops=0, bytes_accessed=4 * total * rows * width, transcendentals=0
         ),
         compiler_params=pltpu.CompilerParams(
-            vmem_limit_bytes=(1 << 20) + 6 * count * rows * width
+            vmem_limit_bytes=(1 << 20) + 2 * total * rows * width
         ),
     )(here, *map(in_hbm, sources))
-
-
-def split(heads, parts):
-    return parts if sum(parts) == heads else (heads,)
 
 
 def partners(size, k):
@@ -140,6 +148,17 @@
             held[k ^ step] = lax.ppermute(held[k], axis, partners(size, step))
         step //= 2
     return [held[k] for k in range(size)]
+
+
+def spread_rows(rows, seen):
+    token = lax.broadcasted_iota(jnp.int32, (rows, seen), 0)
+    source = lax.broadcasted_iota(jnp.int32, (rows, seen), 1)
+    return jnp.where(
+        (token // (2 * GW)) * (GW // 2) + (token % GW) // 2 == source, 1.0, 0.0
+    ).astype(jnp.bfloat16)
+
+
+BOTH_LAST = (((1,), (1,)), ((), ()))
 
 
 def attend_kernel(count, scale, chunk, *refs):
@@ -155,11 +174,7 @@
         q_s[at] = block[0]
         k_s[at] = block[1]
         v_s[at] = block[2]
-    token = lax.broadcasted_iota(jnp.int32, (rows, seen), 0)
-    source = lax.broadcasted_iota(jnp.int32, (rows, seen), 1)
-    spread = jnp.where(
-        (token // (2 * GW)) * (GW // 2) + (token % GW) // 2 == source, 1.0, 0.0
-    ).astype(jnp.bfloat16)
+    spread = spread_rows(rows, seen)
     for j in range(count):
         g_s[pl.ds(j * rows, rows)] = jnp.dot(
             spread, handed_ref[pl.ds(j * seen, seen)], preferred_element_type=jnp.float32
@@ -169,16 +184,15 @@
     key_rows = k_s[...]
     value_rows = v_s[...]
     key_columns = key_rows.T
-    both_last = (((1,), (1,)), ((), ()))
 
     def step(c, carry):
         at = pl.ds(pl.multiple_of(c * chunk, chunk), chunk)
         q = q_s[at]
         g = g_s[at]
-        scores = lax.dot_general(key_rows, q, both_last, preferred_element_type=jnp.float32) * scale
+        scores = lax.dot_general(key_rows, q, BOTH_LAST, preferred_element_type=jnp.float32) * scale
         exp_scores = jnp.exp(scores - jnp.max(scores, axis=0, keepdims=True))
         weights = exp_scores * (1.0 / jnp.sum(exp_scores, axis=0, keepdims=True))
-        grad_weights = lax.dot_general(value_rows, g, both_last, preferred_element_type=jnp.float32)
+        grad_weights = lax.dot_general(value_rows, g, BOTH_LAST, preferred_element_type=jnp.float32)
         row_dot = jnp.sum(weights * grad_weights, axis=0, keepdims=True)
         grad_scores = (weights * (grad_weights - row_dot)).astype(jnp.bfloat16)
         dv_s[...] += jnp.dot(weights.astype(jnp.bfloat16), g, preferred_element_type=jnp.float32)
@@ -222,6 +236,149 @@
     )(handed, *blocks)
 
 
+def load_half(count, handed_ref, far_handed_ref, blocks, q_s, k_s, v_s, g_s):
+    half, rows = count // 2, blocks[0].shape[1]
+    seen = handed_ref.shape[0] // count
+    for j, block in enumerate(blocks):
+        at = pl.ds(j * rows, rows)
+        q_s[at] = block[0]
+        if j < half:
+            k_s[at] = block[1]
+            v_s[at] = block[2]
+    spread = spread_rows(rows, seen)
+
+    def fill(ref, swap):
+        for j in range(count):
+            g_s[pl.ds(j * rows, rows)] = jnp.dot(
+                spread, ref[pl.ds((j ^ swap) * seen, seen)], preferred_element_type=jnp.float32
+            ).astype(jnp.bfloat16)
+
+    own = pl.program_id(0) < pl.num_programs(0) // 2
+
+    @pl.when(own)
+    def _():
+        fill(handed_ref, 0)
+
+    @pl.when(jnp.logical_not(own))
+    def _():
+        fill(far_handed_ref, half)
+
+
+def half_products(scale, key_rows, value_rows, q, g):
+    scores = lax.dot_general(key_rows, q, BOTH_LAST, preferred_element_type=jnp.float32) * scale
+    grad_weights = lax.dot_general(value_rows, g, BOTH_LAST, preferred_element_type=jnp.float32)
+    return scores, grad_weights
+
+
+def half_stats_kernel(count, scale, chunk, *refs):
+    handed_ref, far_handed_ref = refs[:2]
+    blocks = refs[2 : 2 + count]
+    out, q_s, k_s, v_s, g_s = refs[2 + count :]
+    load_half(count, handed_ref, far_handed_ref, blocks, q_s, k_s, v_s, g_s)
+    key_rows, value_rows = k_s[...], v_s[...]
+
+    def step(c, carry):
+        at = pl.ds(pl.multiple_of(c * chunk, chunk), chunk)
+        scores, grad_weights = half_products(scale, key_rows, value_rows, q_s[at], g_s[at])
+        row_max = jnp.max(scores, axis=0, keepdims=True)
+        exp_scores = jnp.exp(scores - row_max)
+        total = jnp.sum(exp_scores, axis=0, keepdims=True)
+        out[0, pl.ds(0, 1), at] = row_max + jnp.log(total)
+        out[0, pl.ds(1, 1), at] = (
+            jnp.sum(exp_scores * grad_weights, axis=0, keepdims=True) / total
+        )
+        return carry
+
+    lax.fori_loop(0, q_s.shape[0] // chunk, step, 0)
+
+
+def half_grads_kernel(count, scale, chunk, *refs):
+    handed_ref, far_handed_ref = refs[:2]
+    blocks = refs[2 : 2 + count]
+    stats_ref, far_stats_ref = refs[2 + count : 4 + count]
+    outs = refs[4 + count : 4 + 2 * count]
+    q_s, k_s, v_s, g_s, dq_s, dk_s, dv_s = refs[4 + 2 * count :]
+    load_half(count, handed_ref, far_handed_ref, blocks, q_s, k_s, v_s, g_s)
+    rows, length = blocks[0].shape[1], q_s.shape[0]
+    dk_s[...] = jnp.zeros_like(dk_s)
+    dv_s[...] = jnp.zeros_like(dv_s)
+    key_rows, value_rows = k_s[...], v_s[...]
+    key_columns = key_rows.T
+
+    def step(c, carry):
+        at = pl.ds(pl.multiple_of(c * chunk, chunk), chunk)
+        far_first = lax.rem(c * chunk + length // 2, length)
+        far_at = pl.ds(pl.multiple_of(far_first, chunk), chunk)
+        q, g = q_s[at], g_s[at]
+        scores, grad_weights = half_products(scale, key_rows, value_rows, q, g)
+        near, far = stats_ref[0, pl.ds(0, 1), at], far_stats_ref[0, pl.ds(0, 1), far_at]
+        top = jnp.maximum(near, far)
+        whole = top + jnp.log(jnp.exp(near - top) + jnp.exp(far - top))
+        row_dot = (
+            jnp.exp(near - whole) * stats_ref[0, pl.ds(1, 1), at]
+            + jnp.exp(far - whole) * far_stats_ref[0, pl.ds(1, 1), far_at]
+        )
+        weights = jnp.exp(scores - whole)
+        grad_scores = (weights * (grad_weights - row_dot)).astype(jnp.bfloat16)
+        dv_s[...] += jnp.dot(weights.astype(jnp.bfloat16), g, preferred_element_type=jnp.float32)
+        dk_s[...] += jnp.dot(grad_scores, q, preferred_element_type=jnp.float32)
+        dq = jnp.dot(key_columns, grad_scores, preferred_element_type=jnp.float32)
+        dq_s[at] = (dq * scale).T.astype(jnp.bfloat16)
+        return carry
+
+    lax.fori_loop(0, length // chunk, step, 0)
+    for j, out in enumerate(outs):
+        at = pl.ds(j * rows, rows)
+        out[0] = dq_s[at]
+        if j < count // 2:
+            out[1] = (dk_s[at] * scale).astype(jnp.bfloat16)
+            out[2] = dv_s[at].astype(jnp.bfloat16)
+
+
+def half_call(kernel, handed, far_handed, blocks, stats, first):
+    count = len(blocks)
+    rows, heads = blocks[0].shape[1], blocks[0].shape[2] // HD
+    length, held = rows * count, rows * count // 2
+    chunk = min(256, held)
+    each = heads // 2
+
+    def block_spec(array):
+        return pl.BlockSpec((array.shape[0], rows, HD), lambda h: (0, 0, h))
+
+    stats_spec = pl.BlockSpec((1, 2, length), lambda h: (h, 0, 0))
+    far_spec = pl.BlockSpec((1, 2, length), lambda h: (lax.rem(h + each, heads), 0, 0))
+    scratch = [pltpu.VMEM((n, HD), jnp.bfloat16) for n in (length, held, held, length)]
+    if stats:
+        out_specs = [block_spec(b) for b in blocks]
+        out_shape = [jax.ShapeDtypeStruct(b.shape, jnp.bfloat16) for b in blocks]
+        scratch += [pltpu.VMEM((length, HD), jnp.bfloat16)]
+        scratch += [pltpu.VMEM((held, HD), jnp.float32)] * 2
+    else:
+        out_specs = stats_spec
+        out_shape = jax.ShapeDtypeStruct((heads, 2, length), jnp.float32)
+    return pl.pallas_call(
+        functools.partial(kernel, count, HD**-0.5, chunk),
+        grid=(heads,),
+        in_specs=[
+            pl.BlockSpec((handed.shape[0], HD), lambda h: (0, first + lax.rem(h, each))),
+            pl.BlockSpec((handed.shape[0], HD), lambda h: (0, lax.rem(h, each))),
+        ]
+        + [block_spec(b) for b in blocks]
+        + [stats_spec, far_spec][: len(stats)],
+        out_specs=out_specs,
+        scratch_shapes=scratch,
+        out_shape=out_shape,
+        cost_estimate=pl.CostEstimate(
+            flops=(10 if stats else 4) * heads * length * held * HD,
+            bytes_accessed=12 * length * heads * HD,
+            transcendentals=heads * length * held,
+        ),
+        compiler_params=pltpu.CompilerParams(
+            vmem_limit_bytes=(4 << 20) + 48 * length * chunk
+        ),
+    )(handed, far_handed, *blocks, *stats)
+
+
 def place_kernel(count, first, *refs):
     here = refs[0][0]
     parts = refs[1 : 1 + count]
@@ -266,6 +423,61 @@
     )(here, *parts, *outs)
 
 
+def place_half_kernel(count, first, *refs):
+    here = refs[0][0]
+    parts = refs[1 : 1 + count]
+    outs = refs[4 + count : 7 + count]
+    added, sems = refs[7 + count :]
+    half, width = count // 2, parts[0].shape[2] // 2
+    own_width = outs[0].shape[2] // count
+    copies = []
+
+    def put(source, out, shard):
+        column = pl.multiple_of((here ^ shard) * own_width + first, HD)
+        copy = pltpu.make_async_copy(
+            source, out.at[0, :, pl.ds(column, width)], sems.at[len(copies)]
+        )
+        copy.start()
+        copies.append(copy)
+
+    for k in range(half):
+        for slot in range(2):
+            for i in (1, 2):
+                put(parts[k].at[i, :, pl.ds(slot * width, width)], outs[i], k ^ (half * slot))
+    for shard in range(count):
+        near = parts[shard][0, :, pl.ds(0, width)].astype(jnp.float32)
+        far = parts[shard ^ half][0, :, pl.ds(width, width)].astype(jnp.float32)
+        added[shard] = (near + far).astype(jnp.bfloat16)
+        put(added.at[shard], outs[0], shard)
+    for copy in copies:
+        copy.wait()
+
+
+def place_half(here, parts, outs, first):
+    count, (rows, width) = len(parts), parts[0].shape[1:]
+    anywhere = pl.BlockSpec(memory_space=pl.ANY)
+    return pl.pallas_call(
+        functools.partial(place_half_kernel, count, first),
+        in_specs=[pl.BlockSpec(memory_space=pltpu.SMEM)]
+        + [pl.BlockSpec(memory_space=pltpu.VMEM)] * count
+        + [anywhere] * 3,
+        out_specs=[anywhere] * 3,
+        out_shape=[jax.ShapeDtypeStruct(out.shape, out.dtype) for out in outs],
+        input_output_aliases={1 + count + i: i for i in range(3)},
+        scratch_shapes=[
+            pltpu.VMEM((count, rows, width // 2), jnp.bfloat16),
+            pltpu.SemaphoreType.DMA((3 * count,)),
+        ],
+        cost_estimate=pl.CostEstimate(
+            flops=0, bytes_accessed=4 * count * parts[0].size, transcendentals=0
+        ),
+        compiler_params=pltpu.CompilerParams(
+            vmem_limit_bytes=(1 << 20) + 4 * count * parts[0].size
+        ),
+        name="place_half",
+    )(here, *parts, *outs)
+
+
 def work(
     rm_hidden, rm_cotangent, rm_gain, rewards, visual_pos, bridge, img_query, img_key, img_value
 ):
@@ -273,17 +485,24 @@
     here = lax.axis_index("tensor")
     place_of = here[None].astype(jnp.int32)
     own_width = img_query.shape[2] // count
+    heads = own_width // HD
+    shared = heads // 2
+    whole = heads - shared
+    half = count // 2
     own = (img_query, img_key, img_value)
+
+    def exchange(blocks):
+        return [blocks[0]] + [
+            lax.ppermute(blocks[k], "tensor", partners(count, k)) for k in range(1, count)
+        ]
+
     visual_grad = visual_grads(place_of, visual_pos, rm_hidden, rm_cotangent, rm_gain)
     visual_blocks = gathered(visual_grad, "tensor")
-
-    arrived = []
-    for heads in split(own_width // HD, IN_HEADS):
-        packed = pack(place_of, own, len(arrived) * HD, heads * HD, count)
-        blocks = [packed[0]] + [
-            lax.ppermute(packed[k], "tensor", partners(count, k)) for k in range(1, count)
-        ]
-        arrived += [(blocks, skip) for skip in range(heads)]
+    blocks = exchange(pack(place_of, own, 0, whole * HD, (0,), (3,) * count))
+    if shared:
+        taken = (3,) * half + (1,) * half
+        packed = pack(place_of, own, whole * HD, shared * HD, (0, half), taken)
+        half_blocks = exchange(packed)
 
     reward_sum = total_over(jnp.sum(rewards), "dp")
     sample_count = lax.axis_size("dp") * rewards.shape[0]
@@ -294,17 +513,20 @@
         )
         * reward_weight
     ).astype(jnp.bfloat16)
+    if shared:
+        far_handed = lax.ppermute(handed[:, whole * HD :], "tensor", partners(count, half))
 
     outs = ()
-    first = 0
-    for heads in split(own_width // HD, OUT_HEADS):
-        blocks, skip = arrived[first]
-        grads = attend(handed, blocks, first, skip, heads)
-        parts = [grads[0]] + [
-            lax.ppermute(grads[k], "tensor", partners(count, k)) for k in range(1, count)
-        ]
-        outs = place(place_of, parts, outs, img_query.shape, first * HD)
-        first += heads
+    for g in range(whole):
+        parts = exchange(attend(handed, blocks, g, g, 1))
+        outs = place(place_of, parts, outs, img_query.shape, g * HD)
+    if shared:
+        stats = half_call(half_stats_kernel, handed, far_handed, half_blocks, (), whole)
+        far_stats = lax.ppermute(stats, "tensor", partners(count, half))
+        grads = half_call(
+            half_grads_kernel, handed, far_handed, half_blocks, (stats, far_stats), whole
+        )
+        outs = place_half(place_of, exchange(grads), outs, whole * HD)
     return tuple(outs)
 
 

time: 97.3 us -> 105 us (1.079)
  the two profiles are of different devices: /device:TPU:0 before, /device:TPU:2 now
where the time goes in v5:
time: 105 us; the launch traced here: 103 us
  starting transfers between devices  41.1 us (39%)
  waiting for transfers between devices  35.4 us (34%)
  Pallas kernels  20.4 us (19%)
  between operations  3.33 us (3%)
  matrix products  2.68 us (3%)
    ppermute x15, starting transfers between devices, exchange(): lax.ppermute(blocks[k], 'tensor', partners(count, k))  29.3 us
    ppermute x15, waiting for transfers between devices, exchange(): lax.ppermute(blocks[k], 'tensor', partners(count, k))  19.8 us
    pallas_call x2, Pallas kernels, half_call(): pl.pallas_call(functools.partial(kernel, count, HD ** (-0.5), chunk), gri...  9.3 us
    ppermute x3, waiting for transfers between devices, gathered(): held[k ^ step] = lax.ppermute(held[k], axis, partners(size, step))  9.1 us
    ppermute x3, starting transfers between devices, gathered(): held[k ^ step] = lax.ppermute(held[k], axis, partners(size, step))  4.8 us
    ppermute x3, starting transfers between devices, total_over(): value = value + lax.ppermute(value, axis, partners(size, step))  4.78 us
    ppermute x1, waiting for transfers between devices, work(): lax.ppermute(handed[:, whole * HD:], 'tensor', partners(count, half))  4.11 us
    pallas_call x2, Pallas kernels, attend(): pl.pallas_call(functools.partial(attend_kernel, count, HD ** (-0.5), chun...  4.02 us
  transfers between devices with their start and end apart: 23, of which 9 were waited for; matrix products, arithmetic and copies ran while one was open for 3% of the time, Pallas kernels for 14%

profile of v5, /device:TPU:2, one launch (start us, length us, event | category | flops | bytes accessed | tf_op | source)
XLA Modules:
  0.0 102.9 jit_solution(9904143224766487490)
XLA Ops:
  0.6 1.8 %visual.1 = bf16[32,3584]{1,0:T(8,128)(2,1)S(1)} custom-call(s32[1]{0:T(128)} %bitcast.here_ref.refs_0_, s32[1,32]{1,0:T(1,128)} %pos_hbm.1, f32[28,128]{1,0:T(8,128)} %bitcast.6, bf16[1,64,3584]{2,1,0:T(8,128)(2,1)} %hidden_hbm.1, bf16[1,64,3584]{2,1,0:T(8,128)(2,1)} %cot_hbm.1), custom_call_target="tpu_custom_call" | custom-call | flops 29360128 | bytes 917504 | tf_op jit(solution)/shard_map/visual/pallas_call | solution.py:66
  2.4 2.7 %collective-permute-start.1 = (bf16[32,3584]{1,0:T(8,128)(2,1)S(1)}, bf16[32,3584]{1,0:T(8,128)(2,1)S(1)}, u32[]{:S(2)}, u32[]{:S(2)}) collective-permute-start(bf16[32,3584]{1,0:T(8,128)(2,1)S(1)} %visual.1), channel_id=1, source_target_pairs={{0,2},{1,3},{2,0},{3,1},{4,6},{5,7},{6,4},{7,5},{8,10},{9,11},{10,... | collective-permute-start | bytes 688136 | tf_op jit(solution)/shard_map/ppermute | solution.py:148
  5.1 1.6 %collective-permute-start = (bf16[32,3584]{1,0:T(8,128)(2,1)S(1)}, bf16[32,3584]{1,0:T(8,128)(2,1)S(1)}, u32[]{:S(2)}, u32[]{:S(2)}) collective-permute-start(bf16[32,3584]{1,0:T(8,128)(2,1)S(1)} %visual.1), channel_id=1, source_target_pairs={{0,1},{1,0},{2,3},{3,2},{4,5},{5,4},{6,7},{7,6},{8,9},{9,8},{10,11... | collective-permute-start | bytes 688136 | tf_op jit(solution)/shard_map/ppermute | solution.py:148
  6.7 9.1 %collective-permute-done.1 = bf16[32,3584]{1,0:T(8,128)(2,1)S(1)} collective-permute-done((bf16[32,3584]{1,0:T(8,128)(2,1)S(1)}, bf16[32,3584]{1,0:T(8,128)(2,1)S(1)}, u32[]{:S(2)}, u32[]{:S(2)}) %collective-permute-start.1) | collective-permute-done | bytes 229408 | tf_op jit(solution)/shard_map/ppermute | solution.py:148
  16.3 1.4 %shard_map.112 = (bf16[3,128,512]{2,1,0:T(8,128)(2,1)S(1)}, bf16[3,128,512]{2,1,0:T(8,128)(2,1)S(1)}, bf16[1,128,512]{2,1,0:T(8,128)(2,1)S(1)}, bf16[1,128,512]{2,1,0:T(8,128)(2,1)S(1)}) custom-call(s32[1]{0:T(128)} %bitcast.here_ref.refs_0_, bf16[1,128,2048]{2,1,0:T(8,128)(2,1)} %refs_0_.3, bf16[1,128,2048]{2,1,0:T(8,128)(2,1)} %refs_1_.3, ...), custom_call_target="tpu_custom_call" | custom-call | bytes 2097152 | tf_op jit(solution)/shard_map/pallas_call | solution.py:111
  17.7 1.5 %collective-permute-start.7 = (bf16[3,128,512]{2,1,0:T(8,128)(2,1)S(1)}, bf16[3,128,512]{2,1,0:T(8,128)(2,1)S(1)}, u32[]{:S(2)}, u32[]{:S(2)}) collective-permute-start(bf16[3,128,512]{2,1,0:T(8,128)(2,1)S(1)} %get-tuple-element.30), channel_id=1, source_target_pairs={{0,1},{1,0},{2,3},{3,2},{4,5},{5,4},{6,7},{7,6},{8,9},{9,8},{10,11... | collective-permute-start | bytes 1179656 | tf_op jit(solution)/shard_map/ppermute | solution.py:496
  19.2 2.0 %collective-permute-start.8 = (bf16[1,128,512]{2,1,0:T(8,128)(2,1)S(1)}, bf16[1,128,512]{2,1,0:T(8,128)(2,1)S(1)}, u32[]{:S(2)}, u32[]{:S(2)}) collective-permute-start(bf16[1,128,512]{2,1,0:T(8,128)(2,1)S(1)} %get-tuple-element.31), channel_id=1, source_target_pairs={{0,2},{1,3},{2,0},{3,1},{4,6},{5,7},{6,4},{7,5},{8,10},{9,11},{10,... | collective-permute-start | bytes 393224 | tf_op jit(solution)/shard_map/ppermute | solution.py:496
  22.5 1.9 %collective-permute-start.4 = (f32[]{:T(128)}, f32[]{:T(128)}, u32[]{:S(2)}, u32[]{:S(2)}) collective-permute-start(f32[]{:T(128)} %add.9), channel_id=1, source_target_pairs={{0,8},{4,12},{8,0},{12,4},{16,24},{20,28},{24,16},{28,20},{1,9},{5... | collective-permute-start | bytes 20 | tf_op jit(solution)/shard_map/ppermute | solution.py:137
  24.4 1.7 %collective-permute-done.4 = f32[]{:T(128)} collective-permute-done((f32[]{:T(128)}, f32[]{:T(128)}, u32[]{:S(2)}, u32[]{:S(2)}) %collective-permute-start.4) | collective-permute-done | bytes 36 | tf_op jit(solution)/shard_map/ppermute | solution.py:137
  26.7 2.9 %collective-permute-start.5 = (f32[]{:T(128)}, f32[]{:T(128)}, u32[]{:S(2)}, u32[]{:S(2)}) collective-permute-start(f32[]{:T(128)} %add.10), channel_id=1, source_target_pairs={{0,16},{4,20},{8,24},{12,28},{16,0},{20,4},{24,8},{28,12},{1,17},{... | collective-permute-start | bytes 20 | tf_op jit(solution)/shard_map/ppermute | solution.py:137
  30.3 1.4 %collective-permute-start.9 = (bf16[1,128,512]{2,1,0:T(8,128)(2,1)S(1)}, bf16[1,128,512]{2,1,0:T(8,128)(2,1)S(1)}, u32[]{:S(2)}, u32[]{:S(2)}) collective-permute-start(bf16[1,128,512]{2,1,0:T(8,128)(2,1)S(1)} %get-tuple-element.32), channel_id=1, source_target_pairs={{0,3},{1,2},{2,1},{3,0},{4,7},{5,6},{6,5},{7,4},{8,11},{9,10},{10,... | collective-permute-start | bytes 393224 | tf_op jit(solution)/shard_map/ppermute | solution.py:496
  32.4 2.7 %fusion.refs_0_ = bf16[128,512]{1,0:T(8,128)(2,1)S(1)} fusion(bf16[3584,512]{1,0:T(8,128)(2,1)} %param.14, bf16[32,3584]{1,0:T(8,128)(2,1)S(1)} %collective-permute-done.2, bf16[32,3584]{1,0:T(8,128)(2,1)S(1)} %collective-permute-done.1, bf16[32,3584]{1,0:T(8,128)(2,1)S(1)} %collective-permute-done, bf16[32,3584]{1,0:T(8,128)(2,1)S(1)} %visual.1, f32[]{:T(128)S(6)} %div.3), kind=kOutput, calls=%fused_computation.1 | convolution fusion | flops 473563136 | bytes 4718596 | tf_op jit(solution)/shard_map/dot_general | solution.py:511
  35.1 2.1 %collective-permute-start.6 = (bf16[128,256]{1,0:T(8,128)(2,1)S(1)}, bf16[128,256]{1,0:T(8,128)(2,1)S(1)}, u32[]{:S(2)}, u32[]{:S(2)}) collective-permute-start(bf16[128,256]{1,0:T(8,128)(2,1)S(1)} %slice.4), channel_id=1, source_target_pairs={{0,2},{1,3},{2,0},{3,1},{4,6},{5,7},{6,4},{7,5},{8,10},{9,11},{10,... | collective-permute-start | bytes 196616 | tf_op jit(solution)/shard_map/ppermute | solution.py:517
  37.2 2.6 %collective-permute-done.9.refs_5_ = bf16[1,128,512]{2,1,0:T(8,128)(2,1)S(1)} collective-permute-done((bf16[1,128,512]{2,1,0:T(8,128)(2,1)S(1)}, bf16[1,128,512]{2,1,0:T(8,128)(2,1)S(1)}, u32[]{:S(2)}, u32[]{:S(2)}) %collective-permute-start.9) | collective-permute-done | bytes 131104 | tf_op jit(solution)/shard_map/ppermute | solution.py:496
  39.7 4.1 %collective-permute-done.6.refs_1_ = bf16[128,256]{1,0:T(8,128)(2,1)S(1)} collective-permute-done((bf16[128,256]{1,0:T(8,128)(2,1)S(1)}, bf16[128,256]{1,0:T(8,128)(2,1)S(1)}, u32[]{:S(2)}, u32[]{:S(2)}) %collective-permute-start.6) | collective-permute-done | bytes 65568 | tf_op jit(solution)/shard_map/ppermute | solution.py:517
  43.9 3.8 %shard_map.113.refs_6_ = f32[4,2,512]{2,1,0:T(2,128)S(1)} custom-call(bf16[128,512]{1,0:T(8,128)(2,1)S(1)} %fusion.refs_0_, bf16[128,256]{1,0:T(8,128)(2,1)S(1)} %collective-permute-done.6.refs_1_, bf16[3,128,512]{2,1,0:T(8,128)(2,1)S(1)} %get-tuple-element.29.refs_2_, bf16[3,128,512]{2,1,0:T(8,128)(2,1)S(1)} %collective-permute-done.7.refs_3_, ...), custom_call_target="tpu_custom_call" | custom-call | flops 268435456 | bytes 3145728 | tf_op jit(solution)/shard_map/pallas_call | solution.py:359
  49.0 1.4 %collective-permute-start.14 = (bf16[3,128,256]{2,1,0:T(8,128)(2,1)S(1)}, bf16[3,128,256]{2,1,0:T(8,128)(2,1)S(1)}, u32[]{:S(2)}, u32[]{:S(2)}) collective-permute-start(bf16[3,128,256]{2,1,0:T(8,128)(2,1)S(1)} %get-tuple-element.38), channel_id=1, source_target_pairs={{0,1},{1,0},{2,3},{3,2},{4,5},{5,4},{6,7},{7,6},{8,9},{9,8},{10,11... | collective-permute-start | bytes 589832 | tf_op jit(solution)/shard_map/ppermute | solution.py:496
  50.4 1.6 %collective-permute-start.15 = (bf16[3,128,256]{2,1,0:T(8,128)(2,1)S(1)}, bf16[3,128,256]{2,1,0:T(8,128)(2,1)S(1)}, u32[]{:S(2)}, u32[]{:S(2)}) collective-permute-start(bf16[3,128,256]{2,1,0:T(8,128)(2,1)S(1)} %get-tuple-element.39), channel_id=1, source_target_pairs={{0,2},{1,3},{2,0},{3,1},{4,6},{5,7},{6,4},{7,5},{8,10},{9,11},{10,... | collective-permute-start | bytes 589832 | tf_op jit(solution)/shard_map/ppermute | solution.py:496
  52.0 1.4 %collective-permute-start.16 = (bf16[3,128,256]{2,1,0:T(8,128)(2,1)S(1)}, bf16[3,128,256]{2,1,0:T(8,128)(2,1)S(1)}, u32[]{:S(2)}, u32[]{:S(2)}) collective-permute-start(bf16[3,128,256]{2,1,0:T(8,128)(2,1)S(1)} %get-tuple-element.40), channel_id=1, source_target_pairs={{0,3},{1,2},{2,1},{3,0},{4,7},{5,6},{6,5},{7,4},{8,11},{9,10},{10,... | collective-permute-start | bytes 589832 | tf_op jit(solution)/shard_map/ppermute | solution.py:496
  53.4 5.5 %shard_map.114 = (bf16[3,128,512]{2,1,0:T(8,128)(2,1)S(1)}, bf16[3,128,512]{2,1,0:T(8,128)(2,1)S(1)}, bf16[1,128,512]{2,1,0:T(8,128)(2,1)S(1)}, bf16[1,128,512]{2,1,0:T(8,128)(2,1)S(1)}) custom-call(bf16[128,512]{1,0:T(8,128)(2,1)S(1)} %fusion.refs_0_, bf16[128,256]{1,0:T(8,128)(2,1)S(1)} %collective-permute-done.6.refs_1_, ...), custom_call_target="tpu_custom_call" | custom-call | flops 671088640 | bytes 3145728 | tf_op jit(solution)/shard_map/pallas_call | solution.py:359
  59.6 7.2 %collective-permute-done.15.refs_3_ = bf16[3,128,256]{2,1,0:T(8,128)(2,1)S(1)} collective-permute-done((bf16[3,128,256]{2,1,0:T(8,128)(2,1)S(1)}, bf16[3,128,256]{2,1,0:T(8,128)(2,1)S(1)}, u32[]{:S(2)}, u32[]{:S(2)}) %collective-permute-start.15) | collective-permute-done | bytes 196640 | tf_op jit(solution)/shard_map/ppermute | solution.py:496
  67.6 2.0 %shard_map.117 = (bf16[3,128,128]{2,1,0:T(8,128)(2,1)S(1)}, bf16[3,128,128]{2,1,0:T(8,128)(2,1)S(1)}, bf16[3,128,128]{2,1,0:T(8,128)(2,1)S(1)}, bf16[3,128,128]{2,1,0:T(8,128)(2,1)S(1)}) custom-call(bf16[128,512]{1,0:T(8,128)(2,1)S(1)} %fusion.refs_0_, bf16[3,128,256]{2,1,0:T(8,128)(2,1)S(1)} %get-tuple-element.37.refs_1_, ...), custom_call_target="tpu_custom_call" | custom-call | flops 335544320 | bytes 786432 | tf_op jit(solution)/shard_map/pallas_call | solution.py:219
  69.6 2.4 %collective-permute-start.20 = (bf16[3,128,128]{2,1,0:T(8,128)(2,1)S(1)}, bf16[3,128,128]{2,1,0:T(8,128)(2,1)S(1)}, u32[]{:S(2)}, u32[]{:S(2)}) collective-permute-start(bf16[3,128,128]{2,1,0:T(8,128)(2,1)S(1)} %get-tuple-element.46), channel_id=1, source_target_pairs={{0,1},{1,0},{2,3},{3,2},{4,5},{5,4},{6,7},{7,6},{8,9},{9,8},{10,11... | collective-permute-start | bytes 294920 | tf_op jit(solution)/shard_map/ppermute | solution.py:496
  72.0 1.5 %collective-permute-start.21 = (bf16[3,128,128]{2,1,0:T(8,128)(2,1)S(1)}, bf16[3,128,128]{2,1,0:T(8,128)(2,1)S(1)}, u32[]{:S(2)}, u32[]{:S(2)}) collective-permute-start(bf16[3,128,128]{2,1,0:T(8,128)(2,1)S(1)} %get-tuple-element.47), channel_id=1, source_target_pairs={{0,2},{1,3},{2,0},{3,1},{4,6},{5,7},{6,4},{7,5},{8,10},{9,11},{10,... | collective-permute-start | bytes 294920 | tf_op jit(solution)/shard_map/ppermute | solution.py:496
  73.5 1.4 %collective-permute-start.22 = (bf16[3,128,128]{2,1,0:T(8,128)(2,1)S(1)}, bf16[3,128,128]{2,1,0:T(8,128)(2,1)S(1)}, u32[]{:S(2)}, u32[]{:S(2)}) collective-permute-start(bf16[3,128,128]{2,1,0:T(8,128)(2,1)S(1)} %get-tuple-element.48), channel_id=1, source_target_pairs={{0,3},{1,2},{2,1},{3,0},{4,7},{5,6},{6,5},{7,4},{8,11},{9,10},{10,... | collective-permute-start | bytes 294920 | tf_op jit(solution)/shard_map/ppermute | solution.py:496
  74.8 2.0 %shard_map.116 = (bf16[3,128,128]{2,1,0:T(8,128)(2,1)S(1)}, bf16[3,128,128]{2,1,0:T(8,128)(2,1)S(1)}, bf16[3,128,128]{2,1,0:T(8,128)(2,1)S(1)}, bf16[3,128,128]{2,1,0:T(8,128)(2,1)S(1)}) custom-call(bf16[128,512]{1,0:T(8,128)(2,1)S(1)} %fusion.refs_0_, bf16[3,128,256]{2,1,0:T(8,128)(2,1)S(1)} %get-tuple-element.37.refs_1_, ...), custom_call_target="tpu_custom_call" | custom-call | flops 335544320 | bytes 786432 | tf_op jit(solution)/shard_map/pallas_call | solution.py:219
  77.6 2.4 %collective-permute-start.12 = (bf16[1,128,512]{2,1,0:T(8,128)(2,1)S(1)}, bf16[1,128,512]{2,1,0:T(8,128)(2,1)S(1)}, u32[]{:S(2)}, u32[]{:S(2)}) collective-permute-start(bf16[1,128,512]{2,1,0:T(8,128)(2,1)S(1)} %get-tuple-element.35), channel_id=1, source_target_pairs={{0,2},{1,3},{2,0},{3,1},{4,6},{5,7},{6,4},{7,5},{8,10},{9,11},{10,... | collective-permute-start | bytes 393224 | tf_op jit(solution)/shard_map/ppermute | solution.py:496
  79.9 2.2 %collective-permute-done.21.refs_3_ = bf16[3,128,128]{2,1,0:T(8,128)(2,1)S(1)} collective-permute-done((bf16[3,128,128]{2,1,0:T(8,128)(2,1)S(1)}, bf16[3,128,128]{2,1,0:T(8,128)(2,1)S(1)}, u32[]{:S(2)}, u32[]{:S(2)}) %collective-permute-start.21) | collective-permute-done | bytes 98336 | tf_op jit(solution)/shard_map/ppermute | solution.py:496
  82.1 3.3 %collective-permute-start.13 = (bf16[1,128,512]{2,1,0:T(8,128)(2,1)S(1)}, bf16[1,128,512]{2,1,0:T(8,128)(2,1)S(1)}, u32[]{:S(2)}, u32[]{:S(2)}) collective-permute-start(bf16[1,128,512]{2,1,0:T(8,128)(2,1)S(1)} %get-tuple-element.36), channel_id=1, source_target_pairs={{0,3},{1,2},{2,1},{3,0},{4,7},{5,6},{6,5},{7,4},{8,11},{9,10},{10,... | collective-permute-start | bytes 393224 | tf_op jit(solution)/shard_map/ppermute | solution.py:496
  85.4 4.4 %collective-permute-start.18 = (bf16[3,128,128]{2,1,0:T(8,128)(2,1)S(1)}, bf16[3,128,128]{2,1,0:T(8,128)(2,1)S(1)}, u32[]{:S(2)}, u32[]{:S(2)}) collective-permute-start(bf16[3,128,128]{2,1,0:T(8,128)(2,1)S(1)} %get-tuple-element.43), channel_id=1, source_target_pairs={{0,2},{1,3},{2,0},{3,1},{4,6},{5,7},{6,4},{7,5},{8,10},{9,11},{10,... | collective-permute-start | bytes 294920 | tf_op jit(solution)/shard_map/ppermute | solution.py:496
  89.8 3.4 %collective-permute-start.19 = (bf16[3,128,128]{2,1,0:T(8,128)(2,1)S(1)}, bf16[3,128,128]{2,1,0:T(8,128)(2,1)S(1)}, u32[]{:S(2)}, u32[]{:S(2)}) collective-permute-start(bf16[3,128,128]{2,1,0:T(8,128)(2,1)S(1)} %get-tuple-element.44), channel_id=1, source_target_pairs={{0,3},{1,2},{2,1},{3,0},{4,7},{5,6},{6,5},{7,4},{8,11},{9,10},{10,... | collective-permute-start | bytes 294920 | tf_op jit(solution)/shard_map/ppermute | solution.py:496
  94.1 7.0 %collective-permute-done.18.refs_3_ = bf16[3,128,128]{2,1,0:T(8,128)(2,1)S(1)} collective-permute-done((bf16[3,128,128]{2,1,0:T(8,128)(2,1)S(1)}, bf16[3,128,128]{2,1,0:T(8,128)(2,1)S(1)}, u32[]{:S(2)}, u32[]{:S(2)}) %collective-permute-start.18) | collective-permute-done | bytes 98336 | tf_op jit(solution)/shard_map/ppermute | solution.py:496
  (26 shorter events, 7.4 us)
Async XLA Ops:
  2.4 13.3 %collective-permute-start.1 = (bf16[32,3584]{1,0:T(8,128)(2,1)S(1)}, bf16[32,3584]{1,0:T(8,128)(2,1)S(1)}, u32[]{:S(2)}, u32[]{:S(2)}) collective-permute-start(bf16[32,3584]{1,0:T(8,128)(2,1)S(1)} %visual.1), channel_id=1, source_target_pairs={{0,2},{1,3},{2,0},{3,1},{4,6},{5,7},{6,4},{7,5},{8,10},{9,11},{10,... | collective-permute-start | bytes 688136 | tf_op jit(solution)/shard_map/ppermute | solution.py:148
  5.1 27.3 %collective-permute-start = (bf16[32,3584]{1,0:T(8,128)(2,1)S(1)}, bf16[32,3584]{1,0:T(8,128)(2,1)S(1)}, u32[]{:S(2)}, u32[]{:S(2)}) collective-permute-start(bf16[32,3584]{1,0:T(8,128)(2,1)S(1)} %visual.1), channel_id=1, source_target_pairs={{0,1},{1,0},{2,3},{3,2},{4,5},{5,4},{6,7},{7,6},{8,9},{9,8},{10,11... | collective-permute-start | bytes 688136 | tf_op jit(solution)/shard_map/ppermute | solution.py:148
  15.8 16.6 %collective-permute-start.2 = (bf16[32,3584]{1,0:T(8,128)(2,1)S(1)}, bf16[32,3584]{1,0:T(8,128)(2,1)S(1)}, u32[]{:S(2)}, u32[]{:S(2)}) collective-permute-start(bf16[32,3584]{1,0:T(8,128)(2,1)S(1)} %collective-permute-done.1), channel_id=1, source_target_pairs={{0,1},{1,0},{2,3},{3,2},{4,5},{5,4},{6,7},{7,6},{8,9},{9,8},{10,11... | collective-permute-start | bytes 688136 | tf_op jit(solution)/shard_map/ppermute | solution.py:148
  16.3 5.6 %collective-permute-start.3 = (f32[]{:T(128)}, f32[]{:T(128)}, u32[]{:S(2)}, u32[]{:S(2)}) collective-permute-start(f32[]{:T(128)} %bitcast.2), channel_id=1, source_target_pairs={{0,4},{4,0},{8,12},{12,8},{16,20},{20,16},{24,28},{28,24},{1,5},{5... | collective-permute-start | bytes 20 | tf_op jit(solution)/shard_map/ppermute | solution.py:137
  17.7 22.0 %collective-permute-start.7 = (bf16[3,128,512]{2,1,0:T(8,128)(2,1)S(1)}, bf16[3,128,512]{2,1,0:T(8,128)(2,1)S(1)}, u32[]{:S(2)}, u32[]{:S(2)}) collective-permute-start(bf16[3,128,512]{2,1,0:T(8,128)(2,1)S(1)} %get-tuple-element.30), channel_id=1, source_target_pairs={{0,1},{1,0},{2,3},{3,2},{4,5},{5,4},{6,7},{7,6},{8,9},{9,8},{10,11... | collective-permute-start | bytes 1179656 | tf_op jit(solution)/shard_map/ppermute | solution.py:496
  19.2 17.9 %collective-permute-start.8 = (bf16[1,128,512]{2,1,0:T(8,128)(2,1)S(1)}, bf16[1,128,512]{2,1,0:T(8,128)(2,1)S(1)}, u32[]{:S(2)}, u32[]{:S(2)}) collective-permute-start(bf16[1,128,512]{2,1,0:T(8,128)(2,1)S(1)} %get-tuple-element.31), channel_id=1, source_target_pairs={{0,2},{1,3},{2,0},{3,1},{4,6},{5,7},{6,4},{7,5},{8,10},{9,11},{10,... | collective-permute-start | bytes 393224 | tf_op jit(solution)/shard_map/ppermute | solution.py:496
  22.5 3.6 %collective-permute-start.4 = (f32[]{:T(128)}, f32[]{:T(128)}, u32[]{:S(2)}, u32[]{:S(2)}) collective-permute-start(f32[]{:T(128)} %add.9), channel_id=1, source_target_pairs={{0,8},{4,12},{8,0},{12,4},{16,24},{20,28},{24,16},{28,20},{1,9},{5... | collective-permute-start | bytes 20 | tf_op jit(solution)/shard_map/ppermute | solution.py:137
  26.7 3.6 %collective-permute-start.5 = (f32[]{:T(128)}, f32[]{:T(128)}, u32[]{:S(2)}, u32[]{:S(2)}) collective-permute-start(f32[]{:T(128)} %add.10), channel_id=1, source_target_pairs={{0,16},{4,20},{8,24},{12,28},{16,0},{20,4},{24,8},{28,12},{1,17},{... | collective-permute-start | bytes 20 | tf_op jit(solution)/shard_map/ppermute | solution.py:137
  30.3 9.4 %collective-permute-start.9 = (bf16[1,128,512]{2,1,0:T(8,128)(2,1)S(1)}, bf16[1,128,512]{2,1,0:T(8,128)(2,1)S(1)}, u32[]{:S(2)}, u32[]{:S(2)}) collective-permute-start(bf16[1,128,512]{2,1,0:T(8,128)(2,1)S(1)} %get-tuple-element.32), channel_id=1, source_target_pairs={{0,3},{1,2},{2,1},{3,0},{4,7},{5,6},{6,5},{7,4},{8,11},{9,10},{10,... | collective-permute-start | bytes 393224 | tf_op jit(solution)/shard_map/ppermute | solution.py:496
  35.1 8.8 %collective-permute-start.6 = (bf16[128,256]{1,0:T(8,128)(2,1)S(1)}, bf16[128,256]{1,0:T(8,128)(2,1)S(1)}, u32[]{:S(2)}, u32[]{:S(2)}) collective-permute-start(bf16[128,256]{1,0:T(8,128)(2,1)S(1)} %slice.4), channel_id=1, source_target_pairs={{0,2},{1,3},{2,0},{3,1},{4,6},{5,7},{6,4},{7,5},{8,10},{9,11},{10,... | collective-permute-start | bytes 196616 | tf_op jit(solution)/shard_map/ppermute | solution.py:517
  47.6 5.8 %collective-permute-start.10 = (f32[4,2,512]{2,1,0:T(2,128)S(1)}, f32[4,2,512]{2,1,0:T(2,128)S(1)}, u32[]{:S(2)}, u32[]{:S(2)}) collective-permute-start(f32[4,2,512]{2,1,0:T(2,128)S(1)} %shard_map.113.refs_6_), channel_id=1, source_target_pairs={{0,2},{1,3},{2,0},{3,1},{4,6},{5,7},{6,4},{7,5},{8,10},{9,11},{10,... | collective-permute-start | bytes 49160 | tf_op jit(solution)/shard_map/ppermute | solution.py:525
  49.0 10.6 %collective-permute-start.14 = (bf16[3,128,256]{2,1,0:T(8,128)(2,1)S(1)}, bf16[3,128,256]{2,1,0:T(8,128)(2,1)S(1)}, u32[]{:S(2)}, u32[]{:S(2)}) collective-permute-start(bf16[3,128,256]{2,1,0:T(8,128)(2,1)S(1)} %get-tuple-element.38), channel_id=1, source_target_pairs={{0,1},{1,0},{2,3},{3,2},{4,5},{5,4},{6,7},{7,6},{8,9},{9,8},{10,11... | collective-permute-start | bytes 589832 | tf_op jit(solution)/shard_map/ppermute | solution.py:496
  50.4 16.4 %collective-permute-start.15 = (bf16[3,128,256]{2,1,0:T(8,128)(2,1)S(1)}, bf16[3,128,256]{2,1,0:T(8,128)(2,1)S(1)}, u32[]{:S(2)}, u32[]{:S(2)}) collective-permute-start(bf16[3,128,256]{2,1,0:T(8,128)(2,1)S(1)} %get-tuple-element.39), channel_id=1, source_target_pairs={{0,2},{1,3},{2,0},{3,1},{4,6},{5,7},{6,4},{7,5},{8,10},{9,11},{10,... | collective-permute-start | bytes 589832 | tf_op jit(solution)/shard_map/ppermute | solution.py:496
  52.0 15.6 %collective-permute-start.16 = (bf16[3,128,256]{2,1,0:T(8,128)(2,1)S(1)}, bf16[3,128,256]{2,1,0:T(8,128)(2,1)S(1)}, u32[]{:S(2)}, u32[]{:S(2)}) collective-permute-start(bf16[3,128,256]{2,1,0:T(8,128)(2,1)S(1)} %get-tuple-element.40), channel_id=1, source_target_pairs={{0,3},{1,2},{2,1},{3,0},{4,7},{5,6},{6,5},{7,4},{8,11},{9,10},{10,... | collective-permute-start | bytes 589832 | tf_op jit(solution)/shard_map/ppermute | solution.py:496
  59.0 43.0 %collective-permute-start.11 = (bf16[3,128,512]{2,1,0:T(8,128)(2,1)S(1)}, bf16[3,128,512]{2,1,0:T(8,128)(2,1)S(1)}, u32[]{:S(2)}, u32[]{:S(2)}) collective-permute-start(bf16[3,128,512]{2,1,0:T(8,128)(2,1)S(1)} %get-tuple-element.34), channel_id=1, source_target_pairs={{0,1},{1,0},{2,3},{3,2},{4,5},{5,4},{6,7},{7,6},{8,9},{9,8},{10,11... | collective-permute-start | bytes 1179656 | tf_op jit(solution)/shard_map/ppermute | solution.py:496
  69.6 8.0 %collective-permute-start.20 = (bf16[3,128,128]{2,1,0:T(8,128)(2,1)S(1)}, bf16[3,128,128]{2,1,0:T(8,128)(2,1)S(1)}, u32[]{:S(2)}, u32[]{:S(2)}) collective-permute-start(bf16[3,128,128]{2,1,0:T(8,128)(2,1)S(1)} %get-tuple-element.46), channel_id=1, source_target_pairs={{0,1},{1,0},{2,3},{3,2},{4,5},{5,4},{6,7},{7,6},{8,9},{9,8},{10,11... | collective-permute-start | bytes 294920 | tf_op jit(solution)/shard_map/ppermute | solution.py:496
  72.0 10.1 %collective-permute-start.21 = (bf16[3,128,128]{2,1,0:T(8,128)(2,1)S(1)}, bf16[3,128,128]{2,1,0:T(8,128)(2,1)S(1)}, u32[]{:S(2)}, u32[]{:S(2)}) collective-permute-start(bf16[3,128,128]{2,1,0:T(8,128)(2,1)S(1)} %get-tuple-element.47), channel_id=1, source_target_pairs={{0,2},{1,3},{2,0},{3,1},{4,6},{5,7},{6,4},{7,5},{8,10},{9,11},{10,... | collective-permute-start | bytes 294920 | tf_op jit(solution)/shard_map/ppermute | solution.py:496
  73.5 12.0 %collective-permute-start.22 = (bf16[3,128,128]{2,1,0:T(8,128)(2,1)S(1)}, bf16[3,128,128]{2,1,0:T(8,128)(2,1)S(1)}, u32[]{:S(2)}, u32[]{:S(2)}) collective-permute-start(bf16[3,128,128]{2,1,0:T(8,128)(2,1)S(1)} %get-tuple-element.48), channel_id=1, source_target_pairs={{0,3},{1,2},{2,1},{3,0},{4,7},{5,6},{6,5},{7,4},{8,11},{9,10},{10,... | collective-permute-start | bytes 294920 | tf_op jit(solution)/shard_map/ppermute | solution.py:496
  76.9 13.0 %collective-permute-start.17 = (bf16[3,128,128]{2,1,0:T(8,128)(2,1)S(1)}, bf16[3,128,128]{2,1,0:T(8,128)(2,1)S(1)}, u32[]{:S(2)}, u32[]{:S(2)}) collective-permute-start(bf16[3,128,128]{2,1,0:T(8,128)(2,1)S(1)} %get-tuple-element.42), channel_id=1, source_target_pairs={{0,1},{1,0},{2,3},{3,2},{4,5},{5,4},{6,7},{7,6},{8,9},{9,8},{10,11... | collective-permute-start | bytes 294920 | tf_op jit(solution)/shard_map/ppermute | solution.py:496
  77.6 24.4 %collective-permute-start.12 = (bf16[1,128,512]{2,1,0:T(8,128)(2,1)S(1)}, bf16[1,128,512]{2,1,0:T(8,128)(2,1)S(1)}, u32[]{:S(2)}, u32[]{:S(2)}) collective-permute-start(bf16[1,128,512]{2,1,0:T(8,128)(2,1)S(1)} %get-tuple-element.35), channel_id=1, source_target_pairs={{0,2},{1,3},{2,0},{3,1},{4,6},{5,7},{6,4},{7,5},{8,10},{9,11},{10,... | collective-permute-start | bytes 393224 | tf_op jit(solution)/shard_map/ppermute | solution.py:496
  82.1 19.8 %collective-permute-start.13 = (bf16[1,128,512]{2,1,0:T(8,128)(2,1)S(1)}, bf16[1,128,512]{2,1,0:T(8,128)(2,1)S(1)}, u32[]{:S(2)}, u32[]{:S(2)}) collective-permute-start(bf16[1,128,512]{2,1,0:T(8,128)(2,1)S(1)} %get-tuple-element.36), channel_id=1, source_target_pairs={{0,3},{1,2},{2,1},{3,0},{4,7},{5,6},{6,5},{7,4},{8,11},{9,10},{10,... | collective-permute-start | bytes 393224 | tf_op jit(solution)/shard_map/ppermute | solution.py:496
  85.4 15.7 %collective-permute-start.18 = (bf16[3,128,128]{2,1,0:T(8,128)(2,1)S(1)}, bf16[3,128,128]{2,1,0:T(8,128)(2,1)S(1)}, u32[]{:S(2)}, u32[]{:S(2)}) collective-permute-start(bf16[3,128,128]{2,1,0:T(8,128)(2,1)S(1)} %get-tuple-element.43), channel_id=1, source_target_pairs={{0,2},{1,3},{2,0},{3,1},{4,6},{5,7},{6,4},{7,5},{8,10},{9,11},{10,... | collective-permute-start | bytes 294920 | tf_op jit(solution)/shard_map/ppermute | solution.py:496
  89.8 11.3 %collective-permute-start.19 = (bf16[3,128,128]{2,1,0:T(8,128)(2,1)S(1)}, bf16[3,128,128]{2,1,0:T(8,128)(2,1)S(1)}, u32[]{:S(2)}, u32[]{:S(2)}) collective-permute-start(bf16[3,128,128]{2,1,0:T(8,128)(2,1)S(1)} %get-tuple-element.44), channel_id=1, source_target_pairs={{0,3},{1,2},{2,1},{3,0},{4,7},{5,6},{6,5},{7,4},{8,11},{9,10},{10,... | collective-permute-start | bytes 294920 | tf_op jit(solution)/shard_map/ppermute | solution.py:496

commit v6 on v5

--- a/solution.py
+++ b/solution.py
@@ -201,7 +201,7 @@
         dq_s[at] = (dq * scale).T.astype(jnp.bfloat16)
         return carry
 
-    lax.fori_loop(0, length // chunk, step, 0)
+    lax.fori_loop(0, length // chunk, step, 0, unroll=length <= 2 * chunk)
     for j, out in enumerate(outs):
         at = pl.ds(j * rows, rows)
         out[0] = dq_s[at]
@@ -289,7 +289,7 @@
         )
         return carry
 
-    lax.fori_loop(0, q_s.shape[0] // chunk, step, 0)
+    lax.fori_loop(0, q_s.shape[0] // chunk, step, 0, unroll=q_s.shape[0] <= 2 * chunk)
 
 
 def half_grads_kernel(count, scale, chunk, *refs):
@@ -326,7 +326,7 @@
         dq_s[at] = (dq * scale).T.astype(jnp.bfloat16)
         return carry
 
-    lax.fori_loop(0, length // chunk, step, 0)
+    lax.fori_loop(0, length // chunk, step, 0, unroll=length <= 2 * chunk)
     for j, out in enumerate(outs):
         at = pl.ds(j * rows, rows)
         out[0] = dq_s[at]
@@ -498,11 +498,14 @@
 
     visual_grad = visual_grads(place_of, visual_pos, rm_hidden, rm_cotangent, rm_gain)
     visual_blocks = gathered(visual_grad, "tensor")
-    blocks = exchange(pack(place_of, own, 0, whole * HD, (0,), (3,) * count))
     if shared:
         taken = (3,) * half + (1,) * half
         packed = pack(place_of, own, whole * HD, shared * HD, (0, half), taken)
         half_blocks = exchange(packed)
+    whole_blocks = [
+        exchange(pack(place_of, own, g * HD, HD, (0,), (3,) * count))
+        for g in range(whole)
+    ]
 
     reward_sum = total_over(jnp.sum(rewards), "dp")
     sample_count = lax.axis_size("dp") * rewards.shape[0]
@@ -518,7 +521,7 @@
 
     outs = ()
     for g in range(whole):
-        parts = exchange(attend(handed, blocks, g, g, 1))
+        parts = exchange(attend(handed, whole_blocks[g], g, 0, 1))
         outs = place(place_of, parts, outs, img_query.shape, g * HD)
     if shared:
         stats = half_call(half_stats_kernel, handed, far_handed, half_blocks, (), whole)

time: 105 us -> 104 us (level)
  waiting for transfers between devices: 35.4 us -> 41.7 us
  starting transfers between devices: 41.1 us -> 36.2 us
  Pallas kernels: 20.4 us -> 18.3 us
    ppermute x15 -> x18, waiting for transfers between devices: 19.8 us -> 25.5 us  [exchange(): lax.ppermute(blocks[k], 'tensor', partners(count, k))]
    ppermute x15 -> x18, starting transfers between devices: 29.3 us -> 24.5 us  [exchange(): lax.ppermute(blocks[k], 'tensor', partners(count, k))]
    pallas_call x2, Pallas kernels: 9.3 us -> 7.01 us  [half_call(): pl.pallas_call(functools.partial(kernel, count, HD ** (-0.5), chunk), gri...]
    pallas_call x2 -> x3, Pallas kernels: 2.67 us -> 3.49 us  [pack(): pl.pallas_call(functools.partial(pack_kernel, count, first, slots), in_sp...]
  transfers between devices with their start and end apart: 23 -> 26, of which waited for: 9 -> 12; matrix products, arithmetic and copies ran while one was open for 3% -> 3% of each run, Pallas kernels for 14% -> 12%
where the time goes in v6:
time: 104 us; the launch traced here: 102 us
  waiting for transfers between devices  41.7 us (40%)
  starting transfers between devices  36.2 us (35%)
  Pallas kernels  18.3 us (18%)
  between operations  3.34 us (3%)
  matrix products  2.68 us (3%)
    ppermute x18, waiting for transfers between devices, exchange(): lax.ppermute(blocks[k], 'tensor', partners(count, k))  25.5 us
    ppermute x18, starting transfers between devices, exchange(): lax.ppermute(blocks[k], 'tensor', partners(count, k))  24.5 us
    ppermute x3, waiting for transfers between devices, gathered(): held[k ^ step] = lax.ppermute(held[k], axis, partners(size, step))  9.1 us
    pallas_call x2, Pallas kernels, half_call(): pl.pallas_call(functools.partial(kernel, count, HD ** (-0.5), chunk), gri...  7.01 us
    ppermute x3, starting transfers between devices, gathered(): held[k ^ step] = lax.ppermute(held[k], axis, partners(size, step))  4.8 us
    ppermute x3, starting transfers between devices, total_over(): value = value + lax.ppermute(value, axis, partners(size, step))  4.78 us
    ppermute x1, waiting for transfers between devices, work(): lax.ppermute(handed[:, whole * HD:], 'tensor', partners(count, half))  4.11 us
    pallas_call x3, Pallas kernels, pack(): pl.pallas_call(functools.partial(pack_kernel, count, first, slots), in_sp...  3.49 us
  transfers between devices with their start and end apart: 26, of which 12 were waited for; matrix products, arithmetic and copies ran while one was open for 3% of the time, Pallas kernels for 12%

profile of v6, /device:TPU:2, one launch (start us, length us, event | category | flops | bytes accessed | tf_op | source)
XLA Modules:
  0.0 102.3 jit_solution(5098466413803499103)
XLA Ops:
  0.6 1.8 %visual.1 = bf16[32,3584]{1,0:T(8,128)(2,1)S(1)} custom-call(s32[1]{0:T(128)} %bitcast.here_ref.refs_0_, s32[1,32]{1,0:T(1,128)} %pos_hbm.1, f32[28,128]{1,0:T(8,128)} %bitcast.6, bf16[1,64,3584]{2,1,0:T(8,128)(2,1)} %hidden_hbm.1, bf16[1,64,3584]{2,1,0:T(8,128)(2,1)} %cot_hbm.1), custom_call_target="tpu_custom_call" | custom-call | flops 29360128 | bytes 917504 | tf_op jit(solution)/shard_map/visual/pallas_call | solution.py:66
  2.4 2.7 %collective-permute-start.1 = (bf16[32,3584]{1,0:T(8,128)(2,1)S(1)}, bf16[32,3584]{1,0:T(8,128)(2,1)S(1)}, u32[]{:S(2)}, u32[]{:S(2)}) collective-permute-start(bf16[32,3584]{1,0:T(8,128)(2,1)S(1)} %visual.1), channel_id=1, source_target_pairs={{0,2},{1,3},{2,0},{3,1},{4,6},{5,7},{6,4},{7,5},{8,10},{9,11},{10,... | collective-permute-start | bytes 688136 | tf_op jit(solution)/shard_map/ppermute | solution.py:148
  5.1 1.6 %collective-permute-start = (bf16[32,3584]{1,0:T(8,128)(2,1)S(1)}, bf16[32,3584]{1,0:T(8,128)(2,1)S(1)}, u32[]{:S(2)}, u32[]{:S(2)}) collective-permute-start(bf16[32,3584]{1,0:T(8,128)(2,1)S(1)} %visual.1), channel_id=1, source_target_pairs={{0,1},{1,0},{2,3},{3,2},{4,5},{5,4},{6,7},{7,6},{8,9},{9,8},{10,11... | collective-permute-start | bytes 688136 | tf_op jit(solution)/shard_map/ppermute | solution.py:148
  6.7 9.1 %collective-permute-done.1 = bf16[32,3584]{1,0:T(8,128)(2,1)S(1)} collective-permute-done((bf16[32,3584]{1,0:T(8,128)(2,1)S(1)}, bf16[32,3584]{1,0:T(8,128)(2,1)S(1)}, u32[]{:S(2)}, u32[]{:S(2)}) %collective-permute-start.1) | collective-permute-done | bytes 229408 | tf_op jit(solution)/shard_map/ppermute | solution.py:148
  16.3 1.4 %shard_map.112 = (bf16[3,128,512]{2,1,0:T(8,128)(2,1)S(1)}, bf16[3,128,512]{2,1,0:T(8,128)(2,1)S(1)}, bf16[1,128,512]{2,1,0:T(8,128)(2,1)S(1)}, bf16[1,128,512]{2,1,0:T(8,128)(2,1)S(1)}) custom-call(s32[1]{0:T(128)} %bitcast.here_ref.refs_0_, bf16[1,128,2048]{2,1,0:T(8,128)(2,1)} %refs_0_.5, bf16[1,128,2048]{2,1,0:T(8,128)(2,1)} %refs_1_.5, ...), custom_call_target="tpu_custom_call" | custom-call | bytes 2097152 | tf_op jit(solution)/shard_map/pallas_call | solution.py:111
  17.7 1.5 %collective-permute-start.7 = (bf16[3,128,512]{2,1,0:T(8,128)(2,1)S(1)}, bf16[3,128,512]{2,1,0:T(8,128)(2,1)S(1)}, u32[]{:S(2)}, u32[]{:S(2)}) collective-permute-start(bf16[3,128,512]{2,1,0:T(8,128)(2,1)S(1)} %get-tuple-element.34), channel_id=1, source_target_pairs={{0,1},{1,0},{2,3},{3,2},{4,5},{5,4},{6,7},{7,6},{8,9},{9,8},{10,11... | collective-permute-start | bytes 1179656 | tf_op jit(solution)/shard_map/ppermute | solution.py:496
  19.2 2.0 %collective-permute-start.8 = (bf16[1,128,512]{2,1,0:T(8,128)(2,1)S(1)}, bf16[1,128,512]{2,1,0:T(8,128)(2,1)S(1)}, u32[]{:S(2)}, u32[]{:S(2)}) collective-permute-start(bf16[1,128,512]{2,1,0:T(8,128)(2,1)S(1)} %get-tuple-element.35), channel_id=1, source_target_pairs={{0,2},{1,3},{2,0},{3,1},{4,6},{5,7},{6,4},{7,5},{8,10},{9,11},{10,... | collective-permute-start | bytes 393224 | tf_op jit(solution)/shard_map/ppermute | solution.py:496
  22.5 1.9 %collective-permute-start.4 = (f32[]{:T(128)}, f32[]{:T(128)}, u32[]{:S(2)}, u32[]{:S(2)}) collective-permute-start(f32[]{:T(128)} %add.9), channel_id=1, source_target_pairs={{0,8},{4,12},{8,0},{12,4},{16,24},{20,28},{24,16},{28,20},{1,9},{5... | collective-permute-start | bytes 20 | tf_op jit(solution)/shard_map/ppermute | solution.py:137
  24.4 1.7 %collective-permute-done.4 = f32[]{:T(128)} collective-permute-done((f32[]{:T(128)}, f32[]{:T(128)}, u32[]{:S(2)}, u32[]{:S(2)}) %collective-permute-start.4) | collective-permute-done | bytes 36 | tf_op jit(solution)/shard_map/ppermute | solution.py:137
  26.7 2.9 %collective-permute-start.5 = (f32[]{:T(128)}, f32[]{:T(128)}, u32[]{:S(2)}, u32[]{:S(2)}) collective-permute-start(f32[]{:T(128)} %add.10), channel_id=1, source_target_pairs={{0,16},{4,20},{8,24},{12,28},{16,0},{20,4},{24,8},{28,12},{1,17},{... | collective-permute-start | bytes 20 | tf_op jit(solution)/shard_map/ppermute | solution.py:137
  30.3 1.4 %collective-permute-start.9 = (bf16[1,128,512]{2,1,0:T(8,128)(2,1)S(1)}, bf16[1,128,512]{2,1,0:T(8,128)(2,1)S(1)}, u32[]{:S(2)}, u32[]{:S(2)}) collective-permute-start(bf16[1,128,512]{2,1,0:T(8,128)(2,1)S(1)} %get-tuple-element.36), channel_id=1, source_target_pairs={{0,3},{1,2},{2,1},{3,0},{4,7},{5,6},{6,5},{7,4},{8,11},{9,10},{10,... | collective-permute-start | bytes 393224 | tf_op jit(solution)/shard_map/ppermute | solution.py:496
  32.4 2.7 %fusion.refs_0_ = bf16[128,512]{1,0:T(8,128)(2,1)S(1)} fusion(bf16[3584,512]{1,0:T(8,128)(2,1)} %param.14, bf16[32,3584]{1,0:T(8,128)(2,1)S(1)} %collective-permute-done.2, bf16[32,3584]{1,0:T(8,128)(2,1)S(1)} %collective-permute-done.1, bf16[32,3584]{1,0:T(8,128)(2,1)S(1)} %collective-permute-done, bf16[32,3584]{1,0:T(8,128)(2,1)S(1)} %visual.1, f32[]{:T(128)S(6)} %div.3), kind=kOutput, calls=%fused_computation.1 | convolution fusion | flops 473563136 | bytes 4718596 | tf_op jit(solution)/shard_map/dot_general | solution.py:514
  35.1 2.1 %collective-permute-start.6 = (bf16[128,256]{1,0:T(8,128)(2,1)S(1)}, bf16[128,256]{1,0:T(8,128)(2,1)S(1)}, u32[]{:S(2)}, u32[]{:S(2)}) collective-permute-start(bf16[128,256]{1,0:T(8,128)(2,1)S(1)} %slice.4), channel_id=1, source_target_pairs={{0,2},{1,3},{2,0},{3,1},{4,6},{5,7},{6,4},{7,5},{8,10},{9,11},{10,... | collective-permute-start | bytes 196616 | tf_op jit(solution)/shard_map/ppermute | solution.py:520
  37.2 2.6 %collective-permute-done.9.refs_5_ = bf16[1,128,512]{2,1,0:T(8,128)(2,1)S(1)} collective-permute-done((bf16[1,128,512]{2,1,0:T(8,128)(2,1)S(1)}, bf16[1,128,512]{2,1,0:T(8,128)(2,1)S(1)}, u32[]{:S(2)}, u32[]{:S(2)}) %collective-permute-start.9) | collective-permute-done | bytes 131104 | tf_op jit(solution)/shard_map/ppermute | solution.py:496
  39.7 4.1 %collective-permute-done.6.refs_1_ = bf16[128,256]{1,0:T(8,128)(2,1)S(1)} collective-permute-done((bf16[128,256]{1,0:T(8,128)(2,1)S(1)}, bf16[128,256]{1,0:T(8,128)(2,1)S(1)}, u32[]{:S(2)}, u32[]{:S(2)}) %collective-permute-start.6) | collective-permute-done | bytes 65568 | tf_op jit(solution)/shard_map/ppermute | solution.py:520
  43.8 2.8 %shard_map.113.refs_6_ = f32[4,2,512]{2,1,0:T(2,128)S(1)} custom-call(bf16[128,512]{1,0:T(8,128)(2,1)S(1)} %fusion.refs_0_, bf16[128,256]{1,0:T(8,128)(2,1)S(1)} %collective-permute-done.6.refs_1_, bf16[3,128,512]{2,1,0:T(8,128)(2,1)S(1)} %get-tuple-element.33.refs_2_, bf16[3,128,512]{2,1,0:T(8,128)(2,1)S(1)} %collective-permute-done.7.refs_3_, ...), custom_call_target="tpu_custom_call" | custom-call | flops 268435456 | bytes 3145728 | tf_op jit(solution)/shard_map/pallas_call | solution.py:359
  47.8 1.5 %collective-permute-start.20 = (bf16[3,128,128]{2,1,0:T(8,128)(2,1)S(1)}, bf16[3,128,128]{2,1,0:T(8,128)(2,1)S(1)}, u32[]{:S(2)}, u32[]{:S(2)}) collective-permute-start(bf16[3,128,128]{2,1,0:T(8,128)(2,1)S(1)} %get-tuple-element.50), channel_id=1, source_target_pairs={{0,1},{1,0},{2,3},{3,2},{4,5},{5,4},{6,7},{7,6},{8,9},{9,8},{10,11... | collective-permute-start | bytes 294920 | tf_op jit(solution)/shard_map/ppermute | solution.py:496
  49.2 1.6 %collective-permute-start.21 = (bf16[3,128,128]{2,1,0:T(8,128)(2,1)S(1)}, bf16[3,128,128]{2,1,0:T(8,128)(2,1)S(1)}, u32[]{:S(2)}, u32[]{:S(2)}) collective-permute-start(bf16[3,128,128]{2,1,0:T(8,128)(2,1)S(1)} %get-tuple-element.51), channel_id=1, source_target_pairs={{0,2},{1,3},{2,0},{3,1},{4,6},{5,7},{6,4},{7,5},{8,10},{9,11},{10,... | collective-permute-start | bytes 294920 | tf_op jit(solution)/shard_map/ppermute | solution.py:496
  51.4 4.2 %shard_map.114 = (bf16[3,128,512]{2,1,0:T(8,128)(2,1)S(1)}, bf16[3,128,512]{2,1,0:T(8,128)(2,1)S(1)}, bf16[1,128,512]{2,1,0:T(8,128)(2,1)S(1)}, bf16[1,128,512]{2,1,0:T(8,128)(2,1)S(1)}) custom-call(bf16[128,512]{1,0:T(8,128)(2,1)S(1)} %fusion.refs_0_, bf16[128,256]{1,0:T(8,128)(2,1)S(1)} %collective-permute-done.6.refs_1_, ...), custom_call_target="tpu_custom_call" | custom-call | flops 671088640 | bytes 3145728 | tf_op jit(solution)/shard_map/pallas_call | solution.py:359
  55.6 1.4 %collective-permute-start.11 = (bf16[3,128,512]{2,1,0:T(8,128)(2,1)S(1)}, bf16[3,128,512]{2,1,0:T(8,128)(2,1)S(1)}, u32[]{:S(2)}, u32[]{:S(2)}) collective-permute-start(bf16[3,128,512]{2,1,0:T(8,128)(2,1)S(1)} %get-tuple-element.38), channel_id=1, source_target_pairs={{0,1},{1,0},{2,3},{3,2},{4,5},{5,4},{6,7},{7,6},{8,9},{9,8},{10,11... | collective-permute-start | bytes 1179656 | tf_op jit(solution)/shard_map/ppermute | solution.py:496
  59.1 3.5 %collective-permute-start.15 = (bf16[3,128,128]{2,1,0:T(8,128)(2,1)S(1)}, bf16[3,128,128]{2,1,0:T(8,128)(2,1)S(1)}, u32[]{:S(2)}, u32[]{:S(2)}) collective-permute-start(bf16[3,128,128]{2,1,0:T(8,128)(2,1)S(1)} %get-tuple-element.43), channel_id=1, source_target_pairs={{0,2},{1,3},{2,0},{3,1},{4,6},{5,7},{6,4},{7,5},{8,10},{9,11},{10,... | collective-permute-start | bytes 294920 | tf_op jit(solution)/shard_map/ppermute | solution.py:496
  63.4 6.7 %collective-permute-done.22.refs_4_ = bf16[3,128,128]{2,1,0:T(8,128)(2,1)S(1)} collective-permute-done((bf16[3,128,128]{2,1,0:T(8,128)(2,1)S(1)}, bf16[3,128,128]{2,1,0:T(8,128)(2,1)S(1)}, u32[]{:S(2)}, u32[]{:S(2)}) %collective-permute-start.22) | collective-permute-done | bytes 98336 | tf_op jit(solution)/shard_map/ppermute | solution.py:496
  70.1 1.7 %shard_map.118 = (bf16[3,128,128]{2,1,0:T(8,128)(2,1)S(1)}, bf16[3,128,128]{2,1,0:T(8,128)(2,1)S(1)}, bf16[3,128,128]{2,1,0:T(8,128)(2,1)S(1)}, bf16[3,128,128]{2,1,0:T(8,128)(2,1)S(1)}) custom-call(bf16[128,512]{1,0:T(8,128)(2,1)S(1)} %fusion.refs_0_, bf16[3,128,128]{2,1,0:T(8,128)(2,1)S(1)} %get-tuple-element.49.refs_1_, ...), custom_call_target="tpu_custom_call" | custom-call | flops 335544320 | bytes 786432 | tf_op jit(solution)/shard_map/pallas_call | solution.py:219
  71.9 2.2 %collective-permute-done.14.refs_2_ = bf16[3,128,128]{2,1,0:T(8,128)(2,1)S(1)} collective-permute-done((bf16[3,128,128]{2,1,0:T(8,128)(2,1)S(1)}, bf16[3,128,128]{2,1,0:T(8,128)(2,1)S(1)}, u32[]{:S(2)}, u32[]{:S(2)}) %collective-permute-start.14) | collective-permute-done | bytes 98336 | tf_op jit(solution)/shard_map/ppermute | solution.py:496
  74.1 1.3 %collective-permute-start.24 = (bf16[3,128,128]{2,1,0:T(8,128)(2,1)S(1)}, bf16[3,128,128]{2,1,0:T(8,128)(2,1)S(1)}, u32[]{:S(2)}, u32[]{:S(2)}) collective-permute-start(bf16[3,128,128]{2,1,0:T(8,128)(2,1)S(1)} %get-tuple-element.55), channel_id=1, source_target_pairs={{0,2},{1,3},{2,0},{3,1},{4,6},{5,7},{6,4},{7,5},{8,10},{9,11},{10,... | collective-permute-start | bytes 294920 | tf_op jit(solution)/shard_map/ppermute | solution.py:496
  76.5 1.7 %shard_map.116 = (bf16[3,128,128]{2,1,0:T(8,128)(2,1)S(1)}, bf16[3,128,128]{2,1,0:T(8,128)(2,1)S(1)}, bf16[3,128,128]{2,1,0:T(8,128)(2,1)S(1)}, bf16[3,128,128]{2,1,0:T(8,128)(2,1)S(1)}) custom-call(bf16[128,512]{1,0:T(8,128)(2,1)S(1)} %fusion.refs_0_, bf16[3,128,128]{2,1,0:T(8,128)(2,1)S(1)} %get-tuple-element.41.refs_1_, ...), custom_call_target="tpu_custom_call" | custom-call | flops 335544320 | bytes 786432 | tf_op jit(solution)/shard_map/pallas_call | solution.py:219
  78.2 1.1 %collective-permute-start.17 = (bf16[3,128,128]{2,1,0:T(8,128)(2,1)S(1)}, bf16[3,128,128]{2,1,0:T(8,128)(2,1)S(1)}, u32[]{:S(2)}, u32[]{:S(2)}) collective-permute-start(bf16[3,128,128]{2,1,0:T(8,128)(2,1)S(1)} %get-tuple-element.46), channel_id=1, source_target_pairs={{0,1},{1,0},{2,3},{3,2},{4,5},{5,4},{6,7},{7,6},{8,9},{9,8},{10,11... | collective-permute-start | bytes 294920 | tf_op jit(solution)/shard_map/ppermute | solution.py:496
  80.3 1.5 %collective-permute-start.12 = (bf16[1,128,512]{2,1,0:T(8,128)(2,1)S(1)}, bf16[1,128,512]{2,1,0:T(8,128)(2,1)S(1)}, u32[]{:S(2)}, u32[]{:S(2)}) collective-permute-start(bf16[1,128,512]{2,1,0:T(8,128)(2,1)S(1)} %get-tuple-element.39), channel_id=1, source_target_pairs={{0,2},{1,3},{2,0},{3,1},{4,6},{5,7},{6,4},{7,5},{8,10},{9,11},{10,... | collective-permute-start | bytes 393224 | tf_op jit(solution)/shard_map/ppermute | solution.py:496
  81.8 7.3 %collective-permute-done.24.refs_3_ = bf16[3,128,128]{2,1,0:T(8,128)(2,1)S(1)} collective-permute-done((bf16[3,128,128]{2,1,0:T(8,128)(2,1)S(1)}, bf16[3,128,128]{2,1,0:T(8,128)(2,1)S(1)}, u32[]{:S(2)}, u32[]{:S(2)}) %collective-permute-start.24) | collective-permute-done | bytes 98336 | tf_op jit(solution)/shard_map/ppermute | solution.py:496
  89.1 3.0 %collective-permute-start.18 = (bf16[3,128,128]{2,1,0:T(8,128)(2,1)S(1)}, bf16[3,128,128]{2,1,0:T(8,128)(2,1)S(1)}, u32[]{:S(2)}, u32[]{:S(2)}) collective-permute-start(bf16[3,128,128]{2,1,0:T(8,128)(2,1)S(1)} %get-tuple-element.47), channel_id=1, source_target_pairs={{0,2},{1,3},{2,0},{3,1},{4,6},{5,7},{6,4},{7,5},{8,10},{9,11},{10,... | collective-permute-start | bytes 294920 | tf_op jit(solution)/shard_map/ppermute | solution.py:496
  92.1 2.0 %collective-permute-start.19 = (bf16[3,128,128]{2,1,0:T(8,128)(2,1)S(1)}, bf16[3,128,128]{2,1,0:T(8,128)(2,1)S(1)}, u32[]{:S(2)}, u32[]{:S(2)}) collective-permute-start(bf16[3,128,128]{2,1,0:T(8,128)(2,1)S(1)} %get-tuple-element.48), channel_id=1, source_target_pairs={{0,3},{1,2},{2,1},{3,0},{4,7},{5,6},{6,5},{7,4},{8,11},{9,10},{10,... | collective-permute-start | bytes 294920 | tf_op jit(solution)/shard_map/ppermute | solution.py:496
  94.9 5.5 %collective-permute-done.18.refs_3_ = bf16[3,128,128]{2,1,0:T(8,128)(2,1)S(1)} collective-permute-done((bf16[3,128,128]{2,1,0:T(8,128)(2,1)S(1)}, bf16[3,128,128]{2,1,0:T(8,128)(2,1)S(1)}, u32[]{:S(2)}, u32[]{:S(2)}) %collective-permute-start.18) | collective-permute-done | bytes 98336 | tf_op jit(solution)/shard_map/ppermute | solution.py:496
  (33 shorter events, 10.8 us)
Async XLA Ops:
  2.4 13.3 %collective-permute-start.1 = (bf16[32,3584]{1,0:T(8,128)(2,1)S(1)}, bf16[32,3584]{1,0:T(8,128)(2,1)S(1)}, u32[]{:S(2)}, u32[]{:S(2)}) collective-permute-start(bf16[32,3584]{1,0:T(8,128)(2,1)S(1)} %visual.1), channel_id=1, source_target_pairs={{0,2},{1,3},{2,0},{3,1},{4,6},{5,7},{6,4},{7,5},{8,10},{9,11},{10,... | collective-permute-start | bytes 688136 | tf_op jit(solution)/shard_map/ppermute | solution.py:148
  5.1 27.3 %collective-permute-start = (bf16[32,3584]{1,0:T(8,128)(2,1)S(1)}, bf16[32,3584]{1,0:T(8,128)(2,1)S(1)}, u32[]{:S(2)}, u32[]{:S(2)}) collective-permute-start(bf16[32,3584]{1,0:T(8,128)(2,1)S(1)} %visual.1), channel_id=1, source_target_pairs={{0,1},{1,0},{2,3},{3,2},{4,5},{5,4},{6,7},{7,6},{8,9},{9,8},{10,11... | collective-permute-start | bytes 688136 | tf_op jit(solution)/shard_map/ppermute | solution.py:148
  15.8 16.6 %collective-permute-start.2 = (bf16[32,3584]{1,0:T(8,128)(2,1)S(1)}, bf16[32,3584]{1,0:T(8,128)(2,1)S(1)}, u32[]{:S(2)}, u32[]{:S(2)}) collective-permute-start(bf16[32,3584]{1,0:T(8,128)(2,1)S(1)} %collective-permute-done.1), channel_id=1, source_target_pairs={{0,1},{1,0},{2,3},{3,2},{4,5},{5,4},{6,7},{7,6},{8,9},{9,8},{10,11... | collective-permute-start | bytes 688136 | tf_op jit(solution)/shard_map/ppermute | solution.py:148
  16.3 5.6 %collective-permute-start.3 = (f32[]{:T(128)}, f32[]{:T(128)}, u32[]{:S(2)}, u32[]{:S(2)}) collective-permute-start(f32[]{:T(128)} %bitcast.2), channel_id=1, source_target_pairs={{0,4},{4,0},{8,12},{12,8},{16,20},{20,16},{24,28},{28,24},{1,5},{5... | collective-permute-start | bytes 20 | tf_op jit(solution)/shard_map/ppermute | solution.py:137
  17.7 22.0 %collective-permute-start.7 = (bf16[3,128,512]{2,1,0:T(8,128)(2,1)S(1)}, bf16[3,128,512]{2,1,0:T(8,128)(2,1)S(1)}, u32[]{:S(2)}, u32[]{:S(2)}) collective-permute-start(bf16[3,128,512]{2,1,0:T(8,128)(2,1)S(1)} %get-tuple-element.34), channel_id=1, source_target_pairs={{0,1},{1,0},{2,3},{3,2},{4,5},{5,4},{6,7},{7,6},{8,9},{9,8},{10,11... | collective-permute-start | bytes 1179656 | tf_op jit(solution)/shard_map/ppermute | solution.py:496
  19.2 17.9 %collective-permute-start.8 = (bf16[1,128,512]{2,1,0:T(8,128)(2,1)S(1)}, bf16[1,128,512]{2,1,0:T(8,128)(2,1)S(1)}, u32[]{:S(2)}, u32[]{:S(2)}) collective-permute-start(bf16[1,128,512]{2,1,0:T(8,128)(2,1)S(1)} %get-tuple-element.35), channel_id=1, source_target_pairs={{0,2},{1,3},{2,0},{3,1},{4,6},{5,7},{6,4},{7,5},{8,10},{9,11},{10,... | collective-permute-start | bytes 393224 | tf_op jit(solution)/shard_map/ppermute | solution.py:496
  22.5 3.6 %collective-permute-start.4 = (f32[]{:T(128)}, f32[]{:T(128)}, u32[]{:S(2)}, u32[]{:S(2)}) collective-permute-start(f32[]{:T(128)} %add.9), channel_id=1, source_target_pairs={{0,8},{4,12},{8,0},{12,4},{16,24},{20,28},{24,16},{28,20},{1,9},{5... | collective-permute-start | bytes 20 | tf_op jit(solution)/shard_map/ppermute | solution.py:137
  26.7 3.6 %collective-permute-start.5 = (f32[]{:T(128)}, f32[]{:T(128)}, u32[]{:S(2)}, u32[]{:S(2)}) collective-permute-start(f32[]{:T(128)} %add.10), channel_id=1, source_target_pairs={{0,16},{4,20},{8,24},{12,28},{16,0},{20,4},{24,8},{28,12},{1,17},{... | collective-permute-start | bytes 20 | tf_op jit(solution)/shard_map/ppermute | solution.py:137
  30.3 9.4 %collective-permute-start.9 = (bf16[1,128,512]{2,1,0:T(8,128)(2,1)S(1)}, bf16[1,128,512]{2,1,0:T(8,128)(2,1)S(1)}, u32[]{:S(2)}, u32[]{:S(2)}) collective-permute-start(bf16[1,128,512]{2,1,0:T(8,128)(2,1)S(1)} %get-tuple-element.36), channel_id=1, source_target_pairs={{0,3},{1,2},{2,1},{3,0},{4,7},{5,6},{6,5},{7,4},{8,11},{9,10},{10,... | collective-permute-start | bytes 393224 | tf_op jit(solution)/shard_map/ppermute | solution.py:496
  35.1 8.8 %collective-permute-start.6 = (bf16[128,256]{1,0:T(8,128)(2,1)S(1)}, bf16[128,256]{1,0:T(8,128)(2,1)S(1)}, u32[]{:S(2)}, u32[]{:S(2)}) collective-permute-start(bf16[128,256]{1,0:T(8,128)(2,1)S(1)} %slice.4), channel_id=1, source_target_pairs={{0,2},{1,3},{2,0},{3,1},{4,6},{5,7},{6,4},{7,5},{8,10},{9,11},{10,... | collective-permute-start | bytes 196616 | tf_op jit(solution)/shard_map/ppermute | solution.py:520
  46.6 4.8 %collective-permute-start.10 = (f32[4,2,512]{2,1,0:T(2,128)S(1)}, f32[4,2,512]{2,1,0:T(2,128)S(1)}, u32[]{:S(2)}, u32[]{:S(2)}) collective-permute-start(f32[4,2,512]{2,1,0:T(2,128)S(1)} %shard_map.113.refs_6_), channel_id=1, source_target_pairs={{0,2},{1,3},{2,0},{3,1},{4,6},{5,7},{6,4},{7,5},{8,10},{9,11},{10,... | collective-permute-start | bytes 49160 | tf_op jit(solution)/shard_map/ppermute | solution.py:528
  47.8 11.3 %collective-permute-start.20 = (bf16[3,128,128]{2,1,0:T(8,128)(2,1)S(1)}, bf16[3,128,128]{2,1,0:T(8,128)(2,1)S(1)}, u32[]{:S(2)}, u32[]{:S(2)}) collective-permute-start(bf16[3,128,128]{2,1,0:T(8,128)(2,1)S(1)} %get-tuple-element.50), channel_id=1, source_target_pairs={{0,1},{1,0},{2,3},{3,2},{4,5},{5,4},{6,7},{7,6},{8,9},{9,8},{10,11... | collective-permute-start | bytes 294920 | tf_op jit(solution)/shard_map/ppermute | solution.py:496
  49.2 13.4 %collective-permute-start.21 = (bf16[3,128,128]{2,1,0:T(8,128)(2,1)S(1)}, bf16[3,128,128]{2,1,0:T(8,128)(2,1)S(1)}, u32[]{:S(2)}, u32[]{:S(2)}) collective-permute-start(bf16[3,128,128]{2,1,0:T(8,128)(2,1)S(1)} %get-tuple-element.51), channel_id=1, source_target_pairs={{0,2},{1,3},{2,0},{3,1},{4,6},{5,7},{6,4},{7,5},{8,10},{9,11},{10,... | collective-permute-start | bytes 294920 | tf_op jit(solution)/shard_map/ppermute | solution.py:496
  55.6 45.6 %collective-permute-start.11 = (bf16[3,128,512]{2,1,0:T(8,128)(2,1)S(1)}, bf16[3,128,512]{2,1,0:T(8,128)(2,1)S(1)}, u32[]{:S(2)}, u32[]{:S(2)}) collective-permute-start(bf16[3,128,512]{2,1,0:T(8,128)(2,1)S(1)} %get-tuple-element.38), channel_id=1, source_target_pairs={{0,1},{1,0},{2,3},{3,2},{4,5},{5,4},{6,7},{7,6},{8,9},{9,8},{10,11... | collective-permute-start | bytes 1179656 | tf_op jit(solution)/shard_map/ppermute | solution.py:496
  57.1 13.0 %collective-permute-start.22 = (bf16[3,128,128]{2,1,0:T(8,128)(2,1)S(1)}, bf16[3,128,128]{2,1,0:T(8,128)(2,1)S(1)}, u32[]{:S(2)}, u32[]{:S(2)}) collective-permute-start(bf16[3,128,128]{2,1,0:T(8,128)(2,1)S(1)} %get-tuple-element.52), channel_id=1, source_target_pairs={{0,3},{1,2},{2,1},{3,0},{4,7},{5,6},{6,5},{7,4},{8,11},{9,10},{10,... | collective-permute-start | bytes 294920 | tf_op jit(solution)/shard_map/ppermute | solution.py:496
  59.0 15.1 %collective-permute-start.14 = (bf16[3,128,128]{2,1,0:T(8,128)(2,1)S(1)}, bf16[3,128,128]{2,1,0:T(8,128)(2,1)S(1)}, u32[]{:S(2)}, u32[]{:S(2)}) collective-permute-start(bf16[3,128,128]{2,1,0:T(8,128)(2,1)S(1)} %get-tuple-element.42), channel_id=1, source_target_pairs={{0,1},{1,0},{2,3},{3,2},{4,5},{5,4},{6,7},{7,6},{8,9},{9,8},{10,11... | collective-permute-start | bytes 294920 | tf_op jit(solution)/shard_map/ppermute | solution.py:496
  59.1 16.3 %collective-permute-start.15 = (bf16[3,128,128]{2,1,0:T(8,128)(2,1)S(1)}, bf16[3,128,128]{2,1,0:T(8,128)(2,1)S(1)}, u32[]{:S(2)}, u32[]{:S(2)}) collective-permute-start(bf16[3,128,128]{2,1,0:T(8,128)(2,1)S(1)} %get-tuple-element.43), channel_id=1, source_target_pairs={{0,2},{1,3},{2,0},{3,1},{4,6},{5,7},{6,4},{7,5},{8,10},{9,11},{10,... | collective-permute-start | bytes 294920 | tf_op jit(solution)/shard_map/ppermute | solution.py:496
  62.6 13.9 %collective-permute-start.16 = (bf16[3,128,128]{2,1,0:T(8,128)(2,1)S(1)}, bf16[3,128,128]{2,1,0:T(8,128)(2,1)S(1)}, u32[]{:S(2)}, u32[]{:S(2)}) collective-permute-start(bf16[3,128,128]{2,1,0:T(8,128)(2,1)S(1)} %get-tuple-element.44), channel_id=1, source_target_pairs={{0,3},{1,2},{2,1},{3,0},{4,7},{5,6},{6,5},{7,4},{8,11},{9,10},{10,... | collective-permute-start | bytes 294920 | tf_op jit(solution)/shard_map/ppermute | solution.py:496
  71.8 8.6 %collective-permute-start.23 = (bf16[3,128,128]{2,1,0:T(8,128)(2,1)S(1)}, bf16[3,128,128]{2,1,0:T(8,128)(2,1)S(1)}, u32[]{:S(2)}, u32[]{:S(2)}) collective-permute-start(bf16[3,128,128]{2,1,0:T(8,128)(2,1)S(1)} %get-tuple-element.54), channel_id=1, source_target_pairs={{0,1},{1,0},{2,3},{3,2},{4,5},{5,4},{6,7},{7,6},{8,9},{9,8},{10,11... | collective-permute-start | bytes 294920 | tf_op jit(solution)/shard_map/ppermute | solution.py:496
  74.1 15.0 %collective-permute-start.24 = (bf16[3,128,128]{2,1,0:T(8,128)(2,1)S(1)}, bf16[3,128,128]{2,1,0:T(8,128)(2,1)S(1)}, u32[]{:S(2)}, u32[]{:S(2)}) collective-permute-start(bf16[3,128,128]{2,1,0:T(8,128)(2,1)S(1)} %get-tuple-element.55), channel_id=1, source_target_pairs={{0,2},{1,3},{2,0},{3,1},{4,6},{5,7},{6,4},{7,5},{8,10},{9,11},{10,... | collective-permute-start | bytes 294920 | tf_op jit(solution)/shard_map/ppermute | solution.py:496
  75.4 13.7 %collective-permute-start.25 = (bf16[3,128,128]{2,1,0:T(8,128)(2,1)S(1)}, bf16[3,128,128]{2,1,0:T(8,128)(2,1)S(1)}, u32[]{:S(2)}, u32[]{:S(2)}) collective-permute-start(bf16[3,128,128]{2,1,0:T(8,128)(2,1)S(1)} %get-tuple-element.56), channel_id=1, source_target_pairs={{0,3},{1,2},{2,1},{3,0},{4,7},{5,6},{6,5},{7,4},{8,11},{9,10},{10,... | collective-permute-start | bytes 294920 | tf_op jit(solution)/shard_map/ppermute | solution.py:496
  78.2 13.9 %collective-permute-start.17 = (bf16[3,128,128]{2,1,0:T(8,128)(2,1)S(1)}, bf16[3,128,128]{2,1,0:T(8,128)(2,1)S(1)}, u32[]{:S(2)}, u32[]{:S(2)}) collective-permute-start(bf16[3,128,128]{2,1,0:T(8,128)(2,1)S(1)} %get-tuple-element.46), channel_id=1, source_target_pairs={{0,1},{1,0},{2,3},{3,2},{4,5},{5,4},{6,7},{7,6},{8,9},{9,8},{10,11... | collective-permute-start | bytes 294920 | tf_op jit(solution)/shard_map/ppermute | solution.py:496
  80.3 20.9 %collective-permute-start.12 = (bf16[1,128,512]{2,1,0:T(8,128)(2,1)S(1)}, bf16[1,128,512]{2,1,0:T(8,128)(2,1)S(1)}, u32[]{:S(2)}, u32[]{:S(2)}) collective-permute-start(bf16[1,128,512]{2,1,0:T(8,128)(2,1)S(1)} %get-tuple-element.39), channel_id=1, source_target_pairs={{0,2},{1,3},{2,0},{3,1},{4,6},{5,7},{6,4},{7,5},{8,10},{9,11},{10,... | collective-permute-start | bytes 393224 | tf_op jit(solution)/shard_map/ppermute | solution.py:496
  89.1 12.2 %collective-permute-start.13 = (bf16[1,128,512]{2,1,0:T(8,128)(2,1)S(1)}, bf16[1,128,512]{2,1,0:T(8,128)(2,1)S(1)}, u32[]{:S(2)}, u32[]{:S(2)}) collective-permute-start(bf16[1,128,512]{2,1,0:T(8,128)(2,1)S(1)} %get-tuple-element.40), channel_id=1, source_target_pairs={{0,3},{1,2},{2,1},{3,0},{4,7},{5,6},{6,5},{7,4},{8,11},{9,10},{10,... | collective-permute-start | bytes 393224 | tf_op jit(solution)/shard_map/ppermute | solution.py:496
  89.1 11.3 %collective-permute-start.18 = (bf16[3,128,128]{2,1,0:T(8,128)(2,1)S(1)}, bf16[3,128,128]{2,1,0:T(8,128)(2,1)S(1)}, u32[]{:S(2)}, u32[]{:S(2)}) collective-permute-start(bf16[3,128,128]{2,1,0:T(8,128)(2,1)S(1)} %get-tuple-element.47), channel_id=1, source_target_pairs={{0,2},{1,3},{2,0},{3,1},{4,6},{5,7},{6,4},{7,5},{8,10},{9,11},{10,... | collective-permute-start | bytes 294920 | tf_op jit(solution)/shard_map/ppermute | solution.py:496
  92.1 8.3 %collective-permute-start.19 = (bf16[3,128,128]{2,1,0:T(8,128)(2,1)S(1)}, bf16[3,128,128]{2,1,0:T(8,128)(2,1)S(1)}, u32[]{:S(2)}, u32[]{:S(2)}) collective-permute-start(bf16[3,128,128]{2,1,0:T(8,128)(2,1)S(1)} %get-tuple-element.48), channel_id=1, source_target_pairs={{0,3},{1,2},{2,1},{3,0},{4,7},{5,6},{6,5},{7,4},{8,11},{9,10},{10,... | collective-permute-start | bytes 294920 | tf_op jit(solution)/shard_map/ppermute | solution.py:496

commit v7 on v5

--- a/solution.py
+++ b/solution.py
@@ -161,7 +161,7 @@
 BOTH_LAST = (((1,), (1,)), ((), ()))
 
 
-def attend_kernel(count, scale, chunk, *refs):
+def attend_kernel(count, scale, chunk, first, skip, *refs):
     handed_ref = refs[0]
     blocks = refs[1 : 1 + count]
     outs = refs[1 + count : 1 + 2 * count]
@@ -171,13 +171,14 @@
     seen = handed_ref.shape[0] // count
     for j, block in enumerate(blocks):
         at = pl.ds(j * rows, rows)
-        q_s[at] = block[0]
-        k_s[at] = block[1]
-        v_s[at] = block[2]
+        for i, held in enumerate((q_s, k_s, v_s)):
+            held[at] = block[i, :, pl.ds(skip * HD, HD)]
     spread = spread_rows(rows, seen)
     for j in range(count):
         g_s[pl.ds(j * rows, rows)] = jnp.dot(
-            spread, handed_ref[pl.ds(j * seen, seen)], preferred_element_type=jnp.float32
+            spread,
+            handed_ref[pl.ds(j * seen, seen), pl.ds(first * HD, HD)],
+            preferred_element_type=jnp.float32,
         ).astype(jnp.bfloat16)
     dk_s[...] = jnp.zeros_like(dk_s)
     dv_s[...] = jnp.zeros_like(dv_s)
@@ -201,7 +202,7 @@
         dq_s[at] = (dq * scale).T.astype(jnp.bfloat16)
         return carry
 
-    lax.fori_loop(0, length // chunk, step, 0)
+    lax.fori_loop(0, length // chunk, step, 0, unroll=length <= 2 * chunk)
     for j, out in enumerate(outs):
         at = pl.ds(j * rows, rows)
         out[0] = dq_s[at]
@@ -209,59 +210,50 @@
         out[2] = dv_s[at].astype(jnp.bfloat16)
 
 
-def attend(handed, blocks, first, skip, heads):
+def attend(handed, blocks, first, skip):
     count = len(blocks)
     rows = blocks[0].shape[1]
     length = rows * count
     chunk = min(256, length)
-    out_spec = pl.BlockSpec((3, rows, HD), lambda h: (0, 0, h))
-    block_spec = pl.BlockSpec((3, rows, HD), lambda h: (0, 0, skip + h))
+    vmem = pl.BlockSpec(memory_space=pltpu.VMEM)
     return pl.pallas_call(
-        functools.partial(attend_kernel, count, HD**-0.5, chunk),
-        grid=(heads,),
-        in_specs=[pl.BlockSpec((handed.shape[0], HD), lambda h: (0, first + h))]
-        + [block_spec] * count,
-        out_specs=[out_spec] * count,
+        functools.partial(attend_kernel, count, HD**-0.5, chunk, first, skip),
+        in_specs=[vmem] * (1 + count),
+        out_specs=[vmem] * count,
         scratch_shapes=[pltpu.VMEM((length, HD), jnp.bfloat16)] * 5
         + [pltpu.VMEM((length, HD), jnp.float32)] * 2,
-        out_shape=[jax.ShapeDtypeStruct((3, rows, heads * HD), jnp.bfloat16)] * count,
+        out_shape=[jax.ShapeDtypeStruct((3, rows, HD), jnp.bfloat16)] * count,
         cost_estimate=pl.CostEstimate(
-            flops=10 * heads * length * length * HD,
-            bytes_accessed=12 * length * heads * HD,
-            transcendentals=heads * length * length,
+            flops=10 * length * length * HD,
+            bytes_accessed=12 * length * HD,
+            transcendentals=length * length,
         ),
         compiler_params=pltpu.CompilerParams(
-            vmem_limit_bytes=(4 << 20) + 48 * length * chunk
+            vmem_limit_bytes=(6 << 20) + 48 * length * chunk
         ),
     )(handed, *blocks)
 
 
-def load_half(count, handed_ref, far_handed_ref, blocks, q_s, k_s, v_s, g_s):
+def load_half(count, head, heads, first, handed_ref, far_handed_ref, blocks, q_s, k_s, v_s, g_s):
     half, rows = count // 2, blocks[0].shape[1]
     seen = handed_ref.shape[0] // count
+    columns = pl.ds(head * HD, HD)
     for j, block in enumerate(blocks):
         at = pl.ds(j * rows, rows)
-        q_s[at] = block[0]
+        q_s[at] = block[0, :, columns]
         if j < half:
-            k_s[at] = block[1]
-            v_s[at] = block[2]
+            k_s[at] = block[1, :, columns]
+            v_s[at] = block[2, :, columns]
     spread = spread_rows(rows, seen)
-
-    def fill(ref, swap):
-        for j in range(count):
-            g_s[pl.ds(j * rows, rows)] = jnp.dot(
-                spread, ref[pl.ds((j ^ swap) * seen, seen)], preferred_element_type=jnp.float32
-            ).astype(jnp.bfloat16)
-
-    own = pl.program_id(0) < pl.num_programs(0) // 2
-
-    @pl.when(own)
-    def _():
-        fill(handed_ref, 0)
-
-    @pl.when(jnp.logical_not(own))
-    def _():
-        fill(far_handed_ref, half)
+    each = heads // 2
+    if head < each:
+        ref, swap, taken = handed_ref, 0, pl.ds((first + head) * HD, HD)
+    else:
+        ref, swap, taken = far_handed_ref, half, pl.ds((head - each) * HD, HD)
+    for j in range(count):
+        g_s[pl.ds(j * rows, rows)] = jnp.dot(
+            spread, ref[pl.ds((j ^ swap) * seen, seen), taken], preferred_element_type=jnp.float32
+        ).astype(jnp.bfloat16)
 
 
 def half_products(scale, key_rows, value_rows, q, g):
@@ -270,69 +262,85 @@
     return scores, grad_weights
 
 
-def half_stats_kernel(count, scale, chunk, *refs):
+def half_stats_kernel(count, scale, chunk, first, *refs):
     handed_ref, far_handed_ref = refs[:2]
     blocks = refs[2 : 2 + count]
-    out, q_s, k_s, v_s, g_s = refs[2 + count :]
-    load_half(count, handed_ref, far_handed_ref, blocks, q_s, k_s, v_s, g_s)
-    key_rows, value_rows = k_s[...], v_s[...]
-
-    def step(c, carry):
-        at = pl.ds(pl.multiple_of(c * chunk, chunk), chunk)
-        scores, grad_weights = half_products(scale, key_rows, value_rows, q_s[at], g_s[at])
-        row_max = jnp.max(scores, axis=0, keepdims=True)
-        exp_scores = jnp.exp(scores - row_max)
-        total = jnp.sum(exp_scores, axis=0, keepdims=True)
-        out[0, pl.ds(0, 1), at] = row_max + jnp.log(total)
-        out[0, pl.ds(1, 1), at] = (
-            jnp.sum(exp_scores * grad_weights, axis=0, keepdims=True) / total
+    out = refs[2 + count]
+    heads = out.shape[0]
+    for head in range(heads):
+        q_s, k_s, v_s, g_s = (ref.at[head] for ref in refs[3 + count :])
+        load_half(
+            count, head, heads, first, handed_ref, far_handed_ref, blocks, q_s, k_s, v_s, g_s
         )
-        return carry
-
-    lax.fori_loop(0, q_s.shape[0] // chunk, step, 0)
-
-
-def half_grads_kernel(count, scale, chunk, *refs):
+        key_rows, value_rows = k_s[...], v_s[...]
+
+        def step(c, carry):
+            at = pl.ds(pl.multiple_of(c * chunk, chunk), chunk)
+            scores, grad_weights = half_products(scale, key_rows, value_rows, q_s[at], g_s[at])
+            row_max = jnp.max(scores, axis=0, keepdims=True)
+            exp_scores = jnp.exp(scores - row_max)
+            total = jnp.sum(exp_scores, axis=0, keepdims=True)
+            out[head, pl.ds(0, 1), at] = row_max + jnp.log(total)
+            out[head, pl.ds(1, 1), at] = (
+                jnp.sum(exp_scores * grad_weights, axis=0, keepdims=True) / total
+            )
+            return carry
+
+        length = q_s.shape[0]
+        lax.fori_loop(0, length // chunk, step, 0, unroll=length <= 2 * chunk)
+
+
+def half_grads_kernel(count, scale, chunk, first, *refs):
     handed_ref, far_handed_ref = refs[:2]
     blocks = refs[2 : 2 + count]
     stats_ref, far_stats_ref = refs[2 + count : 4 + count]
     outs = refs[4 + count : 4 + 2 * count]
-    q_s, k_s, v_s, g_s, dq_s, dk_s, dv_s = refs[4 + 2 * count :]
-    load_half(count, handed_ref, far_handed_ref, blocks, q_s, k_s, v_s, g_s)
-    rows, length = blocks[0].shape[1], q_s.shape[0]
-    dk_s[...] = jnp.zeros_like(dk_s)
-    dv_s[...] = jnp.zeros_like(dv_s)
-    key_rows, value_rows = k_s[...], v_s[...]
-    key_columns = key_rows.T
-
-    def step(c, carry):
-        at = pl.ds(pl.multiple_of(c * chunk, chunk), chunk)
-        far_first = lax.rem(c * chunk + length // 2, length)
-        far_at = pl.ds(pl.multiple_of(far_first, chunk), chunk)
-        q, g = q_s[at], g_s[at]
-        scores, grad_weights = half_products(scale, key_rows, value_rows, q, g)
-        near, far = stats_ref[0, pl.ds(0, 1), at], far_stats_ref[0, pl.ds(0, 1), far_at]
-        top = jnp.maximum(near, far)
-        whole = top + jnp.log(jnp.exp(near - top) + jnp.exp(far - top))
-        row_dot = (
-            jnp.exp(near - whole) * stats_ref[0, pl.ds(1, 1), at]
-            + jnp.exp(far - whole) * far_stats_ref[0, pl.ds(1, 1), far_at]
+    rows = blocks[0].shape[1]
+    heads = stats_ref.shape[0]
+    for head in range(heads):
+        q_s, k_s, v_s, g_s, dq_s, dk_s, dv_s = (ref.at[head] for ref in refs[4 + 2 * count :])
+        load_half(
+            count, head, heads, first, handed_ref, far_handed_ref, blocks, q_s, k_s, v_s, g_s
         )
-        weights = jnp.exp(scores - whole)
-        grad_scores = (weights * (grad_weights - row_dot)).astype(jnp.bfloat16)
-        dv_s[...] += jnp.dot(weights.astype(jnp.bfloat16), g, preferred_element_type=jnp.float32)
-        dk_s[...] += jnp.dot(grad_scores, q, preferred_element_type=jnp.float32)
-        dq = jnp.dot(key_columns, grad_scores, preferred_element_type=jnp.float32)
-        dq_s[at] = (dq * scale).T.astype(jnp.bfloat16)
-        return carry
-
-    lax.fori_loop(0, length // chunk, step, 0)
-    for j, out in enumerate(outs):
-        at = pl.ds(j * rows, rows)
-        out[0] = dq_s[at]
-        if j < count // 2:
-            out[1] = (dk_s[at] * scale).astype(jnp.bfloat16)
-            out[2] = dv_s[at].astype(jnp.bfloat16)
+        length = q_s.shape[0]
+        far_head = (head + heads // 2) % heads
+        dk_s[...] = jnp.zeros(dk_s.shape, dk_s.dtype)
+        dv_s[...] = jnp.zeros(dv_s.shape, dv_s.dtype)
+        key_rows, value_rows = k_s[...], v_s[...]
+        key_columns = key_rows.T
+
+        def step(c, carry):
+            at = pl.ds(pl.multiple_of(c * chunk, chunk), chunk)
+            far_first = lax.rem(c * chunk + length // 2, length)
+            far_at = pl.ds(pl.multiple_of(far_first, chunk), chunk)
+            q, g = q_s[at], g_s[at]
+            scores, grad_weights = half_products(scale, key_rows, value_rows, q, g)
+            near = stats_ref[head, pl.ds(0, 1), at]
+            far = far_stats_ref[far_head, pl.ds(0, 1), far_at]
+            top = jnp.maximum(near, far)
+            whole = top + jnp.log(jnp.exp(near - top) + jnp.exp(far - top))
+            row_dot = (
+                jnp.exp(near - whole) * stats_ref[head, pl.ds(1, 1), at]
+                + jnp.exp(far - whole) * far_stats_ref[far_head, pl.ds(1, 1), far_at]
+            )
+            weights = jnp.exp(scores - whole)
+            grad_scores = (weights * (grad_weights - row_dot)).astype(jnp.bfloat16)
+            dv_s[...] += jnp.dot(
+                weights.astype(jnp.bfloat16), g, preferred_element_type=jnp.float32
+            )
+            dk_s[...] += jnp.dot(grad_scores, q, preferred_element_type=jnp.float32)
+            dq = jnp.dot(key_columns, grad_scores, preferred_element_type=jnp.float32)
+            dq_s[at] = (dq * scale).T.astype(jnp.bfloat16)
+            return carry
+
+        lax.fori_loop(0, length // chunk, step, 0, unroll=length <= 2 * chunk)
+        columns = pl.ds(head * HD, HD)
+        for j, out in enumerate(outs):
+            at = pl.ds(j * rows, rows)
+            out[0, :, columns] = dq_s[at]
+            if j < count // 2:
+                out[1, :, columns] = (dk_s[at] * scale).astype(jnp.bfloat16)
+                out[2, :, columns] = dv_s[at].astype(jnp.bfloat16)
 
 
 def half_call(kernel, handed, far_handed, blocks, stats, first):
@@ -340,31 +348,19 @@
     rows, heads = blocks[0].shape[1], blocks[0].shape[2] // HD
     length, held = rows * count, rows * count // 2
     chunk = min(256, held)
-    each = heads // 2
-
-    def block_spec(array):
-        return pl.BlockSpec((array.shape[0], rows, HD), lambda h: (0, 0, h))
-
-    stats_spec = pl.BlockSpec((1, 2, length), lambda h: (h, 0, 0))
-    far_spec = pl.BlockSpec((1, 2, length), lambda h: (lax.rem(h + each, heads), 0, 0))
-    scratch = [pltpu.VMEM((n, HD), jnp.bfloat16) for n in (length, held, held, length)]
+    vmem = pl.BlockSpec(memory_space=pltpu.VMEM)
+    scratch = [pltpu.VMEM((heads, n, HD), jnp.bfloat16) for n in (length, held, held, length)]
     if stats:
-        out_specs = [block_spec(b) for b in blocks]
+        out_specs = [vmem] * count
         out_shape = [jax.ShapeDtypeStruct(b.shape, jnp.bfloat16) for b in blocks]
-        scratch += [pltpu.VMEM((length, HD), jnp.bfloat16)]
-        scratch += [pltpu.VMEM((held, HD), jnp.float32)] * 2
+        scratch += [pltpu.VMEM((heads, length, HD), jnp.bfloat16)]
+        scratch += [pltpu.VMEM((heads, held, HD), jnp.float32)] * 2
     else:
-        out_specs = stats_spec
+        out_specs = vmem
         out_shape = jax.ShapeDtypeStruct((heads, 2, length), jnp.float32)
     return pl.pallas_call(
-        functools.partial(kernel, count, HD**-0.5, chunk),
-        grid=(heads,),
-        in_specs=[
-            pl.BlockSpec((handed.shape[0], HD), lambda h: (0, first + lax.rem(h, each))),
-            pl.BlockSpec((handed.shape[0], HD), lambda h: (0, lax.rem(h, each))),
-        ]
-        + [block_spec(b) for b in blocks]
-        + [stats_spec, far_spec][: len(stats)],
+        functools.partial(kernel, count, HD**-0.5, chunk, first),
+        in_specs=[vmem] * (2 + count + len(stats)),
         out_specs=out_specs,
         scratch_shapes=scratch,
         out_shape=out_shape,
@@ -374,7 +370,7 @@
             transcendentals=heads * length * held,
         ),
         compiler_params=pltpu.CompilerParams(
-            vmem_limit_bytes=(4 << 20) + 48 * length * chunk
+            vmem_limit_bytes=(4 << 20) + 12 * heads * length * HD + 80 * length * chunk
         ),
     )(handed, far_handed, *blocks, *stats)
 
@@ -498,11 +494,12 @@
 
     visual_grad = visual_grads(place_of, visual_pos, rm_hidden, rm_cotangent, rm_gain)
     visual_blocks = gathered(visual_grad, "tensor")
-    blocks = exchange(pack(place_of, own, 0, whole * HD, (0,), (3,) * count))
     if shared:
         taken = (3,) * half + (1,) * half
         packed = pack(place_of, own, whole * HD, shared * HD, (0, half), taken)
         half_blocks = exchange(packed)
+    packed = pack(place_of, own, 0, whole * HD, (0,), (3,) * count)
+    blocks = exchange(packed)
 
     reward_sum = total_over(jnp.sum(rewards), "dp")
     sample_count = lax.axis_size("dp") * rewards.shape[0]
@@ -518,7 +515,7 @@
 
     outs = ()
     for g in range(whole):
-        parts = exchange(attend(handed, blocks, g, g, 1))
+        parts = exchange(attend(handed, blocks, g, g))
         outs = place(place_of, parts, outs, img_query.shape, g * HD)
     if shared:
         stats = half_call(half_stats_kernel, handed, far_handed, half_blocks, (), whole)

time: 105 us -> 102 us (0.971)
  Pallas kernels: 20.4 us -> 14.8 us
  waiting for transfers between devices: 35.4 us -> 38.9 us
    pallas_call x2, Pallas kernels: 9.3 us -> 4.38 us  [half_call(): pl.pallas_call(functools.partial(kernel, count, HD ** (-0.5), chunk, firs...]
    ppermute x15, waiting for transfers between devices: 19.8 us -> 23.3 us  [exchange(): lax.ppermute(blocks[k], 'tensor', partners(count, k))]
  transfers between devices with their start and end apart: 23 -> 23, of which waited for: 9 -> 10; matrix products, arithmetic and copies ran while one was open for 3% -> 3% of each run, Pallas kernels for 14% -> 10%
where the time goes in v7:
time: 102 us; the launch traced here: 100 us
  starting transfers between devices  40.7 us (40%)
  waiting for transfers between devices  38.9 us (38%)
  Pallas kernels  14.8 us (15%)
  between operations  3.31 us (3%)
  matrix products  2.68 us (3%)
    ppermute x15, starting transfers between devices, exchange(): lax.ppermute(blocks[k], 'tensor', partners(count, k))  28.9 us
    ppermute x15, waiting for transfers between devices, exchange(): lax.ppermute(blocks[k], 'tensor', partners(count, k))  23.3 us
    ppermute x3, waiting for transfers between devices, gathered(): held[k ^ step] = lax.ppermute(held[k], axis, partners(size, step))  9.1 us
    ppermute x3, starting transfers between devices, gathered(): held[k ^ step] = lax.ppermute(held[k], axis, partners(size, step))  4.8 us
    ppermute x3, starting transfers between devices, total_over(): value = value + lax.ppermute(value, axis, partners(size, step))  4.78 us
    pallas_call x2, Pallas kernels, half_call(): pl.pallas_call(functools.partial(kernel, count, HD ** (-0.5), chunk, firs...  4.38 us
    ppermute x1, waiting for transfers between devices, work(): lax.ppermute(handed[:, whole * HD:], 'tensor', partners(count, half))  4.11 us
    pallas_call x2, Pallas kernels, attend(): pl.pallas_call(functools.partial(attend_kernel, count, HD ** (-0.5), chun...  3.34 us
  transfers between devices with their start and end apart: 23, of which 10 were waited for; matrix products, arithmetic and copies ran while one was open for 3% of the time, Pallas kernels for 10%

profile of v7, /device:TPU:2, one launch (start us, length us, event | category | flops | bytes accessed | tf_op | source)
XLA Modules:
  0.0 100.4 jit_solution(11359520108131538086)
XLA Ops:
  0.6 1.8 %visual.1 = bf16[32,3584]{1,0:T(8,128)(2,1)S(1)} custom-call(s32[1]{0:T(128)} %bitcast.here_ref.refs_0_, s32[1,32]{1,0:T(1,128)} %pos_hbm.1, f32[28,128]{1,0:T(8,128)} %bitcast.6, bf16[1,64,3584]{2,1,0:T(8,128)(2,1)} %hidden_hbm.1, bf16[1,64,3584]{2,1,0:T(8,128)(2,1)} %cot_hbm.1), custom_call_target="tpu_custom_call" | custom-call | flops 29360128 | bytes 917504 | tf_op jit(solution)/shard_map/visual/pallas_call | solution.py:66
  2.4 2.7 %collective-permute-start.1 = (bf16[32,3584]{1,0:T(8,128)(2,1)S(1)}, bf16[32,3584]{1,0:T(8,128)(2,1)S(1)}, u32[]{:S(2)}, u32[]{:S(2)}) collective-permute-start(bf16[32,3584]{1,0:T(8,128)(2,1)S(1)} %visual.1), channel_id=1, source_target_pairs={{0,2},{1,3},{2,0},{3,1},{4,6},{5,7},{6,4},{7,5},{8,10},{9,11},{10,... | collective-permute-start | bytes 688136 | tf_op jit(solution)/shard_map/ppermute | solution.py:148
  5.1 1.6 %collective-permute-start = (bf16[32,3584]{1,0:T(8,128)(2,1)S(1)}, bf16[32,3584]{1,0:T(8,128)(2,1)S(1)}, u32[]{:S(2)}, u32[]{:S(2)}) collective-permute-start(bf16[32,3584]{1,0:T(8,128)(2,1)S(1)} %visual.1), channel_id=1, source_target_pairs={{0,1},{1,0},{2,3},{3,2},{4,5},{5,4},{6,7},{7,6},{8,9},{9,8},{10,11... | collective-permute-start | bytes 688136 | tf_op jit(solution)/shard_map/ppermute | solution.py:148
  6.7 9.1 %collective-permute-done.1 = bf16[32,3584]{1,0:T(8,128)(2,1)S(1)} collective-permute-done((bf16[32,3584]{1,0:T(8,128)(2,1)S(1)}, bf16[32,3584]{1,0:T(8,128)(2,1)S(1)}, u32[]{:S(2)}, u32[]{:S(2)}) %collective-permute-start.1) | collective-permute-done | bytes 229408 | tf_op jit(solution)/shard_map/ppermute | solution.py:148
  16.3 1.4 %shard_map.112 = (bf16[3,128,512]{2,1,0:T(8,128)(2,1)S(1)}, bf16[3,128,512]{2,1,0:T(8,128)(2,1)S(1)}, bf16[1,128,512]{2,1,0:T(8,128)(2,1)S(1)}, bf16[1,128,512]{2,1,0:T(8,128)(2,1)S(1)}) custom-call(s32[1]{0:T(128)} %bitcast.here_ref.refs_0_, bf16[1,128,2048]{2,1,0:T(8,128)(2,1)} %refs_0_.3, bf16[1,128,2048]{2,1,0:T(8,128)(2,1)} %refs_1_.3, ...), custom_call_target="tpu_custom_call" | custom-call | bytes 2097152 | tf_op jit(solution)/shard_map/pallas_call | solution.py:111
  17.7 1.5 %collective-permute-start.7 = (bf16[3,128,512]{2,1,0:T(8,128)(2,1)S(1)}, bf16[3,128,512]{2,1,0:T(8,128)(2,1)S(1)}, u32[]{:S(2)}, u32[]{:S(2)}) collective-permute-start(bf16[3,128,512]{2,1,0:T(8,128)(2,1)S(1)} %get-tuple-element.30), channel_id=1, source_target_pairs={{0,1},{1,0},{2,3},{3,2},{4,5},{5,4},{6,7},{7,6},{8,9},{9,8},{10,11... | collective-permute-start | bytes 1179656 | tf_op jit(solution)/shard_map/ppermute | solution.py:492
  19.2 2.0 %collective-permute-start.8 = (bf16[1,128,512]{2,1,0:T(8,128)(2,1)S(1)}, bf16[1,128,512]{2,1,0:T(8,128)(2,1)S(1)}, u32[]{:S(2)}, u32[]{:S(2)}) collective-permute-start(bf16[1,128,512]{2,1,0:T(8,128)(2,1)S(1)} %get-tuple-element.31), channel_id=1, source_target_pairs={{0,2},{1,3},{2,0},{3,1},{4,6},{5,7},{6,4},{7,5},{8,10},{9,11},{10,... | collective-permute-start | bytes 393224 | tf_op jit(solution)/shard_map/ppermute | solution.py:492
  22.5 1.9 %collective-permute-start.4 = (f32[]{:T(128)}, f32[]{:T(128)}, u32[]{:S(2)}, u32[]{:S(2)}) collective-permute-start(f32[]{:T(128)} %add.9), channel_id=1, source_target_pairs={{0,8},{4,12},{8,0},{12,4},{16,24},{20,28},{24,16},{28,20},{1,9},{5... | collective-permute-start | bytes 20 | tf_op jit(solution)/shard_map/ppermute | solution.py:137
  24.4 1.7 %collective-permute-done.4 = f32[]{:T(128)} collective-permute-done((f32[]{:T(128)}, f32[]{:T(128)}, u32[]{:S(2)}, u32[]{:S(2)}) %collective-permute-start.4) | collective-permute-done | bytes 36 | tf_op jit(solution)/shard_map/ppermute | solution.py:137
  26.7 2.9 %collective-permute-start.5 = (f32[]{:T(128)}, f32[]{:T(128)}, u32[]{:S(2)}, u32[]{:S(2)}) collective-permute-start(f32[]{:T(128)} %add.10), channel_id=1, source_target_pairs={{0,16},{4,20},{8,24},{12,28},{16,0},{20,4},{24,8},{28,12},{1,17},{... | collective-permute-start | bytes 20 | tf_op jit(solution)/shard_map/ppermute | solution.py:137
  30.3 1.4 %collective-permute-start.9 = (bf16[1,128,512]{2,1,0:T(8,128)(2,1)S(1)}, bf16[1,128,512]{2,1,0:T(8,128)(2,1)S(1)}, u32[]{:S(2)}, u32[]{:S(2)}) collective-permute-start(bf16[1,128,512]{2,1,0:T(8,128)(2,1)S(1)} %get-tuple-element.32), channel_id=1, source_target_pairs={{0,3},{1,2},{2,1},{3,0},{4,7},{5,6},{6,5},{7,4},{8,11},{9,10},{10,... | collective-permute-start | bytes 393224 | tf_op jit(solution)/shard_map/ppermute | solution.py:492
  32.4 2.7 %fusion.refs_0_ = bf16[128,512]{1,0:T(8,128)(2,1)S(1)} fusion(bf16[3584,512]{1,0:T(8,128)(2,1)} %param.14, bf16[32,3584]{1,0:T(8,128)(2,1)S(1)} %collective-permute-done.2, bf16[32,3584]{1,0:T(8,128)(2,1)S(1)} %collective-permute-done.1, bf16[32,3584]{1,0:T(8,128)(2,1)S(1)} %collective-permute-done, bf16[32,3584]{1,0:T(8,128)(2,1)S(1)} %visual.1, f32[]{:T(128)S(6)} %div.3), kind=kOutput, calls=%fused_computation.1 | convolution fusion | flops 473563136 | bytes 4718596 | tf_op jit(solution)/shard_map/dot_general | solution.py:508
  35.1 2.1 %collective-permute-start.6 = (bf16[128,256]{1,0:T(8,128)(2,1)S(1)}, bf16[128,256]{1,0:T(8,128)(2,1)S(1)}, u32[]{:S(2)}, u32[]{:S(2)}) collective-permute-start(bf16[128,256]{1,0:T(8,128)(2,1)S(1)} %slice.4), channel_id=1, source_target_pairs={{0,2},{1,3},{2,0},{3,1},{4,6},{5,7},{6,4},{7,5},{8,10},{9,11},{10,... | collective-permute-start | bytes 196616 | tf_op jit(solution)/shard_map/ppermute | solution.py:514
  37.2 2.6 %collective-permute-done.9.refs_5_ = bf16[1,128,512]{2,1,0:T(8,128)(2,1)S(1)} collective-permute-done((bf16[1,128,512]{2,1,0:T(8,128)(2,1)S(1)}, bf16[1,128,512]{2,1,0:T(8,128)(2,1)S(1)}, u32[]{:S(2)}, u32[]{:S(2)}) %collective-permute-start.9) | collective-permute-done | bytes 131104 | tf_op jit(solution)/shard_map/ppermute | solution.py:492
  39.7 4.1 %collective-permute-done.6.refs_1_ = bf16[128,256]{1,0:T(8,128)(2,1)S(1)} collective-permute-done((bf16[128,256]{1,0:T(8,128)(2,1)S(1)}, bf16[128,256]{1,0:T(8,128)(2,1)S(1)}, u32[]{:S(2)}, u32[]{:S(2)}) %collective-permute-start.6) | collective-permute-done | bytes 65568 | tf_op jit(solution)/shard_map/ppermute | solution.py:514
  43.9 1.5 %shard_map.113.refs_6_ = f32[4,2,512]{2,1,0:T(2,128)S(1)} custom-call(bf16[128,512]{1,0:T(8,128)(2,1)S(1)} %fusion.refs_0_, bf16[128,256]{1,0:T(8,128)(2,1)S(1)} %collective-permute-done.6.refs_1_, bf16[3,128,512]{2,1,0:T(8,128)(2,1)S(1)} %get-tuple-element.29.refs_2_, bf16[3,128,512]{2,1,0:T(8,128)(2,1)S(1)} %collective-permute-done.7.refs_3_, ...), custom_call_target="tpu_custom_call" | custom-call | flops 268435456 | bytes 3145728 | tf_op jit(solution)/shard_map/pallas_call | solution.py:361
  46.8 1.4 %collective-permute-start.14 = (bf16[3,128,256]{2,1,0:T(8,128)(2,1)S(1)}, bf16[3,128,256]{2,1,0:T(8,128)(2,1)S(1)}, u32[]{:S(2)}, u32[]{:S(2)}) collective-permute-start(bf16[3,128,256]{2,1,0:T(8,128)(2,1)S(1)} %get-tuple-element.38), channel_id=1, source_target_pairs={{0,1},{1,0},{2,3},{3,2},{4,5},{5,4},{6,7},{7,6},{8,9},{9,8},{10,11... | collective-permute-start | bytes 589832 | tf_op jit(solution)/shard_map/ppermute | solution.py:492
  48.2 1.6 %collective-permute-start.15 = (bf16[3,128,256]{2,1,0:T(8,128)(2,1)S(1)}, bf16[3,128,256]{2,1,0:T(8,128)(2,1)S(1)}, u32[]{:S(2)}, u32[]{:S(2)}) collective-permute-start(bf16[3,128,256]{2,1,0:T(8,128)(2,1)S(1)} %get-tuple-element.39), channel_id=1, source_target_pairs={{0,2},{1,3},{2,0},{3,1},{4,6},{5,7},{6,4},{7,5},{8,10},{9,11},{10,... | collective-permute-start | bytes 589832 | tf_op jit(solution)/shard_map/ppermute | solution.py:492
  49.8 1.4 %collective-permute-start.16 = (bf16[3,128,256]{2,1,0:T(8,128)(2,1)S(1)}, bf16[3,128,256]{2,1,0:T(8,128)(2,1)S(1)}, u32[]{:S(2)}, u32[]{:S(2)}) collective-permute-start(bf16[3,128,256]{2,1,0:T(8,128)(2,1)S(1)} %get-tuple-element.40), channel_id=1, source_target_pairs={{0,3},{1,2},{2,1},{3,0},{4,7},{5,6},{6,5},{7,4},{8,11},{9,10},{10,... | collective-permute-start | bytes 589832 | tf_op jit(solution)/shard_map/ppermute | solution.py:492
  51.2 2.9 %shard_map.114 = (bf16[3,128,512]{2,1,0:T(8,128)(2,1)S(1)}, bf16[3,128,512]{2,1,0:T(8,128)(2,1)S(1)}, bf16[1,128,512]{2,1,0:T(8,128)(2,1)S(1)}, bf16[1,128,512]{2,1,0:T(8,128)(2,1)S(1)}) custom-call(bf16[128,512]{1,0:T(8,128)(2,1)S(1)} %fusion.refs_0_, bf16[128,256]{1,0:T(8,128)(2,1)S(1)} %collective-permute-done.6.refs_1_, ...), custom_call_target="tpu_custom_call" | custom-call | flops 671088640 | bytes 3145728 | tf_op jit(solution)/shard_map/pallas_call | solution.py:361
  54.7 1.6 %collective-permute-done.14.refs_2_ = bf16[3,128,256]{2,1,0:T(8,128)(2,1)S(1)} collective-permute-done((bf16[3,128,256]{2,1,0:T(8,128)(2,1)S(1)}, bf16[3,128,256]{2,1,0:T(8,128)(2,1)S(1)}, u32[]{:S(2)}, u32[]{:S(2)}) %collective-permute-start.14) | collective-permute-done | bytes 196640 | tf_op jit(solution)/shard_map/ppermute | solution.py:492
  56.2 8.4 %collective-permute-done.15.refs_3_ = bf16[3,128,256]{2,1,0:T(8,128)(2,1)S(1)} collective-permute-done((bf16[3,128,256]{2,1,0:T(8,128)(2,1)S(1)}, bf16[3,128,256]{2,1,0:T(8,128)(2,1)S(1)}, u32[]{:S(2)}, u32[]{:S(2)}) %collective-permute-start.15) | collective-permute-done | bytes 196640 | tf_op jit(solution)/shard_map/ppermute | solution.py:492
  65.4 1.7 %shard_map.117 = (bf16[3,128,128]{2,1,0:T(8,128)(2,1)S(1)}, bf16[3,128,128]{2,1,0:T(8,128)(2,1)S(1)}, bf16[3,128,128]{2,1,0:T(8,128)(2,1)S(1)}, bf16[3,128,128]{2,1,0:T(8,128)(2,1)S(1)}) custom-call(bf16[128,512]{1,0:T(8,128)(2,1)S(1)} %fusion.refs_0_, bf16[3,128,256]{2,1,0:T(8,128)(2,1)S(1)} %get-tuple-element.37.refs_1_, ...), custom_call_target="tpu_custom_call" | custom-call | flops 335544320 | bytes 786432 | tf_op jit(solution)/shard_map/pallas_call | solution.py:219
  67.0 2.4 %collective-permute-start.20 = (bf16[3,128,128]{2,1,0:T(8,128)(2,1)S(1)}, bf16[3,128,128]{2,1,0:T(8,128)(2,1)S(1)}, u32[]{:S(2)}, u32[]{:S(2)}) collective-permute-start(bf16[3,128,128]{2,1,0:T(8,128)(2,1)S(1)} %get-tuple-element.46), channel_id=1, source_target_pairs={{0,1},{1,0},{2,3},{3,2},{4,5},{5,4},{6,7},{7,6},{8,9},{9,8},{10,11... | collective-permute-start | bytes 294920 | tf_op jit(solution)/shard_map/ppermute | solution.py:492
  69.4 1.5 %collective-permute-start.21 = (bf16[3,128,128]{2,1,0:T(8,128)(2,1)S(1)}, bf16[3,128,128]{2,1,0:T(8,128)(2,1)S(1)}, u32[]{:S(2)}, u32[]{:S(2)}) collective-permute-start(bf16[3,128,128]{2,1,0:T(8,128)(2,1)S(1)} %get-tuple-element.47), channel_id=1, source_target_pairs={{0,2},{1,3},{2,0},{3,1},{4,6},{5,7},{6,4},{7,5},{8,10},{9,11},{10,... | collective-permute-start | bytes 294920 | tf_op jit(solution)/shard_map/ppermute | solution.py:492
  72.3 1.7 %shard_map.116 = (bf16[3,128,128]{2,1,0:T(8,128)(2,1)S(1)}, bf16[3,128,128]{2,1,0:T(8,128)(2,1)S(1)}, bf16[3,128,128]{2,1,0:T(8,128)(2,1)S(1)}, bf16[3,128,128]{2,1,0:T(8,128)(2,1)S(1)}) custom-call(bf16[128,512]{1,0:T(8,128)(2,1)S(1)} %fusion.refs_0_, bf16[3,128,256]{2,1,0:T(8,128)(2,1)S(1)} %get-tuple-element.37.refs_1_, ...), custom_call_target="tpu_custom_call" | custom-call | flops 335544320 | bytes 786432 | tf_op jit(solution)/shard_map/pallas_call | solution.py:219
  74.6 2.4 %collective-permute-start.12 = (bf16[1,128,512]{2,1,0:T(8,128)(2,1)S(1)}, bf16[1,128,512]{2,1,0:T(8,128)(2,1)S(1)}, u32[]{:S(2)}, u32[]{:S(2)}) collective-permute-start(bf16[1,128,512]{2,1,0:T(8,128)(2,1)S(1)} %get-tuple-element.35), channel_id=1, source_target_pairs={{0,2},{1,3},{2,0},{3,1},{4,6},{5,7},{6,4},{7,5},{8,10},{9,11},{10,... | collective-permute-start | bytes 393224 | tf_op jit(solution)/shard_map/ppermute | solution.py:492
  77.0 3.0 %collective-permute-done.21.refs_3_ = bf16[3,128,128]{2,1,0:T(8,128)(2,1)S(1)} collective-permute-done((bf16[3,128,128]{2,1,0:T(8,128)(2,1)S(1)}, bf16[3,128,128]{2,1,0:T(8,128)(2,1)S(1)}, u32[]{:S(2)}, u32[]{:S(2)}) %collective-permute-start.21) | collective-permute-done | bytes 98336 | tf_op jit(solution)/shard_map/ppermute | solution.py:492
  80.0 3.0 %collective-permute-start.13 = (bf16[1,128,512]{2,1,0:T(8,128)(2,1)S(1)}, bf16[1,128,512]{2,1,0:T(8,128)(2,1)S(1)}, u32[]{:S(2)}, u32[]{:S(2)}) collective-permute-start(bf16[1,128,512]{2,1,0:T(8,128)(2,1)S(1)} %get-tuple-element.36), channel_id=1, source_target_pairs={{0,3},{1,2},{2,1},{3,0},{4,7},{5,6},{6,5},{7,4},{8,11},{9,10},{10,... | collective-permute-start | bytes 393224 | tf_op jit(solution)/shard_map/ppermute | solution.py:492
  83.0 4.3 %collective-permute-start.18 = (bf16[3,128,128]{2,1,0:T(8,128)(2,1)S(1)}, bf16[3,128,128]{2,1,0:T(8,128)(2,1)S(1)}, u32[]{:S(2)}, u32[]{:S(2)}) collective-permute-start(bf16[3,128,128]{2,1,0:T(8,128)(2,1)S(1)} %get-tuple-element.43), channel_id=1, source_target_pairs={{0,2},{1,3},{2,0},{3,1},{4,6},{5,7},{6,4},{7,5},{8,10},{9,11},{10,... | collective-permute-start | bytes 294920 | tf_op jit(solution)/shard_map/ppermute | solution.py:492
  87.3 3.4 %collective-permute-start.19 = (bf16[3,128,128]{2,1,0:T(8,128)(2,1)S(1)}, bf16[3,128,128]{2,1,0:T(8,128)(2,1)S(1)}, u32[]{:S(2)}, u32[]{:S(2)}) collective-permute-start(bf16[3,128,128]{2,1,0:T(8,128)(2,1)S(1)} %get-tuple-element.44), channel_id=1, source_target_pairs={{0,3},{1,2},{2,1},{3,0},{4,7},{5,6},{6,5},{7,4},{8,11},{9,10},{10,... | collective-permute-start | bytes 294920 | tf_op jit(solution)/shard_map/ppermute | solution.py:492
  91.5 7.0 %collective-permute-done.18.refs_3_ = bf16[3,128,128]{2,1,0:T(8,128)(2,1)S(1)} collective-permute-done((bf16[3,128,128]{2,1,0:T(8,128)(2,1)S(1)}, bf16[3,128,128]{2,1,0:T(8,128)(2,1)S(1)}, u32[]{:S(2)}, u32[]{:S(2)}) %collective-permute-start.18) | collective-permute-done | bytes 98336 | tf_op jit(solution)/shard_map/ppermute | solution.py:492
  (26 shorter events, 8.8 us)
Async XLA Ops:
  2.4 13.3 %collective-permute-start.1 = (bf16[32,3584]{1,0:T(8,128)(2,1)S(1)}, bf16[32,3584]{1,0:T(8,128)(2,1)S(1)}, u32[]{:S(2)}, u32[]{:S(2)}) collective-permute-start(bf16[32,3584]{1,0:T(8,128)(2,1)S(1)} %visual.1), channel_id=1, source_target_pairs={{0,2},{1,3},{2,0},{3,1},{4,6},{5,7},{6,4},{7,5},{8,10},{9,11},{10,... | collective-permute-start | bytes 688136 | tf_op jit(solution)/shard_map/ppermute | solution.py:148
  5.1 27.3 %collective-permute-start = (bf16[32,3584]{1,0:T(8,128)(2,1)S(1)}, bf16[32,3584]{1,0:T(8,128)(2,1)S(1)}, u32[]{:S(2)}, u32[]{:S(2)}) collective-permute-start(bf16[32,3584]{1,0:T(8,128)(2,1)S(1)} %visual.1), channel_id=1, source_target_pairs={{0,1},{1,0},{2,3},{3,2},{4,5},{5,4},{6,7},{7,6},{8,9},{9,8},{10,11... | collective-permute-start | bytes 688136 | tf_op jit(solution)/shard_map/ppermute | solution.py:148
  15.8 16.6 %collective-permute-start.2 = (bf16[32,3584]{1,0:T(8,128)(2,1)S(1)}, bf16[32,3584]{1,0:T(8,128)(2,1)S(1)}, u32[]{:S(2)}, u32[]{:S(2)}) collective-permute-start(bf16[32,3584]{1,0:T(8,128)(2,1)S(1)} %collective-permute-done.1), channel_id=1, source_target_pairs={{0,1},{1,0},{2,3},{3,2},{4,5},{5,4},{6,7},{7,6},{8,9},{9,8},{10,11... | collective-permute-start | bytes 688136 | tf_op jit(solution)/shard_map/ppermute | solution.py:148
  16.3 5.6 %collective-permute-start.3 = (f32[]{:T(128)}, f32[]{:T(128)}, u32[]{:S(2)}, u32[]{:S(2)}) collective-permute-start(f32[]{:T(128)} %bitcast.2), channel_id=1, source_target_pairs={{0,4},{4,0},{8,12},{12,8},{16,20},{20,16},{24,28},{28,24},{1,5},{5... | collective-permute-start | bytes 20 | tf_op jit(solution)/shard_map/ppermute | solution.py:137
  17.7 22.0 %collective-permute-start.7 = (bf16[3,128,512]{2,1,0:T(8,128)(2,1)S(1)}, bf16[3,128,512]{2,1,0:T(8,128)(2,1)S(1)}, u32[]{:S(2)}, u32[]{:S(2)}) collective-permute-start(bf16[3,128,512]{2,1,0:T(8,128)(2,1)S(1)} %get-tuple-element.30), channel_id=1, source_target_pairs={{0,1},{1,0},{2,3},{3,2},{4,5},{5,4},{6,7},{7,6},{8,9},{9,8},{10,11... | collective-permute-start | bytes 1179656 | tf_op jit(solution)/shard_map/ppermute | solution.py:492
  19.2 17.9 %collective-permute-start.8 = (bf16[1,128,512]{2,1,0:T(8,128)(2,1)S(1)}, bf16[1,128,512]{2,1,0:T(8,128)(2,1)S(1)}, u32[]{:S(2)}, u32[]{:S(2)}) collective-permute-start(bf16[1,128,512]{2,1,0:T(8,128)(2,1)S(1)} %get-tuple-element.31), channel_id=1, source_target_pairs={{0,2},{1,3},{2,0},{3,1},{4,6},{5,7},{6,4},{7,5},{8,10},{9,11},{10,... | collective-permute-start | bytes 393224 | tf_op jit(solution)/shard_map/ppermute | solution.py:492
  22.5 3.6 %collective-permute-start.4 = (f32[]{:T(128)}, f32[]{:T(128)}, u32[]{:S(2)}, u32[]{:S(2)}) collective-permute-start(f32[]{:T(128)} %add.9), channel_id=1, source_target_pairs={{0,8},{4,12},{8,0},{12,4},{16,24},{20,28},{24,16},{28,20},{1,9},{5... | collective-permute-start | bytes 20 | tf_op jit(solution)/shard_map/ppermute | solution.py:137
  26.7 3.6 %collective-permute-start.5 = (f32[]{:T(128)}, f32[]{:T(128)}, u32[]{:S(2)}, u32[]{:S(2)}) collective-permute-start(f32[]{:T(128)} %add.10), channel_id=1, source_target_pairs={{0,16},{4,20},{8,24},{12,28},{16,0},{20,4},{24,8},{28,12},{1,17},{... | collective-permute-start | bytes 20 | tf_op jit(solution)/shard_map/ppermute | solution.py:137
  30.3 9.4 %collective-permute-start.9 = (bf16[1,128,512]{2,1,0:T(8,128)(2,1)S(1)}, bf16[1,128,512]{2,1,0:T(8,128)(2,1)S(1)}, u32[]{:S(2)}, u32[]{:S(2)}) collective-permute-start(bf16[1,128,512]{2,1,0:T(8,128)(2,1)S(1)} %get-tuple-element.32), channel_id=1, source_target_pairs={{0,3},{1,2},{2,1},{3,0},{4,7},{5,6},{6,5},{7,4},{8,11},{9,10},{10,... | collective-permute-start | bytes 393224 | tf_op jit(solution)/shard_map/ppermute | solution.py:492
  35.1 8.8 %collective-permute-start.6 = (bf16[128,256]{1,0:T(8,128)(2,1)S(1)}, bf16[128,256]{1,0:T(8,128)(2,1)S(1)}, u32[]{:S(2)}, u32[]{:S(2)}) collective-permute-start(bf16[128,256]{1,0:T(8,128)(2,1)S(1)} %slice.4), channel_id=1, source_target_pairs={{0,2},{1,3},{2,0},{3,1},{4,6},{5,7},{6,4},{7,5},{8,10},{9,11},{10,... | collective-permute-start | bytes 196616 | tf_op jit(solution)/shard_map/ppermute | solution.py:514
  45.4 5.8 %collective-permute-start.10 = (f32[4,2,512]{2,1,0:T(2,128)S(1)}, f32[4,2,512]{2,1,0:T(2,128)S(1)}, u32[]{:S(2)}, u32[]{:S(2)}) collective-permute-start(f32[4,2,512]{2,1,0:T(2,128)S(1)} %shard_map.113.refs_6_), channel_id=1, source_target_pairs={{0,2},{1,3},{2,0},{3,1},{4,6},{5,7},{6,4},{7,5},{8,10},{9,11},{10,... | collective-permute-start | bytes 49160 | tf_op jit(solution)/shard_map/ppermute | solution.py:522
  46.8 9.5 %collective-permute-start.14 = (bf16[3,128,256]{2,1,0:T(8,128)(2,1)S(1)}, bf16[3,128,256]{2,1,0:T(8,128)(2,1)S(1)}, u32[]{:S(2)}, u32[]{:S(2)}) collective-permute-start(bf16[3,128,256]{2,1,0:T(8,128)(2,1)S(1)} %get-tuple-element.38), channel_id=1, source_target_pairs={{0,1},{1,0},{2,3},{3,2},{4,5},{5,4},{6,7},{7,6},{8,9},{9,8},{10,11... | collective-permute-start | bytes 589832 | tf_op jit(solution)/shard_map/ppermute | solution.py:492
  48.2 16.4 %collective-permute-start.15 = (bf16[3,128,256]{2,1,0:T(8,128)(2,1)S(1)}, bf16[3,128,256]{2,1,0:T(8,128)(2,1)S(1)}, u32[]{:S(2)}, u32[]{:S(2)}) collective-permute-start(bf16[3,128,256]{2,1,0:T(8,128)(2,1)S(1)} %get-tuple-element.39), channel_id=1, source_target_pairs={{0,2},{1,3},{2,0},{3,1},{4,6},{5,7},{6,4},{7,5},{8,10},{9,11},{10,... | collective-permute-start | bytes 589832 | tf_op jit(solution)/shard_map/ppermute | solution.py:492
  49.8 15.6 %collective-permute-start.16 = (bf16[3,128,256]{2,1,0:T(8,128)(2,1)S(1)}, bf16[3,128,256]{2,1,0:T(8,128)(2,1)S(1)}, u32[]{:S(2)}, u32[]{:S(2)}) collective-permute-start(bf16[3,128,256]{2,1,0:T(8,128)(2,1)S(1)} %get-tuple-element.40), channel_id=1, source_target_pairs={{0,3},{1,2},{2,1},{3,0},{4,7},{5,6},{6,5},{7,4},{8,11},{9,10},{10,... | collective-permute-start | bytes 589832 | tf_op jit(solution)/shard_map/ppermute | solution.py:492
  54.1 45.4 %collective-permute-start.11 = (bf16[3,128,512]{2,1,0:T(8,128)(2,1)S(1)}, bf16[3,128,512]{2,1,0:T(8,128)(2,1)S(1)}, u32[]{:S(2)}, u32[]{:S(2)}) collective-permute-start(bf16[3,128,512]{2,1,0:T(8,128)(2,1)S(1)} %get-tuple-element.34), channel_id=1, source_target_pairs={{0,1},{1,0},{2,3},{3,2},{4,5},{5,4},{6,7},{7,6},{8,9},{9,8},{10,11... | collective-permute-start | bytes 1179656 | tf_op jit(solution)/shard_map/ppermute | solution.py:492
  67.0 7.6 %collective-permute-start.20 = (bf16[3,128,128]{2,1,0:T(8,128)(2,1)S(1)}, bf16[3,128,128]{2,1,0:T(8,128)(2,1)S(1)}, u32[]{:S(2)}, u32[]{:S(2)}) collective-permute-start(bf16[3,128,128]{2,1,0:T(8,128)(2,1)S(1)} %get-tuple-element.46), channel_id=1, source_target_pairs={{0,1},{1,0},{2,3},{3,2},{4,5},{5,4},{6,7},{7,6},{8,9},{9,8},{10,11... | collective-permute-start | bytes 294920 | tf_op jit(solution)/shard_map/ppermute | solution.py:492
  69.4 10.6 %collective-permute-start.21 = (bf16[3,128,128]{2,1,0:T(8,128)(2,1)S(1)}, bf16[3,128,128]{2,1,0:T(8,128)(2,1)S(1)}, u32[]{:S(2)}, u32[]{:S(2)}) collective-permute-start(bf16[3,128,128]{2,1,0:T(8,128)(2,1)S(1)} %get-tuple-element.47), channel_id=1, source_target_pairs={{0,2},{1,3},{2,0},{3,1},{4,6},{5,7},{6,4},{7,5},{8,10},{9,11},{10,... | collective-permute-start | bytes 294920 | tf_op jit(solution)/shard_map/ppermute | solution.py:492
  70.9 12.2 %collective-permute-start.22 = (bf16[3,128,128]{2,1,0:T(8,128)(2,1)S(1)}, bf16[3,128,128]{2,1,0:T(8,128)(2,1)S(1)}, u32[]{:S(2)}, u32[]{:S(2)}) collective-permute-start(bf16[3,128,128]{2,1,0:T(8,128)(2,1)S(1)} %get-tuple-element.48), channel_id=1, source_target_pairs={{0,3},{1,2},{2,1},{3,0},{4,7},{5,6},{6,5},{7,4},{8,11},{9,10},{10,... | collective-permute-start | bytes 294920 | tf_op jit(solution)/shard_map/ppermute | solution.py:492
  73.9 13.4 %collective-permute-start.17 = (bf16[3,128,128]{2,1,0:T(8,128)(2,1)S(1)}, bf16[3,128,128]{2,1,0:T(8,128)(2,1)S(1)}, u32[]{:S(2)}, u32[]{:S(2)}) collective-permute-start(bf16[3,128,128]{2,1,0:T(8,128)(2,1)S(1)} %get-tuple-element.42), channel_id=1, source_target_pairs={{0,1},{1,0},{2,3},{3,2},{4,5},{5,4},{6,7},{7,6},{8,9},{9,8},{10,11... | collective-permute-start | bytes 294920 | tf_op jit(solution)/shard_map/ppermute | solution.py:492
  74.6 24.8 %collective-permute-start.12 = (bf16[1,128,512]{2,1,0:T(8,128)(2,1)S(1)}, bf16[1,128,512]{2,1,0:T(8,128)(2,1)S(1)}, u32[]{:S(2)}, u32[]{:S(2)}) collective-permute-start(bf16[1,128,512]{2,1,0:T(8,128)(2,1)S(1)} %get-tuple-element.35), channel_id=1, source_target_pairs={{0,2},{1,3},{2,0},{3,1},{4,6},{5,7},{6,4},{7,5},{8,10},{9,11},{10,... | collective-permute-start | bytes 393224 | tf_op jit(solution)/shard_map/ppermute | solution.py:492
  80.0 19.4 %collective-permute-start.13 = (bf16[1,128,512]{2,1,0:T(8,128)(2,1)S(1)}, bf16[1,128,512]{2,1,0:T(8,128)(2,1)S(1)}, u32[]{:S(2)}, u32[]{:S(2)}) collective-permute-start(bf16[1,128,512]{2,1,0:T(8,128)(2,1)S(1)} %get-tuple-element.36), channel_id=1, source_target_pairs={{0,3},{1,2},{2,1},{3,0},{4,7},{5,6},{6,5},{7,4},{8,11},{9,10},{10,... | collective-permute-start | bytes 393224 | tf_op jit(solution)/shard_map/ppermute | solution.py:492
  83.0 15.5 %collective-permute-start.18 = (bf16[3,128,128]{2,1,0:T(8,128)(2,1)S(1)}, bf16[3,128,128]{2,1,0:T(8,128)(2,1)S(1)}, u32[]{:S(2)}, u32[]{:S(2)}) collective-permute-start(bf16[3,128,128]{2,1,0:T(8,128)(2,1)S(1)} %get-tuple-element.43), channel_id=1, source_target_pairs={{0,2},{1,3},{2,0},{3,1},{4,6},{5,7},{6,4},{7,5},{8,10},{9,11},{10,... | collective-permute-start | bytes 294920 | tf_op jit(solution)/shard_map/ppermute | solution.py:492
  87.3 11.3 %collective-permute-start.19 = (bf16[3,128,128]{2,1,0:T(8,128)(2,1)S(1)}, bf16[3,128,128]{2,1,0:T(8,128)(2,1)S(1)}, u32[]{:S(2)}, u32[]{:S(2)}) collective-permute-start(bf16[3,128,128]{2,1,0:T(8,128)(2,1)S(1)} %get-tuple-element.44), channel_id=1, source_target_pairs={{0,3},{1,2},{2,1},{3,0},{4,7},{5,6},{6,5},{7,4},{8,11},{9,10},{10,... | collective-permute-start | bytes 294920 | tf_op jit(solution)/shard_map/ppermute | solution.py:492
